TPU v7x, 256 devices: a whole 4x4x8 slice. The times are simulated.
256 devices in a mesh: req: 16 (over y, z_lo), kvh: 8 (over z_hi, x), ffn: 2 (over core).
Axes of the slice: x: 4, y: 4, z: 8 (z_hi: 2, z_lo: 4; z = z_hi * 4 + z_lo), core: 2. Of those that a mesh axis runs over, the one named last changes fastest.
Arguments:
- queries: bfloat16 [16, 64, 8192], P('req', None, 'kvh'), may hold values from -8 to 8
- tree_keys: bfloat16 [16, 64, 1024], P('req', None, 'kvh'), may hold values from -4.5 to 4.5
- tree_token_values: bfloat16 [16, 64, 1024], P('req', None, 'kvh'), may hold values from -6 to 6
- cache_keys: bfloat16 [16, 8, 8192, 128], P('req', 'kvh', 'ffn'), may hold values from -4.5 to 4.5
- cached_value_rows: bfloat16 [16, 8, 8192, 128], P('req', 'kvh', 'ffn'), may hold values from -6 to 6
- lengths: int32 [16], replicated, may hold values from 1 to 8192, 32768 in all
- parents: int32 [16, 64], P('req'), may hold values from 0 to 63, as said below
- residual: float32 [1024, 8192], P(('req', 'ffn'), 'kvh'), may hold values from -6 to 6
- out_weight: bfloat16 [8192, 8192], P('kvh', ('req', 'ffn')), may hold values from -0.0625 to 0.0625
- norm_gain: float32 [8192], P('kvh'), may hold values from 0.25 to 1.75
- gate_weight: bfloat16 [8192, 28672], P('kvh', ('req', 'ffn')), may hold values from -0.0625 to 0.0625
- up_weight: bfloat16 [8192, 28672], P('kvh', ('req', 'ffn')), may hold values from -0.0625 to 0.0625
- down_weight: bfloat16 [28672, 8192], P(('req', 'ffn'), 'kvh'), may hold values from -0.03125 to 0.03125
Outputs:
- layer_output: float32 [1024, 8192], P(('req', 'ffn'), 'kvh')
Inputs may be any that keep to these rules, and one draw needn't show every extreme that they name: parents[r, 0] = 0, and parents[r, i] < i for every node i > 0. The lengths of all requests sum to 32768, and the largest is exactly 8192.
All inputs are finite; a program needn't handle non-finite values.
Results may differ from a plain program's by a relative error of at most 0.003.
Values may be sent and summed in bfloat16 or wider, within the bound.
No kernel may reach another device: no remote copies, remote signals or barrier semaphores. Data moves between devices by JAX's collectives and lax.ppermute only.
A program may use at most 64 MiB of HBM per device.

v0:
```python
import jax
import jax.numpy as jnp
from jax import lax
from jax.experimental import pallas as pl
from jax.experimental.pallas import tpu as pltpu
from jax.sharding import Mesh
from jax.sharding import PartitionSpec as P

KB = 1024
REQ = ("y", "zl")
KVH = ("zh", "x")
GRID = ("y", "zl", "zh", "x")
SIZES = (4, 4, 2, 4)
MASKED = -1e30
EPSILON = 1e-05
MASKS = (0, 3, 1, 2)


def sent(array, target):
    pairs = []
    for source in range(128):
        x, zh, zl, y = source % 4, source // 4 % 2, source // 8 % 4, source // 32
        to = target(y, zl, zh, x)
        pairs.append((source, ((to[0] * 4 + to[1]) * 2 + to[2]) * 4 + to[3]))
    return lax.ppermute(array, GRID, pairs)


def over_x(array, mask):
    return lax.ppermute(array, "x", [(i, i ^ mask) for i in range(4)])


def over_zh(array):
    return lax.ppermute(array, "zh", [(0, 1), (1, 0)])


def over_core(array):
    return lax.ppermute(array, "core", [(0, 1), (1, 0)])


def line_target(place):
    part, step = divmod(place, 2)
    return lambda y, zl, zh, x: (y, zl ^ (2 * (part ^ zh) + step), zh, x)


def ring_target(mask):
    return lambda y, zl, zh, x: (y ^ x ^ mask, zl, zh, x)


def home_target(place):
    part, step = divmod(place, 2)
    return lambda y, zl, zh, x: (
        y ^ x,
        zl ^ (2 * (part ^ zh) + step),
        zl >> 1,
        y,
    )


def column_target(y, zl, zh, x):
    return 2 * (y & 1) + (zl >> 1), 2 * (y >> 1) + (zl & 1), zh, x


def gathered(rows):
    line = jnp.concatenate([sent(rows, line_target(place)) for place in range(4)])
    return {mask: sent(line, ring_target(mask)) for mask in MASKS}


def together(move, arrays, *how):
    joined = move(jnp.concatenate(arrays, axis=1), *how)
    cuts = [sum(a.shape[1] for a in arrays[: k + 1]) for k in range(len(arrays) - 1)]
    return jnp.split(joined, cuts, axis=1)


def dot(a, b):
    return jnp.dot(a, b, preferred_element_type=jnp.float32)


def summed_over_x(blocks, first, second, dtype):
    pair = lambda a, b: jnp.concatenate([blocks[a], blocks[b]])
    away1, away2 = pair(1, 2), pair(3, 2)
    stay1, stay2 = pair(0, 3), pair(0, 1)
    half = blocks[0].shape[0]
    got1 = together(over_x, [dot(away1, w).astype(dtype) for w in first], 1)
    got2 = together(over_x, [dot(away2, w).astype(dtype) for w in second], 3)
    sum1 = [dot(stay1, w) + g for w, g in zip(first, got1)]
    sum2 = [dot(stay2, w) + g for w, g in zip(second, got2)]
    got1 = together(over_x, [s[half:].astype(dtype) for s in sum1], 3)
    got2 = together(over_x, [s[half:].astype(dtype) for s in sum2], 1)
    return [
        [s[:half] + g for s, g in zip(sums, got)] for sums, got in ((sum1, got1), (sum2, got2))
    ]


def attend_kernel(
    info, queries, tree_keys, tree_values, parents, keys, values, own, other, rows, top, total, mix
):
    step, live, core = pl.program_id(0), info[0], info[1]
    nodes, width = queries.shape
    block, head = keys.shape
    heads = width // head
    scale = head**-0.5

    def scored(key_block):
        return scale * lax.dot_general(
            rows[...], key_block, (((1,), (1,)), ((), ())), preferred_element_type=jnp.float32
        )

    def mixed(weights, value_block):
        high = weights.astype(jnp.bfloat16)
        low = (weights - high.astype(jnp.float32)).astype(jnp.bfloat16)
        return dot(high, value_block) + dot(low, value_block)

    @pl.when(step == 0)
    def _():
        for j in range(heads):
            rows[j * nodes : (j + 1) * nodes, :] = queries[:, j * head : (j + 1) * head]

        @pl.when(core == 0)
        def _():
            places = lax.broadcasted_iota(jnp.int32, (nodes, nodes), 1)
            level = lax.broadcasted_iota(jnp.int32, (nodes, nodes), 0)
            reach = jnp.where((places == level) | (parents[...] == places), 1.0, 0.0)
            for _ in range((nodes - 1).bit_length()):
                reach = jnp.minimum(dot(reach.astype(jnp.bfloat16), reach.astype(jnp.bfloat16)), 1.0)
            reach = jnp.concatenate([reach] * heads)
            scores = jnp.where(reach > 0.5, scored(tree_keys[...]), MASKED)
            highest = jnp.max(scores, axis=1, keepdims=True)
            weights = jnp.exp(scores - highest)
            top[...] = jnp.broadcast_to(highest, top.shape)
            total[...] = jnp.broadcast_to(jnp.sum(weights, axis=1, keepdims=True), total.shape)
            mix[...] = mixed(weights, tree_values[...])

        @pl.when(core != 0)
        def _():
            top[...] = jnp.full(top.shape, MASKED, jnp.float32)
            total[...] = jnp.zeros(total.shape, jnp.float32)
            mix[...] = jnp.zeros(mix.shape, jnp.float32)

    @pl.when(step * block < live)
    def _():
        scores = scored(keys[...])
        positions = step * block + lax.broadcasted_iota(jnp.int32, scores.shape, 1)
        scores = jnp.where(positions < live, scores, MASKED)
        before = top[:, :1]
        highest = jnp.maximum(before, jnp.max(scores, axis=1, keepdims=True))
        weights = jnp.exp(scores - highest)
        factor = jnp.exp(before - highest)
        top[...] = jnp.broadcast_to(highest, top.shape)
        total[...] = total[...] * factor + jnp.sum(weights, axis=1, keepdims=True)
        mix[...] = mix[...] * factor + mixed(weights, values[...])

    @pl.when(step == pl.num_programs(0) - 1)
    def _():
        half = nodes // 2
        count = heads * half
        first = lax.broadcasted_iota(jnp.int32, (half, head), 1) < head // 2
        for side, out in ((core, own), (1 - core, other)):
            for j in range(heads):
                here = pl.ds(pl.multiple_of(j * nodes + side * half, half), half)
                out[j * half : (j + 1) * half, :] = mix[here, :]
                out[count + j * half : count + (j + 1) * half, :] = jnp.where(
                    first, top[here, :], total[here, :]
                )


def combine_kernel(own, came, out):
    half = out.shape[0]
    count, head = own.shape[0] // 2, own.shape[1]
    for j in range(count // half):
        here = slice(j * half, (j + 1) * half)
        numbers = slice(count + j * half, count + (j + 1) * half)
        top1, total1 = own[numbers, :1], own[numbers, head - 1 :]
        top2, total2 = came[numbers, :1], came[numbers, head - 1 :]
        highest = jnp.maximum(top1, top2)
        factor1, factor2 = jnp.exp(top1 - highest), jnp.exp(top2 - highest)
        total = total1 * factor1 + total2 * factor2
        value = (own[here, :] * factor1 + came[here, :] * factor2) / total
        out[:, j * head : (j + 1) * head] = value.astype(out.dtype)


def attended_parts(queries, tree_keys, tree_values, keys, values, length, parent_row, core):
    nodes, width = queries.shape
    half_len, head = keys.shape
    rows = width // head * nodes
    block = min(KB, half_len)
    live = jnp.clip(length - core * half_len, 0, half_len)
    info = jnp.stack([live, core]).astype(jnp.int32)
    whole = lambda shape: pl.BlockSpec(shape, lambda i, info: (0, 0))
    last = lambda i, info: (jnp.minimum(i, jnp.maximum(info[0] - 1, 0) // block), 0)
    side = jax.ShapeDtypeStruct((rows, head), jnp.float32)
    return pl.pallas_call(
        attend_kernel,
        out_shape=(side, side),
        grid_spec=pltpu.PrefetchScalarGridSpec(
            num_scalar_prefetch=1,
            grid=(half_len // block,),
            in_specs=[
                whole((nodes, width)),
                whole((nodes, head)),
                whole((nodes, head)),
                whole((nodes, 1)),
                pl.BlockSpec((block, head), last),
                pl.BlockSpec((block, head), last),
            ],
            out_specs=(whole((rows, head)), whole((rows, head))),
            scratch_shapes=[
                pltpu.VMEM((rows, head), jnp.bfloat16),
                pltpu.VMEM((rows, head), jnp.float32),
                pltpu.VMEM((rows, head), jnp.float32),
                pltpu.VMEM((rows, head), jnp.float32),
            ],
        ),
        compiler_params=pltpu.CompilerParams(vmem_limit_bytes=32 << 20),
        cost_estimate=pl.CostEstimate(
            flops=6 * rows * half_len * head,
            bytes_accessed=4 * half_len * head,
            transcendentals=rows * half_len,
        ),
        name="attend",
    )(info, queries, tree_keys, tree_values, parent_row[:, None], keys, values)


def attended(own, other, half):
    rows, head = own.shape
    return pl.pallas_call(
        combine_kernel,
        out_shape=jax.ShapeDtypeStruct((half, rows // 2 // half * head), jnp.bfloat16),
        name="combine",
    )(own, over_core(other))


def local(
    queries,
    tree_keys,
    tree_token_values,
    cache_keys,
    cached_value_rows,
    lengths,
    parents,
    residual,
    out_weight,
    norm_gain,
    gate_weight,
    up_weight,
    down_weight,
):
    core = lax.axis_index("core")
    features = norm_gain.shape[0] * 8
    out_weight = sent(out_weight, column_target)
    other_gate = over_core(gate_weight)
    other_up = over_core(up_weight)
    other_down = over_core(down_weight)
    length = lax.dynamic_index_in_dim(lengths, lax.axis_index(REQ), keepdims=False)
    parts = attended_parts(
        queries[0],
        tree_keys[0],
        tree_token_values[0],
        cache_keys[0, 0],
        cached_value_rows[0, 0],
        length,
        parents[0],
        core,
    )
    parts, out_weight, other_gate, other_up, other_down = lax.optimization_barrier(
        (parts, out_weight, other_gate, other_up, other_down)
    )
    attention = attended(*parts, queries.shape[1] // 2)
    other_out = over_core(out_weight)
    tokens = attention.shape[0]

    (mine,), (theirs,) = summed_over_x(
        gathered(attention), [out_weight], [other_out], jnp.float32
    )
    both = jnp.concatenate([mine, theirs], axis=1)
    came = [sent(both[k * tokens : (k + 1) * tokens], home_target(k)) for k in range(4)]
    width = mine.shape[1]
    own_first = core == 0
    sides = []
    for step in range(2):
        total = came[step] + came[2 + step]
        a, b = total[:, :width], total[:, width:]
        sides.append(
            jnp.concatenate([jnp.where(own_first, a, b), jnp.where(own_first, b, a)], axis=1)
        )
    even = lax.axis_index("zl") % 2 == 0
    projected = jnp.concatenate(
        [jnp.where(even, sides[0], sides[1]), jnp.where(even, sides[1], sides[0])], axis=1
    )
    state = residual + projected

    squares = jnp.sum(state * state, axis=1)[None]
    squares = sum([over_x(squares, mask) for mask in (1, 2, 3)], squares)
    squares = squares + over_zh(squares)
    normed = (state * lax.rsqrt(squares[0] / features + EPSILON)[:, None] * norm_gain).astype(
        jnp.bfloat16
    )

    first, second = summed_over_x(
        gathered(normed), [gate_weight, up_weight], [other_gate, other_up], jnp.bfloat16
    )
    half = 2 * tokens

    ours = first + second
    came = together(over_zh, [s[half:].astype(jnp.bfloat16) for s in ours])
    gate1, up1, gate2, up2 = [s[:half] + g for s, g in zip(ours, came)]
    active = [
        (jax.nn.silu(gate) * up).astype(jnp.bfloat16) for gate, up in ((gate1, up1), (gate2, up2))
    ]

    one, two = [
        jnp.concatenate([a, b]) for a, b in zip(active, together(over_zh, active))
    ]
    one3, two1 = over_x(one, 3), over_x(two, 1)
    one12 = over_x(jnp.concatenate([one, one3]), 1)
    two32 = over_x(jnp.concatenate([two, two1]), 3)
    block = one.shape[0]
    parts = {
        0: (one, two),
        3: (one3, two32[:block]),
        1: (one12[:block], two1),
        2: (one12[block:], two32[block:]),
    }
    line = 0.0
    for mask in MASKS:
        a, b = parts[mask]
        down = (dot(a, down_weight) + dot(b, other_down)).astype(jnp.bfloat16)
        line = line + sent(down, ring_target(mask)).astype(jnp.float32)
    line = line.astype(jnp.bfloat16)
    result = state
    for place in range(4):
        piece = line[place * tokens : (place + 1) * tokens]
        result = result + sent(piece, line_target(place)).astype(jnp.float32)
    return result


def solution(mesh):
    split = Mesh(mesh.devices.reshape(4, 4, 2, 4, 2), ("y", "zl", "zh", "x", "core"))
    all_rows = (*REQ, "core")
    in_specs = (
        P(REQ, None, KVH),
        P(REQ, None, KVH),
        P(REQ, None, KVH),
        P(REQ, KVH, "core", None),
        P(REQ, KVH, "core", None),
        P(),
        P(REQ, None),
        P(all_rows, KVH),
        P(KVH, all_rows),
        P(KVH),
        P(KVH, all_rows),
        P(KVH, all_rows),
        P(all_rows, KVH),
    )
    return jax.shard_map(
        local, mesh=split, in_specs=in_specs, out_specs=P(all_rows, KVH), check_vma=False
    )
```

profile of v0, /device:TPU:24, one launch (start us, length us, event | category | flops | bytes accessed | tf_op | source)
XLA Modules:
  0.0 310.3 jit_solution(2141031499460144275)
XLA Ops:
  0.5 5.3 %collective-permute-start = (bf16[1024,256]{1,0:T(8,128)(2,1)}, bf16[1024,256]{1,0:T(8,128)(2,1)S(1)}, u32[]{:S(2)}, u32[]{:S(2)}) collective-permute-start(bf16[1024,256]{1,0:T(8,128)(2,1)} %param.21), channel_id=1, source_target_pairs={{0,0},{2,2},{4,4},{6,6},{8,8},{10,10},{12,12},{14,14},{16,16},{18,... | collective-permute-start | bytes 1572872 | tf_op jit(solution)/shard_map/ppermute | solution.py:25
  13.4 3.8 %attend.1 = (f32[512,128]{1,0:T(8,128)S(1)}, f32[512,128]{1,0:T(8,128)S(1)}) custom-call(s32[2]{0:T(128)S(1)} %pad_add_fusion.info, bf16[64,1024]{1,0:T(8,128)(2,1)S(1)} %bitcast.45, bf16[64,128]{1,0:T(8,128)(2,1)S(1)} %bitcast.46, bf16[64,128]{1,0:T(8,128)(2,1)S(1)} %bitcast.47, s32[64,1]{1,0:T(8,128)S(1)} %copy.27.parents, bf16[4096,128]{1,0:T(8,128)(2,1)S(1)} %bitcast.43, ...), custom_call_target="tpu_custom_call" | custom-call | flops 1610612736 | bytes 2097152 | tf_op jit(solution)/shard_map/attend/pallas_call | solution.py:191
  17.9 13.6 %collective-permute-done = bf16[1024,256]{1,0:T(8,128)(2,1)S(1)} collective-permute-done((bf16[1024,256]{1,0:T(8,128)(2,1)}, bf16[1024,256]{1,0:T(8,128)(2,1)S(1)}, u32[]{:S(2)}, u32[]{:S(2)}) %collective-permute-start) | collective-permute-done | bytes 524320 | tf_op jit(solution)/shard_map/ppermute | solution.py:25
  33.8 2.1 combine.1
  39.5 4.5 %collective-permute-start.8 = (bf16[32,1024]{1,0:T(8,128)(2,1)}, bf16[32,1024]{1,0:T(8,128)(2,1)S(1)}, u32[]{:S(2)}, u32[]{:S(2)}) collective-permute-start(bf16[32,1024]{1,0:T(8,128)(2,1)} %combine.1), channel_id=1, source_target_pairs={{0,48},{2,50},{4,52},{6,54},{8,24},{10,26},{12,28},{14,30},{16,32}... | collective-permute-start | bytes 196616 | tf_op jit(solution)/shard_map/ppermute | solution.py:25
  44.0 4.3 %collective-permute-done.7 = bf16[32,1024]{1,0:T(8,128)(2,1)S(1)} collective-permute-done((bf16[32,1024]{1,0:T(8,128)(2,1)}, bf16[32,1024]{1,0:T(8,128)(2,1)S(1)}, u32[]{:S(2)}, u32[]{:S(2)}) %collective-permute-start.7) | collective-permute-done | bytes 65568 | tf_op jit(solution)/shard_map/ppermute | solution.py:25
  48.3 4.4 %collective-permute-start.10 = (bf16[128,1024]{1,0:T(8,128)(2,1)S(1)}, bf16[128,1024]{1,0:T(8,128)(2,1)S(1)}, u32[]{:S(2)}, u32[]{:S(2)}) collective-permute-start(bf16[128,1024]{1,0:T(8,128)(2,1)S(1)} %constant_dynamic-update-slice_fusion), channel_id=1, source_target_pairs={{0,192},{2,130},{4,68},{6,6},{8,200},{10,138},{12,76},{14,14},{16,... | collective-permute-start | bytes 786440 | tf_op jit(solution)/shard_map/ppermute | solution.py:25
  52.7 3.0 collective-permute-start.12
  55.8 2.4 collective-permute-start.11
  58.8 4.0 %collective-permute-done.10 = bf16[128,1024]{1,0:T(8,128)(2,1)S(1)} collective-permute-done((bf16[128,1024]{1,0:T(8,128)(2,1)S(1)}, bf16[128,1024]{1,0:T(8,128)(2,1)S(1)}, u32[]{:S(2)}, u32[]{:S(2)}) %collective-permute-start.10) | collective-permute-done | bytes 262176 | tf_op jit(solution)/shard_map/ppermute | solution.py:25
  62.8 2.6 collective-permute-done.12
  66.6 6.8 %collective-permute-done.16 = f32[256,256]{0,1:T(8,128)S(1)} collective-permute-done((f32[256,256]{0,1:T(8,128)S(1)}, f32[256,256]{0,1:T(8,128)S(1)}, u32[]{:S(2)}, u32[]{:S(2)}) %collective-permute-start.16) | collective-permute-done | bytes 262176 | tf_op jit(solution)/shard_map/ppermute | solution.py:29
  74.7 2.4 collective-permute-start.14
  78.9 2.2 collective-permute-done.14
  81.3 4.3 %collective-permute-start.18 = (f32[32,512]{0,1:T(8,128)S(1)}, f32[32,512]{0,1:T(8,128)}, u32[]{:S(2)}, u32[]{:S(2)}) collective-permute-start(f32[32,512]{0,1:T(8,128)S(1)} %get-tuple-element.40), channel_id=1, source_target_pairs={{0,0},{2,64},{4,128},{6,192},{8,32},{10,96},{12,160},{14,224},{16,... | collective-permute-start | bytes 196616 | tf_op jit(solution)/shard_map/ppermute | solution.py:25
  85.7 7.3 %collective-permute-start.19 = (f32[32,512]{0,1:T(8,128)S(1)}, f32[32,512]{0,1:T(8,128)}, u32[]{:S(2)}, u32[]{:S(2)}) collective-permute-start(f32[32,512]{0,1:T(8,128)S(1)} %get-tuple-element.39), channel_id=1, source_target_pairs={{0,32},{2,96},{4,160},{6,224},{8,0},{10,64},{12,128},{14,192},{16,... | collective-permute-start | bytes 196616 | tf_op jit(solution)/shard_map/ppermute | solution.py:25
  93.0 4.6 %collective-permute-start.20 = (f32[32,512]{0,1:T(8,128)S(1)}, f32[32,512]{0,1:T(8,128)S(1)}, u32[]{:S(2)}, u32[]{:S(2)}) collective-permute-start(f32[32,512]{0,1:T(8,128)S(1)} %get-tuple-element.42), channel_id=1, source_target_pairs={{0,16},{2,80},{4,144},{6,208},{8,48},{10,112},{12,176},{14,240},{1... | collective-permute-start | bytes 196616 | tf_op jit(solution)/shard_map/ppermute | solution.py:25
  97.6 3.3 %collective-permute-start.21 = (f32[32,512]{0,1:T(8,128)S(1)}, f32[32,512]{0,1:T(8,128)}, u32[]{:S(2)}, u32[]{:S(2)}) collective-permute-start(f32[32,512]{0,1:T(8,128)S(1)} %get-tuple-element.41), channel_id=1, source_target_pairs={{0,48},{2,112},{4,176},{6,240},{8,16},{10,80},{12,144},{14,208},{1... | collective-permute-start | bytes 196616 | tf_op jit(solution)/shard_map/ppermute | solution.py:25
  100.9 31.1 %collective-permute-done.18 = f32[32,512]{0,1:T(8,128)} collective-permute-done((f32[32,512]{0,1:T(8,128)S(1)}, f32[32,512]{0,1:T(8,128)}, u32[]{:S(2)}, u32[]{:S(2)}) %collective-permute-start.18) | collective-permute-done | bytes 65568 | tf_op jit(solution)/shard_map/ppermute | solution.py:25
  135.3 4.1 %collective-permute-start.24 = (f32[1,32]{1,0:T(1,128)S(1)}, f32[1,32]{1,0:T(1,128)S(1)}, u32[]{:S(2)}, u32[]{:S(2)}) collective-permute-start(f32[1,32]{1,0:T(1,128)S(1)} %bitcast.50), channel_id=1, source_target_pairs={{0,6},{2,4},{4,2},{6,0},{1,7},{3,5},{5,3},{7,1},{8,14},{10,12},{12... | collective-permute-start | bytes 392 | tf_op jit(solution)/shard_map/ppermute | solution.py:29
  140.9 8.3 %collective-permute-start.25 = (f32[1,32]{1,0:T(1,128)S(1)}, f32[1,32]{1,0:T(1,128)S(1)}, u32[]{:S(2)}, u32[]{:S(2)}) collective-permute-start(f32[1,32]{1,0:T(1,128)S(1)} %add_add_fusion), channel_id=1, source_target_pairs={{0,8},{8,0},{1,9},{9,1},{2,10},{10,2},{3,11},{11,3},{4,12},{12,4},... | collective-permute-start | bytes 392 | tf_op jit(solution)/shard_map/ppermute | solution.py:33
  152.4 7.9 %collective-permute-start.28 = (bf16[32,1024]{1,0:T(8,128)(2,1)S(1)}, bf16[32,1024]{1,0:T(8,128)(2,1)S(1)}, u32[]{:S(2)}, u32[]{:S(2)}) collective-permute-start(bf16[32,1024]{1,0:T(8,128)(2,1)S(1)} %multiply_convert_fusion), channel_id=1, source_target_pairs={{0,32},{2,34},{4,36},{6,38},{8,8},{10,10},{12,12},{14,14},{16,48},... | collective-permute-start | bytes 196616 | tf_op jit(solution)/shard_map/ppermute | solution.py:25
  162.5 4.0 %collective-permute-done.29 = bf16[32,1024]{1,0:T(8,128)(2,1)S(1)} collective-permute-done((bf16[32,1024]{1,0:T(8,128)(2,1)S(1)}, bf16[32,1024]{1,0:T(8,128)(2,1)S(1)}, u32[]{:S(2)}, u32[]{:S(2)}) %collective-permute-start.29) | collective-permute-done | bytes 65568 | tf_op jit(solution)/shard_map/ppermute | solution.py:25
  169.1 3.1 collective-permute-start.31
  172.2 4.8 %collective-permute-start.33 = (bf16[128,1024]{1,0:T(8,128)(2,1)S(1)}, bf16[128,1024]{1,0:T(8,128)(2,1)S(1)}, u32[]{:S(2)}, u32[]{:S(2)}) collective-permute-start(bf16[128,1024]{1,0:T(8,128)(2,1)S(1)} %constant_dynamic-update-slice_fusion.4), channel_id=1, source_target_pairs={{0,128},{2,194},{4,4},{6,70},{8,136},{10,202},{12,12},{14,78},{16,... | collective-permute-start | bytes 786440 | tf_op jit(solution)/shard_map/ppermute | solution.py:25
  179.0 3.0 collective-permute-done.33
  182.0 2.2 convolution_convert_fusion
  184.3 2.3 convolution_convert_fusion.1
  186.7 2.9 collective-permute-start.36
  191.2 13.4 %collective-permute-done.36 = bf16[256,1792]{1,0:T(8,128)(2,1)S(1)} collective-permute-done((bf16[256,1792]{1,0:T(8,128)(2,1)S(1)}, bf16[256,1792]{1,0:T(8,128)(2,1)S(1)}, u32[]{:S(2)}, u32[]{:S(2)}) %collective-permute-start.36) | collective-permute-done | bytes 917536 | tf_op jit(solution)/shard_map/ppermute | solution.py:29
  204.6 2.2 convolution_add_fusion
  206.9 2.2 convolution_add_fusion.1
  210.9 2.0 collective-permute-start.35
  212.9 4.9 %collective-permute-done.37 = bf16[128,1792]{1,0:T(8,128)(2,1)S(1)} collective-permute-done((bf16[128,1792]{1,0:T(8,128)(2,1)S(1)}, bf16[128,1792]{1,0:T(8,128)(2,1)S(1)}, u32[]{:S(2)}, u32[]{:S(2)}) %collective-permute-start.37) | collective-permute-done | bytes 458784 | tf_op jit(solution)/shard_map/ppermute | solution.py:29
  217.9 3.0 collective-permute-done.35
  221.1 9.0 %collective-permute-start.38 = (bf16[64,3584]{1,0:T(8,128)(2,1)S(1)}, bf16[64,3584]{1,0:T(8,128)(2,1)S(1)}, u32[]{:S(2)}, u32[]{:S(2)}) collective-permute-start(bf16[64,3584]{1,0:T(8,128)(2,1)S(1)} %pad_maximum_fusion.12), channel_id=1, source_target_pairs={{0,8},{8,0},{1,9},{9,1},{2,10},{10,2},{3,11},{11,3},{4,12},{12,4},... | collective-permute-start | bytes 1376264 | tf_op jit(solution)/shard_map/ppermute | solution.py:33
  230.1 10.2 %collective-permute-done.38 = bf16[64,3584]{1,0:T(8,128)(2,1)S(1)} collective-permute-done((bf16[64,3584]{1,0:T(8,128)(2,1)S(1)}, bf16[64,3584]{1,0:T(8,128)(2,1)S(1)}, u32[]{:S(2)}, u32[]{:S(2)}) %collective-permute-start.38) | collective-permute-done | bytes 458784 | tf_op jit(solution)/shard_map/ppermute | solution.py:33
  240.4 6.6 %collective-permute-start.39 = (bf16[64,1792]{1,0:T(8,128)(2,1)S(1)}, bf16[64,1792]{1,0:T(8,128)(2,1)S(1)}, u32[]{:S(2)}, u32[]{:S(2)}) collective-permute-start(bf16[64,1792]{1,0:T(8,128)(2,1)S(1)} %pad_maximum_fusion.16), channel_id=1, source_target_pairs={{0,8},{8,0},{1,9},{9,1},{2,10},{10,2},{3,11},{11,3},{4,12},{12,4},... | collective-permute-start | bytes 688136 | tf_op jit(solution)/shard_map/ppermute | solution.py:33
  247.1 9.2 %collective-permute-done.39 = bf16[64,1792]{1,0:T(8,128)(2,1)S(1)} collective-permute-done((bf16[64,1792]{1,0:T(8,128)(2,1)S(1)}, bf16[64,1792]{1,0:T(8,128)(2,1)S(1)}, u32[]{:S(2)}, u32[]{:S(2)}) %collective-permute-start.39) | collective-permute-done | bytes 229408 | tf_op jit(solution)/shard_map/ppermute | solution.py:33
  258.3 6.1 %collective-permute-done.42 = bf16[128,896]{1,0:T(8,128)(2,1)S(1)} collective-permute-done((bf16[128,896]{1,0:T(8,128)(2,1)S(1)}, bf16[128,896]{1,0:T(8,128)(2,1)S(1)}, u32[]{:S(2)}, u32[]{:S(2)}) %collective-permute-start.42) | collective-permute-done | bytes 229408 | tf_op jit(solution)/shard_map/ppermute | solution.py:29
  269.1 5.2 %collective-permute-done.43 = bf16[256,896]{1,0:T(8,128)(2,1)S(1)} collective-permute-done((bf16[256,896]{1,0:T(8,128)(2,1)S(1)}, bf16[256,896]{1,0:T(8,128)(2,1)S(1)}, u32[]{:S(2)}, u32[]{:S(2)}) %collective-permute-start.43) | collective-permute-done | bytes 458784 | tf_op jit(solution)/shard_map/ppermute | solution.py:29
  277.6 5.1 %collective-permute-start.46 = (bf16[128,1024]{1,0:T(8,128)(2,1)S(1)}, bf16[128,1024]{1,0:T(8,128)(2,1)S(1)}, u32[]{:S(2)}, u32[]{:S(2)}) collective-permute-start(bf16[128,1024]{1,0:T(8,128)(2,1)S(1)} %fusion.2), channel_id=1, source_target_pairs={{0,64},{2,2},{4,196},{6,134},{8,72},{10,10},{12,204},{14,142},{16,... | collective-permute-start | bytes 786440 | tf_op jit(solution)/shard_map/ppermute | solution.py:25
  283.6 3.4 %collective-permute-start.47 = (bf16[128,1024]{1,0:T(8,128)(2,1)S(1)}, bf16[128,1024]{1,0:T(8,128)(2,1)S(1)}, u32[]{:S(2)}, u32[]{:S(2)}) collective-permute-start(bf16[128,1024]{1,0:T(8,128)(2,1)S(1)} %fusion.3), channel_id=1, source_target_pairs={{0,128},{2,194},{4,4},{6,70},{8,136},{10,202},{12,12},{14,78},{16,... | collective-permute-start | bytes 786440 | tf_op jit(solution)/shard_map/ppermute | solution.py:25
  287.0 6.3 %collective-permute-done.47 = bf16[128,1024]{1,0:T(8,128)(2,1)S(1)} collective-permute-done((bf16[128,1024]{1,0:T(8,128)(2,1)S(1)}, bf16[128,1024]{1,0:T(8,128)(2,1)S(1)}, u32[]{:S(2)}, u32[]{:S(2)}) %collective-permute-start.47) | collective-permute-done | bytes 262176 | tf_op jit(solution)/shard_map/ppermute | solution.py:25
  294.2 6.9 %collective-permute-start.49 = (bf16[32,1024]{1,0:T(8,128)(2,1)S(1)}, bf16[32,1024]{1,0:T(8,128)(2,1)S(1)}, u32[]{:S(2)}, u32[]{:S(2)}) collective-permute-start(bf16[32,1024]{1,0:T(8,128)(2,1)S(1)} %get-tuple-element.30), channel_id=1, source_target_pairs={{0,16},{2,18},{4,20},{6,22},{8,56},{10,58},{12,60},{14,62},{16,0},... | collective-permute-start | bytes 196616 | tf_op jit(solution)/shard_map/ppermute | solution.py:25
  301.1 2.2 collective-permute-start.50
  303.4 2.1 collective-permute-start.51
  305.5 2.8 collective-permute-done.50
  (160 shorter events, 51.2 us)
Async XLA Ops:
  0.0 31.5 %collective-permute-start.1 = (bf16[1024,896]{1,0:T(8,128)(2,1)}, bf16[1024,896]{1,0:T(8,128)(2,1)}, u32[]{:S(2)}, u32[]{:S(2)}) collective-permute-start(bf16[1024,896]{1,0:T(8,128)(2,1)} %param.23), channel_id=1, source_target_pairs={{0,1},{1,0},{2,3},{3,2},{4,5},{5,4},{6,7},{7,6},{8,9},{9,8},{10,11... | collective-permute-start | bytes 5505032 | tf_op jit(solution)/shard_map/ppermute | solution.py:37
  0.0 31.5 %collective-permute-start.2 = (bf16[1024,896]{1,0:T(8,128)(2,1)}, bf16[1024,896]{1,0:T(8,128)(2,1)}, u32[]{:S(2)}, u32[]{:S(2)}) collective-permute-start(bf16[1024,896]{1,0:T(8,128)(2,1)} %param.24), channel_id=1, source_target_pairs={{0,1},{1,0},{2,3},{3,2},{4,5},{5,4},{6,7},{7,6},{8,9},{9,8},{10,11... | collective-permute-start | bytes 5505032 | tf_op jit(solution)/shard_map/ppermute | solution.py:37
  0.5 31.0 %collective-permute-start.3 = (bf16[896,1024]{1,0:T(8,128)(2,1)}, bf16[896,1024]{1,0:T(8,128)(2,1)S(1)}, u32[]{:S(2)}, u32[]{:S(2)}) collective-permute-start(bf16[896,1024]{1,0:T(8,128)(2,1)} %param.25), channel_id=1, source_target_pairs={{0,1},{1,0},{2,3},{3,2},{4,5},{5,4},{6,7},{7,6},{8,9},{9,8},{10,11... | collective-permute-start | bytes 5505032 | tf_op jit(solution)/shard_map/ppermute | solution.py:37
  0.5 31.0 %collective-permute-start = (bf16[1024,256]{1,0:T(8,128)(2,1)}, bf16[1024,256]{1,0:T(8,128)(2,1)S(1)}, u32[]{:S(2)}, u32[]{:S(2)}) collective-permute-start(bf16[1024,256]{1,0:T(8,128)(2,1)} %param.21), channel_id=1, source_target_pairs={{0,0},{2,2},{4,4},{6,6},{8,8},{10,10},{12,12},{14,14},{16,16},{18,... | collective-permute-start | bytes 1572872 | tf_op jit(solution)/shard_map/ppermute | solution.py:25
  35.9 8.0 %collective-permute-start.5 = (bf16[32,1024]{1,0:T(8,128)(2,1)}, bf16[32,1024]{1,0:T(8,128)(2,1)S(1)}, u32[]{:S(2)}, u32[]{:S(2)}) collective-permute-start(bf16[32,1024]{1,0:T(8,128)(2,1)} %combine.1), channel_id=1, source_target_pairs={{0,0},{2,2},{4,4},{6,6},{8,40},{10,42},{12,44},{14,46},{16,16},{18... | collective-permute-start | bytes 196616 | tf_op jit(solution)/shard_map/ppermute | solution.py:25
  37.4 21.4 %collective-permute-start.15 = (bf16[1024,256]{1,0:T(8,128)(2,1)S(1)}, bf16[1024,256]{1,0:T(8,128)(2,1)S(1)}, u32[]{:S(2)}, u32[]{:S(2)}) collective-permute-start(bf16[1024,256]{1,0:T(8,128)(2,1)S(1)} %collective-permute-done), channel_id=1, source_target_pairs={{0,1},{1,0},{2,3},{3,2},{4,5},{5,4},{6,7},{7,6},{8,9},{9,8},{10,11... | collective-permute-start | bytes 1572872 | tf_op jit(solution)/shard_map/ppermute | solution.py:37
  37.5 6.4 %collective-permute-start.6 = (bf16[32,1024]{1,0:T(8,128)(2,1)}, bf16[32,1024]{1,0:T(8,128)(2,1)S(1)}, u32[]{:S(2)}, u32[]{:S(2)}) collective-permute-start(bf16[32,1024]{1,0:T(8,128)(2,1)} %combine.1), channel_id=1, source_target_pairs={{0,16},{2,18},{4,20},{6,22},{8,56},{10,58},{12,60},{14,62},{16,0},... | collective-permute-start | bytes 196616 | tf_op jit(solution)/shard_map/ppermute | solution.py:25
  37.5 10.7 %collective-permute-start.7 = (bf16[32,1024]{1,0:T(8,128)(2,1)}, bf16[32,1024]{1,0:T(8,128)(2,1)S(1)}, u32[]{:S(2)}, u32[]{:S(2)}) collective-permute-start(bf16[32,1024]{1,0:T(8,128)(2,1)} %combine.1), channel_id=1, source_target_pairs={{0,32},{2,34},{4,36},{6,38},{8,8},{10,10},{12,12},{14,14},{16,48},... | collective-permute-start | bytes 196616 | tf_op jit(solution)/shard_map/ppermute | solution.py:25
  39.5 8.8 %collective-permute-start.8 = (bf16[32,1024]{1,0:T(8,128)(2,1)}, bf16[32,1024]{1,0:T(8,128)(2,1)S(1)}, u32[]{:S(2)}, u32[]{:S(2)}) collective-permute-start(bf16[32,1024]{1,0:T(8,128)(2,1)} %combine.1), channel_id=1, source_target_pairs={{0,48},{2,50},{4,52},{6,54},{8,24},{10,26},{12,28},{14,30},{16,32}... | collective-permute-start | bytes 196616 | tf_op jit(solution)/shard_map/ppermute | solution.py:25
  48.3 14.5 %collective-permute-start.10 = (bf16[128,1024]{1,0:T(8,128)(2,1)S(1)}, bf16[128,1024]{1,0:T(8,128)(2,1)S(1)}, u32[]{:S(2)}, u32[]{:S(2)}) collective-permute-start(bf16[128,1024]{1,0:T(8,128)(2,1)S(1)} %constant_dynamic-update-slice_fusion), channel_id=1, source_target_pairs={{0,192},{2,130},{4,68},{6,6},{8,200},{10,138},{12,76},{14,14},{16,... | collective-permute-start | bytes 786440 | tf_op jit(solution)/shard_map/ppermute | solution.py:25
  52.7 12.6 %collective-permute-start.12 = (bf16[128,1024]{1,0:T(8,128)(2,1)S(1)}, bf16[128,1024]{1,0:T(8,128)(2,1)S(1)}, u32[]{:S(2)}, u32[]{:S(2)}) collective-permute-start(bf16[128,1024]{1,0:T(8,128)(2,1)S(1)} %constant_dynamic-update-slice_fusion), channel_id=1, source_target_pairs={{0,128},{2,194},{4,4},{6,70},{8,136},{10,202},{12,12},{14,78},{16,... | collective-permute-start | bytes 786440 | tf_op jit(solution)/shard_map/ppermute | solution.py:25
  55.8 10.4 %collective-permute-start.11 = (bf16[128,1024]{1,0:T(8,128)(2,1)S(1)}, bf16[128,1024]{1,0:T(8,128)(2,1)S(1)}, u32[]{:S(2)}, u32[]{:S(2)}) collective-permute-start(bf16[128,1024]{1,0:T(8,128)(2,1)S(1)} %constant_dynamic-update-slice_fusion), channel_id=1, source_target_pairs={{0,64},{2,2},{4,196},{6,134},{8,72},{10,10},{12,204},{14,142},{16,... | collective-permute-start | bytes 786440 | tf_op jit(solution)/shard_map/ppermute | solution.py:25
  58.1 8.5 %collective-permute-start.9 = (bf16[128,1024]{1,0:T(8,128)(2,1)S(1)}, bf16[128,1024]{1,0:T(8,128)(2,1)S(1)}, u32[]{:S(2)}, u32[]{:S(2)}) collective-permute-start(bf16[128,1024]{1,0:T(8,128)(2,1)S(1)} %constant_dynamic-update-slice_fusion), channel_id=1, source_target_pairs={{0,0},{2,66},{4,132},{6,198},{8,8},{10,74},{12,140},{14,206},{16,1... | collective-permute-start | bytes 786440 | tf_op jit(solution)/shard_map/ppermute | solution.py:25
  65.7 7.7 %collective-permute-start.16 = (f32[256,256]{0,1:T(8,128)S(1)}, f32[256,256]{0,1:T(8,128)S(1)}, u32[]{:S(2)}, u32[]{:S(2)}) collective-permute-start(f32[256,256]{0,1:T(8,128)S(1)} %fusion.5), channel_id=1, source_target_pairs={{0,6},{2,4},{4,2},{6,0},{1,7},{3,5},{5,3},{7,1},{8,14},{10,12},{12... | collective-permute-start | bytes 786440 | tf_op jit(solution)/shard_map/ppermute | solution.py:29
  66.5 7.9 %collective-permute-start.13 = (f32[256,256]{0,1:T(8,128)S(1)}, f32[256,256]{0,1:T(8,128)S(1)}, u32[]{:S(2)}, u32[]{:S(2)}) collective-permute-start(f32[256,256]{0,1:T(8,128)S(1)} %fusion.4), channel_id=1, source_target_pairs={{0,2},{2,0},{4,6},{6,4},{1,3},{3,1},{5,7},{7,5},{8,10},{10,8},{12,... | collective-permute-start | bytes 786440 | tf_op jit(solution)/shard_map/ppermute | solution.py:29
  74.7 6.3 %collective-permute-start.14 = (f32[128,256]{0,1:T(8,128)S(1)}, f32[128,256]{0,1:T(8,128)S(1)}, u32[]{:S(2)}, u32[]{:S(2)}) collective-permute-start(f32[128,256]{0,1:T(8,128)S(1)} %slice.153), channel_id=1, source_target_pairs={{0,6},{2,4},{4,2},{6,0},{1,7},{3,5},{5,3},{7,1},{8,14},{10,12},{12... | collective-permute-start | bytes 393224 | tf_op jit(solution)/shard_map/ppermute | solution.py:29
  81.3 50.7 %collective-permute-start.18 = (f32[32,512]{0,1:T(8,128)S(1)}, f32[32,512]{0,1:T(8,128)}, u32[]{:S(2)}, u32[]{:S(2)}) collective-permute-start(f32[32,512]{0,1:T(8,128)S(1)} %get-tuple-element.40), channel_id=1, source_target_pairs={{0,0},{2,64},{4,128},{6,192},{8,32},{10,96},{12,160},{14,224},{16,... | collective-permute-start | bytes 196616 | tf_op jit(solution)/shard_map/ppermute | solution.py:25
  85.7 46.4 %collective-permute-start.19 = (f32[32,512]{0,1:T(8,128)S(1)}, f32[32,512]{0,1:T(8,128)}, u32[]{:S(2)}, u32[]{:S(2)}) collective-permute-start(f32[32,512]{0,1:T(8,128)S(1)} %get-tuple-element.39), channel_id=1, source_target_pairs={{0,32},{2,96},{4,160},{6,224},{8,0},{10,64},{12,128},{14,192},{16,... | collective-permute-start | bytes 196616 | tf_op jit(solution)/shard_map/ppermute | solution.py:25
  93.0 40.1 %collective-permute-start.20 = (f32[32,512]{0,1:T(8,128)S(1)}, f32[32,512]{0,1:T(8,128)S(1)}, u32[]{:S(2)}, u32[]{:S(2)}) collective-permute-start(f32[32,512]{0,1:T(8,128)S(1)} %get-tuple-element.42), channel_id=1, source_target_pairs={{0,16},{2,80},{4,144},{6,208},{8,48},{10,112},{12,176},{14,240},{1... | collective-permute-start | bytes 196616 | tf_op jit(solution)/shard_map/ppermute | solution.py:25
  97.6 35.5 %collective-permute-start.21 = (f32[32,512]{0,1:T(8,128)S(1)}, f32[32,512]{0,1:T(8,128)}, u32[]{:S(2)}, u32[]{:S(2)}) collective-permute-start(f32[32,512]{0,1:T(8,128)S(1)} %get-tuple-element.41), channel_id=1, source_target_pairs={{0,48},{2,112},{4,176},{6,240},{8,16},{10,80},{12,144},{14,208},{1... | collective-permute-start | bytes 196616 | tf_op jit(solution)/shard_map/ppermute | solution.py:25
  135.3 5.7 %collective-permute-start.24 = (f32[1,32]{1,0:T(1,128)S(1)}, f32[1,32]{1,0:T(1,128)S(1)}, u32[]{:S(2)}, u32[]{:S(2)}) collective-permute-start(f32[1,32]{1,0:T(1,128)S(1)} %bitcast.50), channel_id=1, source_target_pairs={{0,6},{2,4},{4,2},{6,0},{1,7},{3,5},{5,3},{7,1},{8,14},{10,12},{12... | collective-permute-start | bytes 392 | tf_op jit(solution)/shard_map/ppermute | solution.py:29
  140.9 9.8 %collective-permute-start.25 = (f32[1,32]{1,0:T(1,128)S(1)}, f32[1,32]{1,0:T(1,128)S(1)}, u32[]{:S(2)}, u32[]{:S(2)}) collective-permute-start(f32[1,32]{1,0:T(1,128)S(1)} %add_add_fusion), channel_id=1, source_target_pairs={{0,8},{8,0},{1,9},{9,1},{2,10},{10,2},{3,11},{11,3},{4,12},{12,4},... | collective-permute-start | bytes 392 | tf_op jit(solution)/shard_map/ppermute | solution.py:33
  150.8 11.0 %collective-permute-start.26 = (bf16[32,1024]{1,0:T(8,128)(2,1)S(1)}, bf16[32,1024]{1,0:T(8,128)(2,1)S(1)}, u32[]{:S(2)}, u32[]{:S(2)}) collective-permute-start(bf16[32,1024]{1,0:T(8,128)(2,1)S(1)} %multiply_convert_fusion), channel_id=1, source_target_pairs={{0,0},{2,2},{4,4},{6,6},{8,40},{10,42},{12,44},{14,46},{16,16},{18... | collective-permute-start | bytes 196616 | tf_op jit(solution)/shard_map/ppermute | solution.py:25
  151.5 10.3 %collective-permute-start.27 = (bf16[32,1024]{1,0:T(8,128)(2,1)S(1)}, bf16[32,1024]{1,0:T(8,128)(2,1)S(1)}, u32[]{:S(2)}, u32[]{:S(2)}) collective-permute-start(bf16[32,1024]{1,0:T(8,128)(2,1)S(1)} %multiply_convert_fusion), channel_id=1, source_target_pairs={{0,16},{2,18},{4,20},{6,22},{8,56},{10,58},{12,60},{14,62},{16,0},... | collective-permute-start | bytes 196616 | tf_op jit(solution)/shard_map/ppermute | solution.py:25
  152.4 10.1 %collective-permute-start.28 = (bf16[32,1024]{1,0:T(8,128)(2,1)S(1)}, bf16[32,1024]{1,0:T(8,128)(2,1)S(1)}, u32[]{:S(2)}, u32[]{:S(2)}) collective-permute-start(bf16[32,1024]{1,0:T(8,128)(2,1)S(1)} %multiply_convert_fusion), channel_id=1, source_target_pairs={{0,32},{2,34},{4,36},{6,38},{8,8},{10,10},{12,12},{14,14},{16,48},... | collective-permute-start | bytes 196616 | tf_op jit(solution)/shard_map/ppermute | solution.py:25
  160.2 6.3 %collective-permute-start.29 = (bf16[32,1024]{1,0:T(8,128)(2,1)S(1)}, bf16[32,1024]{1,0:T(8,128)(2,1)S(1)}, u32[]{:S(2)}, u32[]{:S(2)}) collective-permute-start(bf16[32,1024]{1,0:T(8,128)(2,1)S(1)} %multiply_convert_fusion), channel_id=1, source_target_pairs={{0,48},{2,50},{4,52},{6,54},{8,24},{10,26},{12,28},{14,30},{16,32}... | collective-permute-start | bytes 196616 | tf_op jit(solution)/shard_map/ppermute | solution.py:25
  166.5 10.5 %collective-permute-start.30 = (bf16[128,1024]{1,0:T(8,128)(2,1)S(1)}, bf16[128,1024]{1,0:T(8,128)(2,1)S(1)}, u32[]{:S(2)}, u32[]{:S(2)}) collective-permute-start(bf16[128,1024]{1,0:T(8,128)(2,1)S(1)} %constant_dynamic-update-slice_fusion.4), channel_id=1, source_target_pairs={{0,0},{2,66},{4,132},{6,198},{8,8},{10,74},{12,140},{14,206},{16,1... | collective-permute-start | bytes 786440 | tf_op jit(solution)/shard_map/ppermute | solution.py:25
  167.2 9.9 %collective-permute-start.32 = (bf16[128,1024]{1,0:T(8,128)(2,1)S(1)}, bf16[128,1024]{1,0:T(8,128)(2,1)S(1)}, u32[]{:S(2)}, u32[]{:S(2)}) collective-permute-start(bf16[128,1024]{1,0:T(8,128)(2,1)S(1)} %constant_dynamic-update-slice_fusion.4), channel_id=1, source_target_pairs={{0,64},{2,2},{4,196},{6,134},{8,72},{10,10},{12,204},{14,142},{16,... | collective-permute-start | bytes 786440 | tf_op jit(solution)/shard_map/ppermute | solution.py:25
  169.1 9.8 %collective-permute-start.31 = (bf16[128,1024]{1,0:T(8,128)(2,1)S(1)}, bf16[128,1024]{1,0:T(8,128)(2,1)S(1)}, u32[]{:S(2)}, u32[]{:S(2)}) collective-permute-start(bf16[128,1024]{1,0:T(8,128)(2,1)S(1)} %constant_dynamic-update-slice_fusion.4), channel_id=1, source_target_pairs={{0,192},{2,130},{4,68},{6,6},{8,200},{10,138},{12,76},{14,14},{16,... | collective-permute-start | bytes 786440 | tf_op jit(solution)/shard_map/ppermute | solution.py:25
  172.2 9.8 %collective-permute-start.33 = (bf16[128,1024]{1,0:T(8,128)(2,1)S(1)}, bf16[128,1024]{1,0:T(8,128)(2,1)S(1)}, u32[]{:S(2)}, u32[]{:S(2)}) collective-permute-start(bf16[128,1024]{1,0:T(8,128)(2,1)S(1)} %constant_dynamic-update-slice_fusion.4), channel_id=1, source_target_pairs={{0,128},{2,194},{4,4},{6,70},{8,136},{10,202},{12,12},{14,78},{16,... | collective-permute-start | bytes 786440 | tf_op jit(solution)/shard_map/ppermute | solution.py:25
  186.7 17.9 %collective-permute-start.36 = (bf16[256,1792]{1,0:T(8,128)(2,1)S(1)}, bf16[256,1792]{1,0:T(8,128)(2,1)S(1)}, u32[]{:S(2)}, u32[]{:S(2)}) collective-permute-start(bf16[256,1792]{1,0:T(8,128)(2,1)S(1)} %pad_maximum_fusion.1), channel_id=1, source_target_pairs={{0,6},{2,4},{4,2},{6,0},{1,7},{3,5},{5,3},{7,1},{8,14},{10,12},{12... | collective-permute-start | bytes 2752520 | tf_op jit(solution)/shard_map/ppermute | solution.py:29
  191.1 18.2 %collective-permute-start.34 = (bf16[256,1792]{1,0:T(8,128)(2,1)S(1)}, bf16[256,1792]{1,0:T(8,128)(2,1)S(1)}, u32[]{:S(2)}, u32[]{:S(2)}) collective-permute-start(bf16[256,1792]{1,0:T(8,128)(2,1)S(1)} %pad_maximum_fusion), channel_id=1, source_target_pairs={{0,2},{2,0},{4,6},{6,4},{1,3},{3,1},{5,7},{7,5},{8,10},{10,8},{12,... | collective-permute-start | bytes 2752520 | tf_op jit(solution)/shard_map/ppermute | solution.py:29
  209.2 8.6 %collective-permute-start.37 = (bf16[128,1792]{1,0:T(8,128)(2,1)S(1)}, bf16[128,1792]{1,0:T(8,128)(2,1)S(1)}, u32[]{:S(2)}, u32[]{:S(2)}) collective-permute-start(bf16[128,1792]{1,0:T(8,128)(2,1)S(1)} %pad_maximum_fusion.11), channel_id=1, source_target_pairs={{0,2},{2,0},{4,6},{6,4},{1,3},{3,1},{5,7},{7,5},{8,10},{10,8},{12,... | collective-permute-start | bytes 1376264 | tf_op jit(solution)/shard_map/ppermute | solution.py:29
  210.9 10.0 %collective-permute-start.35 = (bf16[128,1792]{1,0:T(8,128)(2,1)S(1)}, bf16[128,1792]{1,0:T(8,128)(2,1)S(1)}, u32[]{:S(2)}, u32[]{:S(2)}) collective-permute-start(bf16[128,1792]{1,0:T(8,128)(2,1)S(1)} %pad_maximum_fusion.10), channel_id=1, source_target_pairs={{0,6},{2,4},{4,2},{6,0},{1,7},{3,5},{5,3},{7,1},{8,14},{10,12},{12... | collective-permute-start | bytes 1376264 | tf_op jit(solution)/shard_map/ppermute | solution.py:29
  221.1 19.2 %collective-permute-start.38 = (bf16[64,3584]{1,0:T(8,128)(2,1)S(1)}, bf16[64,3584]{1,0:T(8,128)(2,1)S(1)}, u32[]{:S(2)}, u32[]{:S(2)}) collective-permute-start(bf16[64,3584]{1,0:T(8,128)(2,1)S(1)} %pad_maximum_fusion.12), channel_id=1, source_target_pairs={{0,8},{8,0},{1,9},{9,1},{2,10},{10,2},{3,11},{11,3},{4,12},{12,4},... | collective-permute-start | bytes 1376264 | tf_op jit(solution)/shard_map/ppermute | solution.py:33
  240.4 15.8 %collective-permute-start.39 = (bf16[64,1792]{1,0:T(8,128)(2,1)S(1)}, bf16[64,1792]{1,0:T(8,128)(2,1)S(1)}, u32[]{:S(2)}, u32[]{:S(2)}) collective-permute-start(bf16[64,1792]{1,0:T(8,128)(2,1)S(1)} %pad_maximum_fusion.16), channel_id=1, source_target_pairs={{0,8},{8,0},{1,9},{9,1},{2,10},{10,2},{3,11},{11,3},{4,12},{12,4},... | collective-permute-start | bytes 688136 | tf_op jit(solution)/shard_map/ppermute | solution.py:33
  256.3 8.1 %collective-permute-start.42 = (bf16[128,896]{1,0:T(8,128)(2,1)S(1)}, bf16[128,896]{1,0:T(8,128)(2,1)S(1)}, u32[]{:S(2)}, u32[]{:S(2)}) collective-permute-start(bf16[128,896]{1,0:T(8,128)(2,1)S(1)} %pad_maximum_fusion.18), channel_id=1, source_target_pairs={{0,2},{2,0},{4,6},{6,4},{1,3},{3,1},{5,7},{7,5},{8,10},{10,8},{12,... | collective-permute-start | bytes 688136 | tf_op jit(solution)/shard_map/ppermute | solution.py:29
  256.5 10.1 %collective-permute-start.41 = (bf16[128,896]{1,0:T(8,128)(2,1)S(1)}, bf16[128,896]{1,0:T(8,128)(2,1)S(1)}, u32[]{:S(2)}, u32[]{:S(2)}) collective-permute-start(bf16[128,896]{1,0:T(8,128)(2,1)S(1)} %pad_maximum_fusion.17), channel_id=1, source_target_pairs={{0,6},{2,4},{4,2},{6,0},{1,7},{3,5},{5,3},{7,1},{8,14},{10,12},{12... | collective-permute-start | bytes 688136 | tf_op jit(solution)/shard_map/ppermute | solution.py:29
  264.5 9.8 %collective-permute-start.43 = (bf16[256,896]{1,0:T(8,128)(2,1)S(1)}, bf16[256,896]{1,0:T(8,128)(2,1)S(1)}, u32[]{:S(2)}, u32[]{:S(2)}) collective-permute-start(bf16[256,896]{1,0:T(8,128)(2,1)S(1)} %pad_maximum_fusion.13), channel_id=1, source_target_pairs={{0,6},{2,4},{4,2},{6,0},{1,7},{3,5},{5,3},{7,1},{8,14},{10,12},{12... | collective-permute-start | bytes 1376264 | tf_op jit(solution)/shard_map/ppermute | solution.py:29
  265.9 21.1 %collective-permute-start.40 = (bf16[128,1024]{1,0:T(8,128)(2,1)S(1)}, bf16[128,1024]{1,0:T(8,128)(2,1)S(1)}, u32[]{:S(2)}, u32[]{:S(2)}) collective-permute-start(bf16[128,1024]{1,0:T(8,128)(2,1)S(1)} %fusion), channel_id=1, source_target_pairs={{0,0},{2,66},{4,132},{6,198},{8,8},{10,74},{12,140},{14,206},{16,1... | collective-permute-start | bytes 786440 | tf_op jit(solution)/shard_map/ppermute | solution.py:25
  266.6 10.4 %collective-permute-start.45 = (bf16[256,896]{1,0:T(8,128)(2,1)S(1)}, bf16[256,896]{1,0:T(8,128)(2,1)S(1)}, u32[]{:S(2)}, u32[]{:S(2)}) collective-permute-start(bf16[256,896]{1,0:T(8,128)(2,1)S(1)} %pad_maximum_fusion.14), channel_id=1, source_target_pairs={{0,2},{2,0},{4,6},{6,4},{1,3},{3,1},{5,7},{7,5},{8,10},{10,8},{12,... | collective-permute-start | bytes 1376264 | tf_op jit(solution)/shard_map/ppermute | solution.py:29
  275.1 11.9 %collective-permute-start.44 = (bf16[128,1024]{1,0:T(8,128)(2,1)S(1)}, bf16[128,1024]{1,0:T(8,128)(2,1)S(1)}, u32[]{:S(2)}, u32[]{:S(2)}) collective-permute-start(bf16[128,1024]{1,0:T(8,128)(2,1)S(1)} %fusion.1), channel_id=1, source_target_pairs={{0,192},{2,130},{4,68},{6,6},{8,200},{10,138},{12,76},{14,14},{16,... | collective-permute-start | bytes 786440 | tf_op jit(solution)/shard_map/ppermute | solution.py:25
  277.6 9.5 %collective-permute-start.46 = (bf16[128,1024]{1,0:T(8,128)(2,1)S(1)}, bf16[128,1024]{1,0:T(8,128)(2,1)S(1)}, u32[]{:S(2)}, u32[]{:S(2)}) collective-permute-start(bf16[128,1024]{1,0:T(8,128)(2,1)S(1)} %fusion.2), channel_id=1, source_target_pairs={{0,64},{2,2},{4,196},{6,134},{8,72},{10,10},{12,204},{14,142},{16,... | collective-permute-start | bytes 786440 | tf_op jit(solution)/shard_map/ppermute | solution.py:25
  283.6 9.8 %collective-permute-start.47 = (bf16[128,1024]{1,0:T(8,128)(2,1)S(1)}, bf16[128,1024]{1,0:T(8,128)(2,1)S(1)}, u32[]{:S(2)}, u32[]{:S(2)}) collective-permute-start(bf16[128,1024]{1,0:T(8,128)(2,1)S(1)} %fusion.3), channel_id=1, source_target_pairs={{0,128},{2,194},{4,4},{6,70},{8,136},{10,202},{12,12},{14,78},{16,... | collective-permute-start | bytes 786440 | tf_op jit(solution)/shard_map/ppermute | solution.py:25
  293.6 11.9 %collective-permute-start.48 = (bf16[32,1024]{1,0:T(8,128)(2,1)S(1)}, bf16[32,1024]{1,0:T(8,128)(2,1)S(1)}, u32[]{:S(2)}, u32[]{:S(2)}) collective-permute-start(bf16[32,1024]{1,0:T(8,128)(2,1)S(1)} %get-tuple-element.27), channel_id=1, source_target_pairs={{0,0},{2,2},{4,4},{6,6},{8,40},{10,42},{12,44},{14,46},{16,16},{18... | collective-permute-start | bytes 196616 | tf_op jit(solution)/shard_map/ppermute | solution.py:25
  294.2 11.3 %collective-permute-start.49 = (bf16[32,1024]{1,0:T(8,128)(2,1)S(1)}, bf16[32,1024]{1,0:T(8,128)(2,1)S(1)}, u32[]{:S(2)}, u32[]{:S(2)}) collective-permute-start(bf16[32,1024]{1,0:T(8,128)(2,1)S(1)} %get-tuple-element.30), channel_id=1, source_target_pairs={{0,16},{2,18},{4,20},{6,22},{8,56},{10,58},{12,60},{14,62},{16,0},... | collective-permute-start | bytes 196616 | tf_op jit(solution)/shard_map/ppermute | solution.py:25
  301.1 7.2 %collective-permute-start.50 = (bf16[32,1024]{1,0:T(8,128)(2,1)S(1)}, bf16[32,1024]{1,0:T(8,128)(2,1)S(1)}, u32[]{:S(2)}, u32[]{:S(2)}) collective-permute-start(bf16[32,1024]{1,0:T(8,128)(2,1)S(1)} %get-tuple-element.29), channel_id=1, source_target_pairs={{0,32},{2,34},{4,36},{6,38},{8,8},{10,10},{12,12},{14,14},{16,48},... | collective-permute-start | bytes 196616 | tf_op jit(solution)/shard_map/ppermute | solution.py:25
  303.4 6.3 %collective-permute-start.51 = (bf16[32,1024]{1,0:T(8,128)(2,1)S(1)}, bf16[32,1024]{1,0:T(8,128)(2,1)S(1)}, u32[]{:S(2)}, u32[]{:S(2)}) collective-permute-start(bf16[32,1024]{1,0:T(8,128)(2,1)S(1)} %get-tuple-element.28), channel_id=1, source_target_pairs={{0,48},{2,50},{4,52},{6,54},{8,24},{10,26},{12,28},{14,30},{16,32}... | collective-permute-start | bytes 196616 | tf_op jit(solution)/shard_map/ppermute | solution.py:25
  (16 other events, 143.7 us)
where the time goes:
time: 312 us; the launch traced here: 310 us
  waiting for transfers between devices  143 us (46%)
  starting transfers between devices  130 us (42%)
  matrix products  16.8 us (5%)
  local copies, waits for them, and re-layouts  8.98 us (3%)
  Pallas kernels  5.89 us (2%)
  other arithmetic  4.31 us (1%)
    ppermute x29, starting transfers between devices, sent(): return lax.ppermute(array, GRID, pairs)  87.8 us
    ppermute x29, waiting for transfers between devices, sent(): return lax.ppermute(array, GRID, pairs)  75.8 us
    ppermute x15, waiting for transfers between devices, over_x(): return lax.ppermute(array, 'x', [(i, i ^ mask) for i in range(4)])  44.7 us
    ppermute x3, starting transfers between devices, over_zh(): return lax.ppermute(array, 'zh', [(0, 1), (1, 0)])  23.9 us
    ppermute x3, waiting for transfers between devices, over_zh(): return lax.ppermute(array, 'zh', [(0, 1), (1, 0)])  20.9 us
    ppermute x15, starting transfers between devices, over_x(): return lax.ppermute(array, 'x', [(i, i ^ mask) for i in range(4)])  17.4 us
    dot_general x20, matrix products, dot(): return jnp.dot(a, b, preferred_element_type=jnp.float32)  16.8 us
    unnamed x33, local copies, waits for them, and re-layouts  6.35 us
  transfers between devices with their start and end apart: 52, of which 27 were waited for; matrix products, arithmetic and copies ran while one was open for 5% of the time, Pallas kernels for 1%

commit v1 on v0

--- a/solution.py
+++ b/solution.py
@@ -46,18 +46,30 @@
     return lambda y, zl, zh, x: (y ^ x ^ mask, zl, zh, x)
 
 
+def near_target(place):
+    part, step = divmod(place, 2)
+    return lambda y, zl, zh, x: (y, zl ^ (2 * (part ^ turn(x)) + step), zh, x)
+
+
+def turn(x):
+    return (x >> 1) ^ (x & 1)
+
+
 def home_target(place):
     part, step = divmod(place, 2)
     return lambda y, zl, zh, x: (
-        y ^ x,
-        zl ^ (2 * (part ^ zh) + step),
-        zl >> 1,
         y,
-    )
-
-
-def column_target(y, zl, zh, x):
-    return 2 * (y & 1) + (zl >> 1), 2 * (y >> 1) + (zl & 1), zh, x
+        2 * (turn(x) ^ (zl >> 1)) + ((zl & 1) ^ step),
+        zh ^ part,
+        2 * (x >> 1) + (zl >> 1),
+    )
+
+
+def columns_over_y(weight):
+    blocks = [weight] + [
+        lax.ppermute(weight, "y", [(i, i ^ mask) for i in range(4)]) for mask in (2, 1, 3)
+    ]
+    return jnp.concatenate(blocks, axis=1)
 
 
 def gathered(rows):
@@ -80,8 +92,12 @@
     away1, away2 = pair(1, 2), pair(3, 2)
     stay1, stay2 = pair(0, 3), pair(0, 1)
     half = blocks[0].shape[0]
-    got1 = together(over_x, [dot(away1, w).astype(dtype) for w in first], 1)
-    got2 = together(over_x, [dot(away2, w).astype(dtype) for w in second], 3)
+    sides = [
+        jnp.concatenate([dot(away, w).astype(dtype) for w in weights], axis=1)
+        for away, weights in ((away1, first), (away2, second))
+    ]
+    sides = lax.optimization_barrier(sides)
+    got1, got2 = [jnp.split(over_x(a, mask), 2, axis=1) for a, mask in zip(sides, (1, 3))]
     sum1 = [dot(stay1, w) + g for w, g in zip(first, got1)]
     sum2 = [dot(stay2, w) + g for w, g in zip(second, got2)]
     got1 = together(over_x, [s[half:].astype(dtype) for s in sum1], 3)
@@ -210,7 +226,7 @@
                 pltpu.VMEM((rows, head), jnp.float32),
             ],
         ),
-        compiler_params=pltpu.CompilerParams(vmem_limit_bytes=32 << 20),
+        compiler_params=pltpu.CompilerParams(vmem_limit_bytes=56 << 20),
         cost_estimate=pl.CostEstimate(
             flops=6 * rows * half_len * head,
             bytes_accessed=4 * half_len * head,
@@ -246,10 +262,9 @@
 ):
     core = lax.axis_index("core")
     features = norm_gain.shape[0] * 8
-    out_weight = sent(out_weight, column_target)
+    out_weight = columns_over_y(out_weight)
     other_gate = over_core(gate_weight)
     other_up = over_core(up_weight)
-    other_down = over_core(down_weight)
     length = lax.dynamic_index_in_dim(lengths, lax.axis_index(REQ), keepdims=False)
     parts = attended_parts(
         queries[0],
@@ -261,19 +276,45 @@
         parents[0],
         core,
     )
-    parts, out_weight, other_gate, other_up, other_down = lax.optimization_barrier(
-        (parts, out_weight, other_gate, other_up, other_down)
+    parts, out_weight, other_gate, other_up = lax.optimization_barrier(
+        (parts, out_weight, other_gate, other_up)
     )
     attention = attended(*parts, queries.shape[1] // 2)
     other_out = over_core(out_weight)
     tokens = attention.shape[0]
 
-    (mine,), (theirs,) = summed_over_x(
-        gathered(attention), [out_weight], [other_out], jnp.float32
-    )
-    both = jnp.concatenate([mine, theirs], axis=1)
-    came = [sent(both[k * tokens : (k + 1) * tokens], home_target(k)) for k in range(4)]
-    width = mine.shape[1]
+    rows = jnp.concatenate([sent(attention, near_target(place)) for place in range(4)])
+    rows, out_weight, other_out = lax.optimization_barrier((rows, out_weight, other_out))
+    y, zh, x = [lax.axis_index(name) for name in ("y", "zh", "x")]
+    odd = ((y & 1) ^ (x >> 1)) == 1
+
+    def classes(products):
+        half = products.shape[1] // 2
+        a, b = products[:, :half], products[:, half:]
+        return jnp.where(odd, b, a), jnp.where(odd, a, b)
+
+    half = 2 * tokens
+    mine_stay, mine_away = classes(dot(rows, out_weight))
+    theirs = dot(rows, other_out)
+    mine_away, theirs_away = lax.optimization_barrier((mine_away, theirs[half:]))
+    mine_came, theirs_came = over_x(mine_away, 3), over_x(theirs_away, 1)
+    mine = mine_stay + mine_came
+    mine_came = over_x(mine[half:], 1)
+    theirs_stay, theirs_away = classes(theirs[:half] + theirs_came)
+    theirs_came = over_x(theirs_away, 3)
+    mine = mine[:half] + mine_came
+    theirs = theirs_stay + theirs_came
+    width = mine.shape[1] // 2
+    swap = (zh ^ (y >> 1)) == 1
+
+    def item(part, step):
+        near, far = [
+            jnp.concatenate([a[step * tokens : (step + 1) * tokens, k * width : (k + 1) * width] for a in (mine, theirs)], axis=1)
+            for k in (part, 1 - part)
+        ]
+        return jnp.where(swap, far, near)
+
+    came = [sent(item(*divmod(place, 2)), home_target(place)) for place in range(4)]
     own_first = core == 0
     sides = []
     for step in range(2):
@@ -288,12 +329,13 @@
     )
     state = residual + projected
 
-    squares = jnp.sum(state * state, axis=1)[None]
-    squares = sum([over_x(squares, mask) for mask in (1, 2, 3)], squares)
-    squares = squares + over_zh(squares)
-    normed = (state * lax.rsqrt(squares[0] / features + EPSILON)[:, None] * norm_gain).astype(
+    squares = jnp.broadcast_to(jnp.sum(state * state, axis=1), (8, 1, tokens))
+    squares = lax.all_to_all(squares, KVH, 0, 0, tiled=True).sum(axis=(0, 1))
+    normed = (state * lax.rsqrt(squares / features + EPSILON)[:, None] * norm_gain).astype(
         jnp.bfloat16
     )
+
+    other_down = over_core(down_weight)
 
     first, second = summed_over_x(
         gathered(normed), [gate_weight, up_weight], [other_gate, other_up], jnp.bfloat16

time: 312 us -> 252 us (0.81)
  starting transfers between devices: 130 us -> 73.3 us
  waiting for transfers between devices: 143 us -> 121 us
  blocking collectives: 0 us -> 17.8 us
  local copies, waits for them, and re-layouts: 8.98 us -> 4.58 us
  Pallas kernels: 5.89 us -> 10 us
    ppermute x29 -> x24, waiting for transfers between devices: 75.8 us -> 32 us  [sent(): return lax.ppermute(array, GRID, pairs)]
    ppermute x29 -> x24, starting transfers between devices: 87.8 us -> 52.4 us  [sent(): return lax.ppermute(array, GRID, pairs)]
    ppermute x3 -> x2, starting transfers between devices: 23.9 us -> 4.04 us  [over_zh(): return lax.ppermute(array, 'zh', [(0, 1), (1, 0)])]
    all_to_all x0 -> x1, blocking collectives: none -> 17.8 us  [local(): squares = lax.all_to_all(squares, KVH, 0, 0, tiled=True).sum(axis=(0, 1))]
    ppermute x0 -> x3, waiting for transfers between devices: none -> 11 us  [columns_over_y(): lax.ppermute(weight, 'y', [(i, i ^ mask) for i in range(4)])]
    ppermute x3 -> x2, waiting for transfers between devices: 20.9 us -> 27.4 us  [over_zh(): return lax.ppermute(array, 'zh', [(0, 1), (1, 0)])]
    ppermute x15 -> x12, starting transfers between devices: 17.4 us -> 11.7 us  [over_x(): return lax.ppermute(array, 'x', [(i, i ^ mask) for i in range(4)])]
    unnamed x33 -> x22, local copies, waits for them, and re-layouts: 6.35 us -> 1.6 us
  transfers between devices with their start and end apart: 52 -> 46, of which waited for: 27 -> 27; matrix products, arithmetic and copies ran while one was open for 5% -> 6% of each run, Pallas kernels for 1% -> 4%
where the time goes in v1:
time: 252 us; the launch traced here: 250 us
  waiting for transfers between devices  121 us (48%)
  starting transfers between devices  73.3 us (29%)
  blocking collectives  17.8 us (7%)
  matrix products  17.7 us (7%)
  Pallas kernels  10 us (4%)
  local copies, waits for them, and re-layouts  4.58 us (2%)
  other arithmetic  4.06 us (2%)
    ppermute x24, starting transfers between devices, sent(): return lax.ppermute(array, GRID, pairs)  52.4 us
    ppermute x12, waiting for transfers between devices, over_x(): return lax.ppermute(array, 'x', [(i, i ^ mask) for i in range(4)])  46.7 us
    ppermute x24, waiting for transfers between devices, sent(): return lax.ppermute(array, GRID, pairs)  32 us
    ppermute x2, waiting for transfers between devices, over_zh(): return lax.ppermute(array, 'zh', [(0, 1), (1, 0)])  27.4 us
    all_to_all x1, blocking collectives, local(): squares = lax.all_to_all(squares, KVH, 0, 0, tiled=True).sum(axis=(0, 1))  17.8 us
    dot_general x18, matrix products, dot(): return jnp.dot(a, b, preferred_element_type=jnp.float32)  17.7 us
    ppermute x12, starting transfers between devices, over_x(): return lax.ppermute(array, 'x', [(i, i ^ mask) for i in range(4)])  11.7 us
    ppermute x3, waiting for transfers between devices, columns_over_y(): lax.ppermute(weight, 'y', [(i, i ^ mask) for i in range(4)])  11 us
  transfers between devices with their start and end apart: 46, of which 27 were waited for; matrix products, arithmetic and copies ran while one was open for 6% of the time, Pallas kernels for 4%

profile of v1, /device:TPU:24, one launch (start us, length us, event | category | flops | bytes accessed | tf_op | source)
XLA Modules:
  0.0 249.7 jit_solution(11402522071586329000)
XLA Ops:
  8.5 7.9 %attend.1 = (f32[512,128]{1,0:T(8,128)}, f32[512,128]{1,0:T(8,128)}) custom-call(s32[2]{0:T(128)} %pad_add_fusion.info, bf16[64,1024]{1,0:T(8,128)(2,1)} %bitcast.44, bf16[64,128]{1,0:T(8,128)(2,1)} %bitcast.45, bf16[64,128]{1,0:T(8,128)(2,1)} %bitcast.46, s32[64,1]{1,0:T(8,128)} %copy.16.parents, bf16[4096,128]{1,0:T(8,128)(2,1)} %bitcast.42, ...), custom_call_target="tpu_custom_call" | custom-call | flops 1610612736 | bytes 2097152 | tf_op jit(solution)/shard_map/attend/pallas_call | solution.py:207
  17.1 9.6 %collective-permute-done.1 = bf16[1024,256]{1,0:T(8,128)(2,1)S(1)} collective-permute-done((bf16[1024,256]{1,0:T(8,128)(2,1)}, bf16[1024,256]{1,0:T(8,128)(2,1)S(1)}, u32[]{:S(2)}, u32[]{:S(2)}) %collective-permute-start.1) | collective-permute-done | bytes 524320 | tf_op jit(solution)/shard_map/ppermute | solution.py:70
  29.4 3.7 %collective-permute-done.5.came = f32[512,128]{1,0:T(8,128)S(1)} collective-permute-done((f32[512,128]{1,0:T(8,128)S(1)}, f32[512,128]{1,0:T(8,128)S(1)}, u32[]{:S(2)}, u32[]{:S(2)}) %collective-permute-start.5) | collective-permute-done | bytes 262176 | tf_op jit(solution)/shard_map/ppermute | solution.py:37
  33.7 2.1 combine.1
  37.3 1.9 collective-permute-start.7
  39.3 5.2 %collective-permute-start.8 = (bf16[32,1024]{1,0:T(8,128)(2,1)}, bf16[32,1024]{1,0:T(8,128)(2,1)S(1)}, u32[]{:S(2)}, u32[]{:S(2)}) collective-permute-start(bf16[32,1024]{1,0:T(8,128)(2,1)} %combine.1), channel_id=1, source_target_pairs={{0,32},{2,2},{4,4},{6,38},{8,40},{10,10},{12,12},{14,46},{16,48},{... | collective-permute-start | bytes 196616 | tf_op jit(solution)/shard_map/ppermute | solution.py:25
  44.6 3.6 %collective-permute-done.8 = bf16[32,1024]{1,0:T(8,128)(2,1)S(1)} collective-permute-done((bf16[32,1024]{1,0:T(8,128)(2,1)}, bf16[32,1024]{1,0:T(8,128)(2,1)S(1)}, u32[]{:S(2)}, u32[]{:S(2)}) %collective-permute-start.8) | collective-permute-done | bytes 65568 | tf_op jit(solution)/shard_map/ppermute | solution.py:25
  48.2 2.7 %collective-permute-done.9 = bf16[32,1024]{1,0:T(8,128)(2,1)S(1)} collective-permute-done((bf16[32,1024]{1,0:T(8,128)(2,1)}, bf16[32,1024]{1,0:T(8,128)(2,1)S(1)}, u32[]{:S(2)}, u32[]{:S(2)}) %collective-permute-start.9) | collective-permute-done | bytes 65568 | tf_op jit(solution)/shard_map/ppermute | solution.py:25
  50.9 2.0 fusion.26
  53.5 2.8 %collective-permute-start.11 = (f32[128,512]{1,0:T(8,128)S(1)}, f32[128,512]{1,0:T(8,128)S(1)}, u32[]{:S(2)}, u32[]{:S(2)}) collective-permute-start(f32[128,512]{1,0:T(8,128)S(1)} %slice_select_fusion), channel_id=1, source_target_pairs={{0,6},{2,4},{4,2},{6,0},{1,7},{3,5},{5,3},{7,1},{8,14},{10,12},{12... | collective-permute-start | bytes 786440 | tf_op jit(solution)/shard_map/ppermute | solution.py:29
  56.3 5.4 %collective-permute-done.11 = f32[128,512]{1,0:T(8,128)S(1)} collective-permute-done((f32[128,512]{1,0:T(8,128)S(1)}, f32[128,512]{1,0:T(8,128)S(1)}, u32[]{:S(2)}, u32[]{:S(2)}) %collective-permute-start.11) | collective-permute-done | bytes 262176 | tf_op jit(solution)/shard_map/ppermute | solution.py:29
  61.8 1.8 collective-permute-done.13
  64.8 2.0 collective-permute-done.12
  66.8 3.1 %collective-permute-done.14 = f32[64,512]{1,0:T(8,128)S(1)} collective-permute-done((f32[64,512]{1,0:T(8,128)S(1)}, f32[64,512]{1,0:T(8,128)S(1)}, u32[]{:S(2)}, u32[]{:S(2)}) %collective-permute-start.14) | collective-permute-done | bytes 131104 | tf_op jit(solution)/shard_map/ppermute | solution.py:29
  70.7 5.3 %collective-permute-start.16 = (f32[32,512]{1,0:T(8,128)S(1)}, f32[32,512]{1,0:T(8,128)S(1)}, u32[]{:S(2)}, u32[]{:S(2)}) collective-permute-start(f32[32,512]{1,0:T(8,128)S(1)} %get-tuple-element.53), channel_id=1, source_target_pairs={{0,8},{2,40},{4,44},{6,12},{8,0},{10,32},{12,36},{14,4},{16,24},{1... | collective-permute-start | bytes 196616 | tf_op jit(solution)/shard_map/ppermute | solution.py:25
  76.0 1.8 collective-permute-start.17
  79.0 2.5 %collective-permute-done.17 = f32[32,512]{1,0:T(8,128)S(1)} collective-permute-done((f32[32,512]{1,0:T(8,128)S(1)}, f32[32,512]{1,0:T(8,128)S(1)}, u32[]{:S(2)}, u32[]{:S(2)}) %collective-permute-start.17) | collective-permute-done | bytes 65568 | tf_op jit(solution)/shard_map/ppermute | solution.py:25
  81.5 3.5 %collective-permute-done.18 = f32[32,512]{1,0:T(8,128)S(1)} collective-permute-done((f32[32,512]{1,0:T(8,128)S(1)}, f32[32,512]{1,0:T(8,128)S(1)}, u32[]{:S(2)}, u32[]{:S(2)}) %collective-permute-start.18) | collective-permute-done | bytes 65568 | tf_op jit(solution)/shard_map/ppermute | solution.py:25
  85.3 17.8 %all_to_all.5 = f32[8,1,32]{2,1,0:T(1,128)S(1)} all-to-all(f32[8,1,32]{2,1,0:T(1,128)S(1)} %broadcast_in_dim.2), channel_id=1, replica_groups=mesh['y'=4,'zl'=4,'zh'=2,'x'=4,'core'=2] {'zh','x'}, dimensions={0} | all-to-all | bytes 2048 | tf_op jit(solution)/shard_map/all_to_all | solution.py:333
  104.1 3.4 %collective-permute-start.21 = (bf16[32,1024]{1,0:T(8,128)(2,1)S(1)}, bf16[32,1024]{1,0:T(8,128)(2,1)S(1)}, u32[]{:S(2)}, u32[]{:S(2)}) collective-permute-start(bf16[32,1024]{1,0:T(8,128)(2,1)S(1)} %multiply_convert_fusion), channel_id=1, source_target_pairs={{0,32},{2,34},{4,36},{6,38},{8,8},{10,10},{12,12},{14,14},{16,48},... | collective-permute-start | bytes 196616 | tf_op jit(solution)/shard_map/ppermute | solution.py:25
  107.5 2.9 %collective-permute-start.22 = (bf16[32,1024]{1,0:T(8,128)(2,1)S(1)}, bf16[32,1024]{1,0:T(8,128)(2,1)S(1)}, u32[]{:S(2)}, u32[]{:S(2)}) collective-permute-start(bf16[32,1024]{1,0:T(8,128)(2,1)S(1)} %multiply_convert_fusion), channel_id=1, source_target_pairs={{0,48},{2,50},{4,52},{6,54},{8,24},{10,26},{12,28},{14,30},{16,32}... | collective-permute-start | bytes 196616 | tf_op jit(solution)/shard_map/ppermute | solution.py:25
  111.1 2.5 collective-permute-done.22
  114.3 2.7 %collective-permute-start.25 = (bf16[128,1024]{1,0:T(8,128)(2,1)S(1)}, bf16[128,1024]{1,0:T(8,128)(2,1)S(1)}, u32[]{:S(2)}, u32[]{:S(2)}) collective-permute-start(bf16[128,1024]{1,0:T(8,128)(2,1)S(1)} %constant_dynamic-update-slice_fusion), channel_id=1, source_target_pairs={{0,64},{2,2},{4,196},{6,134},{8,72},{10,10},{12,204},{14,142},{16,... | collective-permute-start | bytes 786440 | tf_op jit(solution)/shard_map/ppermute | solution.py:25
  116.9 3.0 %collective-permute-start.24 = (bf16[128,1024]{1,0:T(8,128)(2,1)S(1)}, bf16[128,1024]{1,0:T(8,128)(2,1)S(1)}, u32[]{:S(2)}, u32[]{:S(2)}) collective-permute-start(bf16[128,1024]{1,0:T(8,128)(2,1)S(1)} %constant_dynamic-update-slice_fusion), channel_id=1, source_target_pairs={{0,192},{2,130},{4,68},{6,6},{8,200},{10,138},{12,76},{14,14},{16,... | collective-permute-start | bytes 786440 | tf_op jit(solution)/shard_map/ppermute | solution.py:25
  120.0 4.2 %collective-permute-start.26 = (bf16[128,1024]{1,0:T(8,128)(2,1)S(1)}, bf16[128,1024]{1,0:T(8,128)(2,1)S(1)}, u32[]{:S(2)}, u32[]{:S(2)}) collective-permute-start(bf16[128,1024]{1,0:T(8,128)(2,1)S(1)} %constant_dynamic-update-slice_fusion), channel_id=1, source_target_pairs={{0,128},{2,194},{4,4},{6,70},{8,136},{10,202},{12,12},{14,78},{16,... | collective-permute-start | bytes 786440 | tf_op jit(solution)/shard_map/ppermute | solution.py:25
  124.3 2.1 collective-permute-done.24
  126.5 3.2 %collective-permute-done.26 = bf16[128,1024]{1,0:T(8,128)(2,1)S(1)} collective-permute-done((bf16[128,1024]{1,0:T(8,128)(2,1)S(1)}, bf16[128,1024]{1,0:T(8,128)(2,1)S(1)}, u32[]{:S(2)}, u32[]{:S(2)}) %collective-permute-start.26) | collective-permute-done | bytes 262176 | tf_op jit(solution)/shard_map/ppermute | solution.py:25
  132.0 2.2 convolution_convert_fusion.1
  134.2 2.2 convolution_convert_fusion
  137.3 15.5 %collective-permute-done.29 = bf16[256,1792]{1,0:T(8,128)(2,1)S(1)} collective-permute-done((bf16[256,1792]{1,0:T(8,128)(2,1)S(1)}, bf16[256,1792]{1,0:T(8,128)(2,1)S(1)}, u32[]{:S(2)}, u32[]{:S(2)}) %collective-permute-start.29) | collective-permute-done | bytes 917536 | tf_op jit(solution)/shard_map/ppermute | solution.py:29
  152.8 2.2 convolution_add_fusion
  155.0 2.2 convolution_add_fusion.1
  160.2 5.8 %collective-permute-done.30 = bf16[128,1792]{1,0:T(8,128)(2,1)S(1)} collective-permute-done((bf16[128,1792]{1,0:T(8,128)(2,1)S(1)}, bf16[128,1792]{1,0:T(8,128)(2,1)S(1)}, u32[]{:S(2)}, u32[]{:S(2)}) %collective-permute-start.30) | collective-permute-done | bytes 458784 | tf_op jit(solution)/shard_map/ppermute | solution.py:29
  166.1 2.7 %collective-permute-done.28 = bf16[128,1792]{1,0:T(8,128)(2,1)S(1)} collective-permute-done((bf16[128,1792]{1,0:T(8,128)(2,1)S(1)}, bf16[128,1792]{1,0:T(8,128)(2,1)S(1)}, u32[]{:S(2)}, u32[]{:S(2)}) %collective-permute-start.28) | collective-permute-done | bytes 458784 | tf_op jit(solution)/shard_map/ppermute | solution.py:29
  169.2 21.0 %collective-permute-done.31 = bf16[64,3584]{1,0:T(8,128)(2,1)S(1)} collective-permute-done((bf16[64,3584]{1,0:T(8,128)(2,1)S(1)}, bf16[64,3584]{1,0:T(8,128)(2,1)S(1)}, u32[]{:S(2)}, u32[]{:S(2)}) %collective-permute-start.31) | collective-permute-done | bytes 458784 | tf_op jit(solution)/shard_map/ppermute | solution.py:33
  190.4 3.8 %collective-permute-start.32 = (bf16[64,1792]{1,0:T(8,128)(2,1)S(1)}, bf16[64,1792]{1,0:T(8,128)(2,1)S(1)}, u32[]{:S(2)}, u32[]{:S(2)}) collective-permute-start(bf16[64,1792]{1,0:T(8,128)(2,1)S(1)} %pad_maximum_fusion.9), channel_id=1, source_target_pairs={{0,8},{8,0},{1,9},{9,1},{2,10},{10,2},{3,11},{11,3},{4,12},{12,4},... | collective-permute-start | bytes 688136 | tf_op jit(solution)/shard_map/ppermute | solution.py:33
  194.2 6.4 %collective-permute-done.32 = bf16[64,1792]{1,0:T(8,128)(2,1)S(1)} collective-permute-done((bf16[64,1792]{1,0:T(8,128)(2,1)S(1)}, bf16[64,1792]{1,0:T(8,128)(2,1)S(1)}, u32[]{:S(2)}, u32[]{:S(2)}) %collective-permute-start.32) | collective-permute-done | bytes 229408 | tf_op jit(solution)/shard_map/ppermute | solution.py:33
  203.7 5.5 %collective-permute-done.36 = bf16[128,896]{1,0:T(8,128)(2,1)S(1)} collective-permute-done((bf16[128,896]{1,0:T(8,128)(2,1)S(1)}, bf16[128,896]{1,0:T(8,128)(2,1)S(1)}, u32[]{:S(2)}, u32[]{:S(2)}) %collective-permute-start.36) | collective-permute-done | bytes 229408 | tf_op jit(solution)/shard_map/ppermute | solution.py:29
  209.2 2.6 %collective-permute-start.37 = (bf16[256,896]{1,0:T(8,128)(2,1)S(1)}, bf16[256,896]{1,0:T(8,128)(2,1)S(1)}, u32[]{:S(2)}, u32[]{:S(2)}) collective-permute-start(bf16[256,896]{1,0:T(8,128)(2,1)S(1)} %pad_maximum_fusion.6), channel_id=1, source_target_pairs={{0,6},{2,4},{4,2},{6,0},{1,7},{3,5},{5,3},{7,1},{8,14},{10,12},{12... | collective-permute-start | bytes 1376264 | tf_op jit(solution)/shard_map/ppermute | solution.py:29
  214.0 5.0 %collective-permute-done.37 = bf16[256,896]{1,0:T(8,128)(2,1)S(1)} collective-permute-done((bf16[256,896]{1,0:T(8,128)(2,1)S(1)}, bf16[256,896]{1,0:T(8,128)(2,1)S(1)}, u32[]{:S(2)}, u32[]{:S(2)}) %collective-permute-start.37) | collective-permute-done | bytes 458784 | tf_op jit(solution)/shard_map/ppermute | solution.py:29
  219.9 2.9 %collective-permute-start.38 = (bf16[128,1024]{1,0:T(8,128)(2,1)S(1)}, bf16[128,1024]{1,0:T(8,128)(2,1)S(1)}, u32[]{:S(2)}, u32[]{:S(2)}) collective-permute-start(bf16[128,1024]{1,0:T(8,128)(2,1)S(1)} %fusion.1), channel_id=1, source_target_pairs={{0,192},{2,130},{4,68},{6,6},{8,200},{10,138},{12,76},{14,14},{16,... | collective-permute-start | bytes 786440 | tf_op jit(solution)/shard_map/ppermute | solution.py:25
  223.2 2.5 %collective-permute-start.40 = (bf16[128,1024]{1,0:T(8,128)(2,1)S(1)}, bf16[128,1024]{1,0:T(8,128)(2,1)S(1)}, u32[]{:S(2)}, u32[]{:S(2)}) collective-permute-start(bf16[128,1024]{1,0:T(8,128)(2,1)S(1)} %fusion.2), channel_id=1, source_target_pairs={{0,64},{2,2},{4,196},{6,134},{8,72},{10,10},{12,204},{14,142},{16,... | collective-permute-start | bytes 786440 | tf_op jit(solution)/shard_map/ppermute | solution.py:25
  226.7 5.0 %collective-permute-start.41 = (bf16[128,1024]{1,0:T(8,128)(2,1)S(1)}, bf16[128,1024]{1,0:T(8,128)(2,1)S(1)}, u32[]{:S(2)}, u32[]{:S(2)}) collective-permute-start(bf16[128,1024]{1,0:T(8,128)(2,1)S(1)} %fusion.3), channel_id=1, source_target_pairs={{0,128},{2,194},{4,4},{6,70},{8,136},{10,202},{12,12},{14,78},{16,... | collective-permute-start | bytes 786440 | tf_op jit(solution)/shard_map/ppermute | solution.py:25
  231.7 4.7 %collective-permute-done.41 = bf16[128,1024]{1,0:T(8,128)(2,1)S(1)} collective-permute-done((bf16[128,1024]{1,0:T(8,128)(2,1)S(1)}, bf16[128,1024]{1,0:T(8,128)(2,1)S(1)}, u32[]{:S(2)}, u32[]{:S(2)}) %collective-permute-start.41) | collective-permute-done | bytes 262176 | tf_op jit(solution)/shard_map/ppermute | solution.py:25
  237.3 2.2 collective-permute-start.43
  239.5 3.3 %collective-permute-start.44 = (bf16[32,1024]{1,0:T(8,128)(2,1)S(1)}, bf16[32,1024]{1,0:T(8,128)(2,1)S(1)}, u32[]{:S(2)}, u32[]{:S(2)}) collective-permute-start(bf16[32,1024]{1,0:T(8,128)(2,1)S(1)} %get-tuple-element.41), channel_id=1, source_target_pairs={{0,32},{2,34},{4,36},{6,38},{8,8},{10,10},{12,12},{14,14},{16,48},... | collective-permute-start | bytes 196616 | tf_op jit(solution)/shard_map/ppermute | solution.py:25
  243.9 2.8 %collective-permute-done.44 = bf16[32,1024]{1,0:T(8,128)(2,1)S(1)} collective-permute-done((bf16[32,1024]{1,0:T(8,128)(2,1)S(1)}, bf16[32,1024]{1,0:T(8,128)(2,1)S(1)}, u32[]{:S(2)}, u32[]{:S(2)}) %collective-permute-start.44) | collective-permute-done | bytes 65568 | tf_op jit(solution)/shard_map/ppermute | solution.py:25
  246.7 2.3 collective-permute-done.45
  (141 shorter events, 36.8 us)
Async XLA Ops:
  0.0 28.7 %collective-permute-start.3 = (bf16[1024,896]{1,0:T(8,128)(2,1)}, bf16[1024,896]{1,0:T(8,128)(2,1)}, u32[]{:S(2)}, u32[]{:S(2)}) collective-permute-start(bf16[1024,896]{1,0:T(8,128)(2,1)} %param.23), channel_id=1, source_target_pairs={{0,1},{1,0},{2,3},{3,2},{4,5},{5,4},{6,7},{7,6},{8,9},{9,8},{10,11... | collective-permute-start | bytes 5505032 | tf_op jit(solution)/shard_map/ppermute | solution.py:37
  0.0 28.7 %collective-permute-start.4 = (bf16[1024,896]{1,0:T(8,128)(2,1)}, bf16[1024,896]{1,0:T(8,128)(2,1)}, u32[]{:S(2)}, u32[]{:S(2)}) collective-permute-start(bf16[1024,896]{1,0:T(8,128)(2,1)} %param.24), channel_id=1, source_target_pairs={{0,1},{1,0},{2,3},{3,2},{4,5},{5,4},{6,7},{7,6},{8,9},{9,8},{10,11... | collective-permute-start | bytes 5505032 | tf_op jit(solution)/shard_map/ppermute | solution.py:37
  0.5 16.6 %collective-permute-start = (bf16[1024,256]{1,0:T(8,128)(2,1)}, bf16[1024,256]{1,0:T(8,128)(2,1)S(1)}, u32[]{:S(2)}, u32[]{:S(2)}) collective-permute-start(bf16[1024,256]{1,0:T(8,128)(2,1)} %param.21), channel_id=1, source_target_pairs={{0,128},{64,192},{128,0},{192,64},{1,129},{65,193},{129,1},{193,65... | collective-permute-start | bytes 1572872 | tf_op jit(solution)/shard_map/ppermute | solution.py:70
  1.7 24.9 %collective-permute-start.1 = (bf16[1024,256]{1,0:T(8,128)(2,1)}, bf16[1024,256]{1,0:T(8,128)(2,1)S(1)}, u32[]{:S(2)}, u32[]{:S(2)}) collective-permute-start(bf16[1024,256]{1,0:T(8,128)(2,1)} %param.21), channel_id=1, source_target_pairs={{0,64},{64,0},{128,192},{192,128},{1,65},{65,1},{129,193},{193,129... | collective-permute-start | bytes 1572872 | tf_op jit(solution)/shard_map/ppermute | solution.py:70
  3.3 24.1 %collective-permute-start.2 = (bf16[1024,256]{1,0:T(8,128)(2,1)}, bf16[1024,256]{1,0:T(8,128)(2,1)}, u32[]{:S(2)}, u32[]{:S(2)}) collective-permute-start(bf16[1024,256]{1,0:T(8,128)(2,1)} %param.21), channel_id=1, source_target_pairs={{0,192},{64,128},{128,64},{192,0},{1,193},{65,129},{129,65},{193,1... | collective-permute-start | bytes 1572872 | tf_op jit(solution)/shard_map/ppermute | solution.py:70
  28.8 22.1 %collective-permute-start.10 = (bf16[1024,1024]{1,0:T(8,128)(2,1)S(1)}, bf16[1024,1024]{1,0:T(8,128)(2,1)}, u32[]{:S(2)}, u32[]{:S(2)}) collective-permute-start(bf16[1024,1024]{1,0:T(8,128)(2,1)S(1)} %pad_maximum_fusion), channel_id=1, source_target_pairs={{0,1},{1,0},{2,3},{3,2},{4,5},{5,4},{6,7},{7,6},{8,9},{9,8},{10,11... | collective-permute-start | bytes 6291464 | tf_op jit(solution)/shard_map/ppermute | solution.py:37
  28.9 4.2 %collective-permute-start.5 = (f32[512,128]{1,0:T(8,128)S(1)}, f32[512,128]{1,0:T(8,128)S(1)}, u32[]{:S(2)}, u32[]{:S(2)}) collective-permute-start(f32[512,128]{1,0:T(8,128)S(1)} %copy-done.7), channel_id=1, source_target_pairs={{0,1},{1,0},{2,3},{3,2},{4,5},{5,4},{6,7},{7,6},{8,9},{9,8},{10,11... | collective-permute-start | bytes 786440 | tf_op jit(solution)/shard_map/ppermute | solution.py:37
  35.9 8.7 %collective-permute-start.6 = (bf16[32,1024]{1,0:T(8,128)(2,1)}, bf16[32,1024]{1,0:T(8,128)(2,1)S(1)}, u32[]{:S(2)}, u32[]{:S(2)}) collective-permute-start(bf16[32,1024]{1,0:T(8,128)(2,1)} %combine.1), channel_id=1, source_target_pairs={{0,0},{2,34},{4,36},{6,6},{8,8},{10,42},{12,44},{14,14},{16,16},{1... | collective-permute-start | bytes 196616 | tf_op jit(solution)/shard_map/ppermute | solution.py:25
  37.3 7.2 %collective-permute-start.7 = (bf16[32,1024]{1,0:T(8,128)(2,1)}, bf16[32,1024]{1,0:T(8,128)(2,1)S(1)}, u32[]{:S(2)}, u32[]{:S(2)}) collective-permute-start(bf16[32,1024]{1,0:T(8,128)(2,1)} %combine.1), channel_id=1, source_target_pairs={{0,16},{2,50},{4,52},{6,22},{8,24},{10,58},{12,60},{14,30},{16,0},... | collective-permute-start | bytes 196616 | tf_op jit(solution)/shard_map/ppermute | solution.py:25
  39.3 8.9 %collective-permute-start.8 = (bf16[32,1024]{1,0:T(8,128)(2,1)}, bf16[32,1024]{1,0:T(8,128)(2,1)S(1)}, u32[]{:S(2)}, u32[]{:S(2)}) collective-permute-start(bf16[32,1024]{1,0:T(8,128)(2,1)} %combine.1), channel_id=1, source_target_pairs={{0,32},{2,2},{4,4},{6,38},{8,40},{10,10},{12,12},{14,46},{16,48},{... | collective-permute-start | bytes 196616 | tf_op jit(solution)/shard_map/ppermute | solution.py:25
  44.5 6.4 %collective-permute-start.9 = (bf16[32,1024]{1,0:T(8,128)(2,1)}, bf16[32,1024]{1,0:T(8,128)(2,1)S(1)}, u32[]{:S(2)}, u32[]{:S(2)}) collective-permute-start(bf16[32,1024]{1,0:T(8,128)(2,1)} %combine.1), channel_id=1, source_target_pairs={{0,48},{2,18},{4,20},{6,54},{8,56},{10,26},{12,28},{14,62},{16,32}... | collective-permute-start | bytes 196616 | tf_op jit(solution)/shard_map/ppermute | solution.py:25
  53.5 8.2 %collective-permute-start.11 = (f32[128,512]{1,0:T(8,128)S(1)}, f32[128,512]{1,0:T(8,128)S(1)}, u32[]{:S(2)}, u32[]{:S(2)}) collective-permute-start(f32[128,512]{1,0:T(8,128)S(1)} %slice_select_fusion), channel_id=1, source_target_pairs={{0,6},{2,4},{4,2},{6,0},{1,7},{3,5},{5,3},{7,1},{8,14},{10,12},{12... | collective-permute-start | bytes 786440 | tf_op jit(solution)/shard_map/ppermute | solution.py:29
  56.3 7.3 %collective-permute-start.13 = (f32[64,1024]{1,0:T(8,128)S(1)}, f32[64,1024]{1,0:T(8,128)S(1)}, u32[]{:S(2)}, u32[]{:S(2)}) collective-permute-start(f32[64,1024]{1,0:T(8,128)S(1)} %slice.194), channel_id=1, source_target_pairs={{0,2},{2,0},{4,6},{6,4},{1,3},{3,1},{5,7},{7,5},{8,10},{10,8},{12,... | collective-permute-start | bytes 786440 | tf_op jit(solution)/shard_map/ppermute | solution.py:29
  61.7 5.1 %collective-permute-start.12 = (f32[64,512]{1,0:T(8,128)S(1)}, f32[64,512]{1,0:T(8,128)S(1)}, u32[]{:S(2)}, u32[]{:S(2)}) collective-permute-start(f32[64,512]{1,0:T(8,128)S(1)} %slice.196), channel_id=1, source_target_pairs={{0,2},{2,0},{4,6},{6,4},{1,3},{3,1},{5,7},{7,5},{8,10},{10,8},{12,... | collective-permute-start | bytes 393224 | tf_op jit(solution)/shard_map/ppermute | solution.py:29
  63.6 21.5 %copy-start.3 = (f32[32,1024]{1,0:T(8,128)S(1)}, f32[32,1024]{1,0:T(8,128)}, u32[]{:S(2)}) copy-start(f32[32,1024]{1,0:T(8,128)} %param.20) | copy-start | bytes 393220
  63.7 39.4 %copy-start.6 = (f32[1024]{0:T(1024)S(1)}, f32[1024]{0:T(1024)}, u32[]{:S(2)}) copy-start(f32[1024]{0:T(1024)} %param.22) | copy-start | bytes 12292
  63.7 6.3 %collective-permute-start.14 = (f32[64,512]{1,0:T(8,128)S(1)}, f32[64,512]{1,0:T(8,128)S(1)}, u32[]{:S(2)}, u32[]{:S(2)}) collective-permute-start(f32[64,512]{1,0:T(8,128)S(1)} %slice_select_fusion.1), channel_id=1, source_target_pairs={{0,6},{2,4},{4,2},{6,0},{1,7},{3,5},{5,3},{7,1},{8,14},{10,12},{12... | collective-permute-start | bytes 393224 | tf_op jit(solution)/shard_map/ppermute | solution.py:29
  70.0 7.8 %collective-permute-start.15 = (f32[32,512]{1,0:T(8,128)S(1)}, f32[32,512]{1,0:T(8,128)S(1)}, u32[]{:S(2)}, u32[]{:S(2)}) collective-permute-start(f32[32,512]{1,0:T(8,128)S(1)} %get-tuple-element.54), channel_id=1, source_target_pairs={{0,0},{2,32},{4,36},{6,4},{8,8},{10,40},{12,44},{14,12},{16,16},{1... | collective-permute-start | bytes 196616 | tf_op jit(solution)/shard_map/ppermute | solution.py:25
  70.7 8.3 %collective-permute-start.16 = (f32[32,512]{1,0:T(8,128)S(1)}, f32[32,512]{1,0:T(8,128)S(1)}, u32[]{:S(2)}, u32[]{:S(2)}) collective-permute-start(f32[32,512]{1,0:T(8,128)S(1)} %get-tuple-element.53), channel_id=1, source_target_pairs={{0,8},{2,40},{4,44},{6,12},{8,0},{10,32},{12,36},{14,4},{16,24},{1... | collective-permute-start | bytes 196616 | tf_op jit(solution)/shard_map/ppermute | solution.py:25
  76.0 5.5 %collective-permute-start.17 = (f32[32,512]{1,0:T(8,128)S(1)}, f32[32,512]{1,0:T(8,128)S(1)}, u32[]{:S(2)}, u32[]{:S(2)}) collective-permute-start(f32[32,512]{1,0:T(8,128)S(1)} %get-tuple-element.64), channel_id=1, source_target_pairs={{0,16},{2,48},{4,52},{6,20},{8,24},{10,56},{12,60},{14,28},{16,0},... | collective-permute-start | bytes 196616 | tf_op jit(solution)/shard_map/ppermute | solution.py:25
  77.8 7.3 %collective-permute-start.18 = (f32[32,512]{1,0:T(8,128)S(1)}, f32[32,512]{1,0:T(8,128)S(1)}, u32[]{:S(2)}, u32[]{:S(2)}) collective-permute-start(f32[32,512]{1,0:T(8,128)S(1)} %get-tuple-element.63), channel_id=1, source_target_pairs={{0,24},{2,56},{4,60},{6,28},{8,16},{10,48},{12,52},{14,20},{16,8},... | collective-permute-start | bytes 196616 | tf_op jit(solution)/shard_map/ppermute | solution.py:25
  103.2 7.1 %collective-permute-start.19 = (bf16[32,1024]{1,0:T(8,128)(2,1)S(1)}, bf16[32,1024]{1,0:T(8,128)(2,1)S(1)}, u32[]{:S(2)}, u32[]{:S(2)}) collective-permute-start(bf16[32,1024]{1,0:T(8,128)(2,1)S(1)} %multiply_convert_fusion), channel_id=1, source_target_pairs={{0,0},{2,2},{4,4},{6,6},{8,40},{10,42},{12,44},{14,46},{16,16},{18... | collective-permute-start | bytes 196616 | tf_op jit(solution)/shard_map/ppermute | solution.py:25
  103.9 6.5 %collective-permute-start.20 = (bf16[32,1024]{1,0:T(8,128)(2,1)S(1)}, bf16[32,1024]{1,0:T(8,128)(2,1)S(1)}, u32[]{:S(2)}, u32[]{:S(2)}) collective-permute-start(bf16[32,1024]{1,0:T(8,128)(2,1)S(1)} %multiply_convert_fusion), channel_id=1, source_target_pairs={{0,16},{2,18},{4,20},{6,22},{8,56},{10,58},{12,60},{14,62},{16,0},... | collective-permute-start | bytes 196616 | tf_op jit(solution)/shard_map/ppermute | solution.py:25
  104.1 7.0 %collective-permute-start.21 = (bf16[32,1024]{1,0:T(8,128)(2,1)S(1)}, bf16[32,1024]{1,0:T(8,128)(2,1)S(1)}, u32[]{:S(2)}, u32[]{:S(2)}) collective-permute-start(bf16[32,1024]{1,0:T(8,128)(2,1)S(1)} %multiply_convert_fusion), channel_id=1, source_target_pairs={{0,32},{2,34},{4,36},{6,38},{8,8},{10,10},{12,12},{14,14},{16,48},... | collective-permute-start | bytes 196616 | tf_op jit(solution)/shard_map/ppermute | solution.py:25
  107.5 6.2 %collective-permute-start.22 = (bf16[32,1024]{1,0:T(8,128)(2,1)S(1)}, bf16[32,1024]{1,0:T(8,128)(2,1)S(1)}, u32[]{:S(2)}, u32[]{:S(2)}) collective-permute-start(bf16[32,1024]{1,0:T(8,128)(2,1)S(1)} %multiply_convert_fusion), channel_id=1, source_target_pairs={{0,48},{2,50},{4,52},{6,54},{8,24},{10,26},{12,28},{14,30},{16,32}... | collective-permute-start | bytes 196616 | tf_op jit(solution)/shard_map/ppermute | solution.py:25
  113.6 10.5 %collective-permute-start.23 = (bf16[128,1024]{1,0:T(8,128)(2,1)S(1)}, bf16[128,1024]{1,0:T(8,128)(2,1)S(1)}, u32[]{:S(2)}, u32[]{:S(2)}) collective-permute-start(bf16[128,1024]{1,0:T(8,128)(2,1)S(1)} %constant_dynamic-update-slice_fusion), channel_id=1, source_target_pairs={{0,0},{2,66},{4,132},{6,198},{8,8},{10,74},{12,140},{14,206},{16,1... | collective-permute-start | bytes 786440 | tf_op jit(solution)/shard_map/ppermute | solution.py:25
  114.3 9.9 %collective-permute-start.25 = (bf16[128,1024]{1,0:T(8,128)(2,1)S(1)}, bf16[128,1024]{1,0:T(8,128)(2,1)S(1)}, u32[]{:S(2)}, u32[]{:S(2)}) collective-permute-start(bf16[128,1024]{1,0:T(8,128)(2,1)S(1)} %constant_dynamic-update-slice_fusion), channel_id=1, source_target_pairs={{0,64},{2,2},{4,196},{6,134},{8,72},{10,10},{12,204},{14,142},{16,... | collective-permute-start | bytes 786440 | tf_op jit(solution)/shard_map/ppermute | solution.py:25
  116.9 9.5 %collective-permute-start.24 = (bf16[128,1024]{1,0:T(8,128)(2,1)S(1)}, bf16[128,1024]{1,0:T(8,128)(2,1)S(1)}, u32[]{:S(2)}, u32[]{:S(2)}) collective-permute-start(bf16[128,1024]{1,0:T(8,128)(2,1)S(1)} %constant_dynamic-update-slice_fusion), channel_id=1, source_target_pairs={{0,192},{2,130},{4,68},{6,6},{8,200},{10,138},{12,76},{14,14},{16,... | collective-permute-start | bytes 786440 | tf_op jit(solution)/shard_map/ppermute | solution.py:25
  120.0 9.8 %collective-permute-start.26 = (bf16[128,1024]{1,0:T(8,128)(2,1)S(1)}, bf16[128,1024]{1,0:T(8,128)(2,1)S(1)}, u32[]{:S(2)}, u32[]{:S(2)}) collective-permute-start(bf16[128,1024]{1,0:T(8,128)(2,1)S(1)} %constant_dynamic-update-slice_fusion), channel_id=1, source_target_pairs={{0,128},{2,194},{4,4},{6,70},{8,136},{10,202},{12,12},{14,78},{16,... | collective-permute-start | bytes 786440 | tf_op jit(solution)/shard_map/ppermute | solution.py:25
  136.5 16.2 %collective-permute-start.29 = (bf16[256,1792]{1,0:T(8,128)(2,1)S(1)}, bf16[256,1792]{1,0:T(8,128)(2,1)S(1)}, u32[]{:S(2)}, u32[]{:S(2)}) collective-permute-start(bf16[256,1792]{1,0:T(8,128)(2,1)S(1)} %get-tuple-element.32), channel_id=1, source_target_pairs={{0,6},{2,4},{4,2},{6,0},{1,7},{3,5},{5,3},{7,1},{8,14},{10,12},{12... | collective-permute-start | bytes 2752520 | tf_op jit(solution)/shard_map/ppermute | solution.py:29
  137.3 20.2 %collective-permute-start.27 = (bf16[256,1792]{1,0:T(8,128)(2,1)S(1)}, bf16[256,1792]{1,0:T(8,128)(2,1)S(1)}, u32[]{:S(2)}, u32[]{:S(2)}) collective-permute-start(bf16[256,1792]{1,0:T(8,128)(2,1)S(1)} %get-tuple-element.31), channel_id=1, source_target_pairs={{0,2},{2,0},{4,6},{6,4},{1,3},{3,1},{5,7},{7,5},{8,10},{10,8},{12,... | collective-permute-start | bytes 2752520 | tf_op jit(solution)/shard_map/ppermute | solution.py:29
  157.3 8.6 %collective-permute-start.30 = (bf16[128,1792]{1,0:T(8,128)(2,1)S(1)}, bf16[128,1792]{1,0:T(8,128)(2,1)S(1)}, u32[]{:S(2)}, u32[]{:S(2)}) collective-permute-start(bf16[128,1792]{1,0:T(8,128)(2,1)S(1)} %pad_maximum_fusion.4), channel_id=1, source_target_pairs={{0,2},{2,0},{4,6},{6,4},{1,3},{3,1},{5,7},{7,5},{8,10},{10,8},{12,... | collective-permute-start | bytes 1376264 | tf_op jit(solution)/shard_map/ppermute | solution.py:29
  159.0 9.8 %collective-permute-start.28 = (bf16[128,1792]{1,0:T(8,128)(2,1)S(1)}, bf16[128,1792]{1,0:T(8,128)(2,1)S(1)}, u32[]{:S(2)}, u32[]{:S(2)}) collective-permute-start(bf16[128,1792]{1,0:T(8,128)(2,1)S(1)} %pad_maximum_fusion.3), channel_id=1, source_target_pairs={{0,6},{2,4},{4,2},{6,0},{1,7},{3,5},{5,3},{7,1},{8,14},{10,12},{12... | collective-permute-start | bytes 1376264 | tf_op jit(solution)/shard_map/ppermute | solution.py:29
  160.1 43.1 %collective-permute-start.33 = (bf16[896,1024]{1,0:T(8,128)(2,1)S(1)}, bf16[896,1024]{1,0:T(8,128)(2,1)S(1)}, u32[]{:S(2)}, u32[]{:S(2)}) collective-permute-start(bf16[896,1024]{1,0:T(8,128)(2,1)S(1)} %copy-done), channel_id=1, source_target_pairs={{0,1},{1,0},{2,3},{3,2},{4,5},{5,4},{6,7},{7,6},{8,9},{9,8},{10,11... | collective-permute-start | bytes 5505032 | tf_op jit(solution)/shard_map/ppermute | solution.py:37
  169.0 21.2 %collective-permute-start.31 = (bf16[64,3584]{1,0:T(8,128)(2,1)S(1)}, bf16[64,3584]{1,0:T(8,128)(2,1)S(1)}, u32[]{:S(2)}, u32[]{:S(2)}) collective-permute-start(bf16[64,3584]{1,0:T(8,128)(2,1)S(1)} %pad_maximum_fusion.5), channel_id=1, source_target_pairs={{0,8},{8,0},{1,9},{9,1},{2,10},{10,2},{3,11},{11,3},{4,12},{12,4},... | collective-permute-start | bytes 1376264 | tf_op jit(solution)/shard_map/ppermute | solution.py:33
  190.4 10.2 %collective-permute-start.32 = (bf16[64,1792]{1,0:T(8,128)(2,1)S(1)}, bf16[64,1792]{1,0:T(8,128)(2,1)S(1)}, u32[]{:S(2)}, u32[]{:S(2)}) collective-permute-start(bf16[64,1792]{1,0:T(8,128)(2,1)S(1)} %pad_maximum_fusion.9), channel_id=1, source_target_pairs={{0,8},{8,0},{1,9},{9,1},{2,10},{10,2},{3,11},{11,3},{4,12},{12,4},... | collective-permute-start | bytes 688136 | tf_op jit(solution)/shard_map/ppermute | solution.py:33
  200.7 8.5 %collective-permute-start.36 = (bf16[128,896]{1,0:T(8,128)(2,1)S(1)}, bf16[128,896]{1,0:T(8,128)(2,1)S(1)}, u32[]{:S(2)}, u32[]{:S(2)}) collective-permute-start(bf16[128,896]{1,0:T(8,128)(2,1)S(1)} %pad_maximum_fusion.11), channel_id=1, source_target_pairs={{0,2},{2,0},{4,6},{6,4},{1,3},{3,1},{5,7},{7,5},{8,10},{10,8},{12,... | collective-permute-start | bytes 688136 | tf_op jit(solution)/shard_map/ppermute | solution.py:29
  202.3 10.6 %collective-permute-start.35 = (bf16[128,896]{1,0:T(8,128)(2,1)S(1)}, bf16[128,896]{1,0:T(8,128)(2,1)S(1)}, u32[]{:S(2)}, u32[]{:S(2)}) collective-permute-start(bf16[128,896]{1,0:T(8,128)(2,1)S(1)} %pad_maximum_fusion.10), channel_id=1, source_target_pairs={{0,6},{2,4},{4,2},{6,0},{1,7},{3,5},{5,3},{7,1},{8,14},{10,12},{12... | collective-permute-start | bytes 688136 | tf_op jit(solution)/shard_map/ppermute | solution.py:29
  209.2 9.8 %collective-permute-start.37 = (bf16[256,896]{1,0:T(8,128)(2,1)S(1)}, bf16[256,896]{1,0:T(8,128)(2,1)S(1)}, u32[]{:S(2)}, u32[]{:S(2)}) collective-permute-start(bf16[256,896]{1,0:T(8,128)(2,1)S(1)} %pad_maximum_fusion.6), channel_id=1, source_target_pairs={{0,6},{2,4},{4,2},{6,0},{1,7},{3,5},{5,3},{7,1},{8,14},{10,12},{12... | collective-permute-start | bytes 1376264 | tf_op jit(solution)/shard_map/ppermute | solution.py:29
  212.2 19.5 %collective-permute-start.34 = (bf16[128,1024]{1,0:T(8,128)(2,1)S(1)}, bf16[128,1024]{1,0:T(8,128)(2,1)S(1)}, u32[]{:S(2)}, u32[]{:S(2)}) collective-permute-start(bf16[128,1024]{1,0:T(8,128)(2,1)S(1)} %fusion), channel_id=1, source_target_pairs={{0,0},{2,66},{4,132},{6,198},{8,8},{10,74},{12,140},{14,206},{16,1... | collective-permute-start | bytes 786440 | tf_op jit(solution)/shard_map/ppermute | solution.py:25
  213.0 9.8 %collective-permute-start.39 = (bf16[256,896]{1,0:T(8,128)(2,1)S(1)}, bf16[256,896]{1,0:T(8,128)(2,1)S(1)}, u32[]{:S(2)}, u32[]{:S(2)}) collective-permute-start(bf16[256,896]{1,0:T(8,128)(2,1)S(1)} %pad_maximum_fusion.7), channel_id=1, source_target_pairs={{0,2},{2,0},{4,6},{6,4},{1,3},{3,1},{5,7},{7,5},{8,10},{10,8},{12,... | collective-permute-start | bytes 1376264 | tf_op jit(solution)/shard_map/ppermute | solution.py:29
  219.9 11.8 %collective-permute-start.38 = (bf16[128,1024]{1,0:T(8,128)(2,1)S(1)}, bf16[128,1024]{1,0:T(8,128)(2,1)S(1)}, u32[]{:S(2)}, u32[]{:S(2)}) collective-permute-start(bf16[128,1024]{1,0:T(8,128)(2,1)S(1)} %fusion.1), channel_id=1, source_target_pairs={{0,192},{2,130},{4,68},{6,6},{8,200},{10,138},{12,76},{14,14},{16,... | collective-permute-start | bytes 786440 | tf_op jit(solution)/shard_map/ppermute | solution.py:25
  223.2 8.5 %collective-permute-start.40 = (bf16[128,1024]{1,0:T(8,128)(2,1)S(1)}, bf16[128,1024]{1,0:T(8,128)(2,1)S(1)}, u32[]{:S(2)}, u32[]{:S(2)}) collective-permute-start(bf16[128,1024]{1,0:T(8,128)(2,1)S(1)} %fusion.2), channel_id=1, source_target_pairs={{0,64},{2,2},{4,196},{6,134},{8,72},{10,10},{12,204},{14,142},{16,... | collective-permute-start | bytes 786440 | tf_op jit(solution)/shard_map/ppermute | solution.py:25
  226.7 9.8 %collective-permute-start.41 = (bf16[128,1024]{1,0:T(8,128)(2,1)S(1)}, bf16[128,1024]{1,0:T(8,128)(2,1)S(1)}, u32[]{:S(2)}, u32[]{:S(2)}) collective-permute-start(bf16[128,1024]{1,0:T(8,128)(2,1)S(1)} %fusion.3), channel_id=1, source_target_pairs={{0,128},{2,194},{4,4},{6,70},{8,136},{10,202},{12,12},{14,78},{16,... | collective-permute-start | bytes 786440 | tf_op jit(solution)/shard_map/ppermute | solution.py:25
  236.6 7.3 %collective-permute-start.42 = (bf16[32,1024]{1,0:T(8,128)(2,1)S(1)}, bf16[32,1024]{1,0:T(8,128)(2,1)S(1)}, u32[]{:S(2)}, u32[]{:S(2)}) collective-permute-start(bf16[32,1024]{1,0:T(8,128)(2,1)S(1)} %get-tuple-element.39), channel_id=1, source_target_pairs={{0,0},{2,2},{4,4},{6,6},{8,40},{10,42},{12,44},{14,46},{16,16},{18... | collective-permute-start | bytes 196616 | tf_op jit(solution)/shard_map/ppermute | solution.py:25
  237.3 6.6 %collective-permute-start.43 = (bf16[32,1024]{1,0:T(8,128)(2,1)S(1)}, bf16[32,1024]{1,0:T(8,128)(2,1)S(1)}, u32[]{:S(2)}, u32[]{:S(2)}) collective-permute-start(bf16[32,1024]{1,0:T(8,128)(2,1)S(1)} %get-tuple-element.42), channel_id=1, source_target_pairs={{0,16},{2,18},{4,20},{6,22},{8,56},{10,58},{12,60},{14,62},{16,0},... | collective-permute-start | bytes 196616 | tf_op jit(solution)/shard_map/ppermute | solution.py:25
  239.5 7.2 %collective-permute-start.44 = (bf16[32,1024]{1,0:T(8,128)(2,1)S(1)}, bf16[32,1024]{1,0:T(8,128)(2,1)S(1)}, u32[]{:S(2)}, u32[]{:S(2)}) collective-permute-start(bf16[32,1024]{1,0:T(8,128)(2,1)S(1)} %get-tuple-element.41), channel_id=1, source_target_pairs={{0,32},{2,34},{4,36},{6,38},{8,8},{10,10},{12,12},{14,14},{16,48},... | collective-permute-start | bytes 196616 | tf_op jit(solution)/shard_map/ppermute | solution.py:25
  242.9 6.2 %collective-permute-start.45 = (bf16[32,1024]{1,0:T(8,128)(2,1)S(1)}, bf16[32,1024]{1,0:T(8,128)(2,1)S(1)}, u32[]{:S(2)}, u32[]{:S(2)}) collective-permute-start(bf16[32,1024]{1,0:T(8,128)(2,1)S(1)} %get-tuple-element.40), channel_id=1, source_target_pairs={{0,48},{2,50},{4,52},{6,54},{8,24},{10,26},{12,28},{14,30},{16,32}... | collective-permute-start | bytes 196616 | tf_op jit(solution)/shard_map/ppermute | solution.py:25
  (6 other events, 41.3 us)

commit v2 on v1

--- a/solution.py
+++ b/solution.py
@@ -1,3 +1,5 @@
+import math
+
 import jax
 import jax.numpy as jnp
 from jax import lax
@@ -65,11 +67,8 @@
     )
 
 
-def columns_over_y(weight):
-    blocks = [weight] + [
-        lax.ppermute(weight, "y", [(i, i ^ mask) for i in range(4)]) for mask in (2, 1, 3)
-    ]
-    return jnp.concatenate(blocks, axis=1)
+def over_y(array, mask):
+    return lax.ppermute(array, "y", [(i, i ^ mask) for i in range(4)])
 
 
 def gathered(rows):
@@ -107,14 +106,19 @@
     ]
 
 
+def live_positions(place, lengths, half_len):
+    return jnp.clip(lengths[place[0]] - place[1] * half_len, 0, half_len)
+
+
 def attend_kernel(
-    info, queries, tree_keys, tree_values, parents, keys, values, own, other, rows, top, total, mix
+    place, lengths, queries, tree_keys, tree_values, parents, keys, values, own, other, rows, top, total, mix
 ):
-    step, live, core = pl.program_id(0), info[0], info[1]
+    step, core = pl.program_id(0), place[1]
     nodes, width = queries.shape
     block, head = keys.shape
+    live = live_positions(place, lengths, block * pl.num_programs(0))
     heads = width // head
-    scale = head**-0.5
+    scale = head**-0.5 * math.log2(math.e)
 
     def scored(key_block):
         return scale * lax.dot_general(
@@ -141,7 +145,7 @@
             reach = jnp.concatenate([reach] * heads)
             scores = jnp.where(reach > 0.5, scored(tree_keys[...]), MASKED)
             highest = jnp.max(scores, axis=1, keepdims=True)
-            weights = jnp.exp(scores - highest)
+            weights = jnp.exp2(scores - highest)
             top[...] = jnp.broadcast_to(highest, top.shape)
             total[...] = jnp.broadcast_to(jnp.sum(weights, axis=1, keepdims=True), total.shape)
             mix[...] = mixed(weights, tree_values[...])
@@ -152,18 +156,23 @@
             total[...] = jnp.zeros(total.shape, jnp.float32)
             mix[...] = jnp.zeros(mix.shape, jnp.float32)
 
-    @pl.when(step * block < live)
-    def _():
-        scores = scored(keys[...])
-        positions = step * block + lax.broadcasted_iota(jnp.int32, scores.shape, 1)
-        scores = jnp.where(positions < live, scores, MASKED)
+    def absorb(scores):
         before = top[:, :1]
         highest = jnp.maximum(before, jnp.max(scores, axis=1, keepdims=True))
-        weights = jnp.exp(scores - highest)
-        factor = jnp.exp(before - highest)
+        weights = jnp.exp2(scores - highest)
+        factor = jnp.exp2(before - highest)
         top[...] = jnp.broadcast_to(highest, top.shape)
         total[...] = total[...] * factor + jnp.sum(weights, axis=1, keepdims=True)
         mix[...] = mix[...] * factor + mixed(weights, values[...])
+
+    @pl.when((step + 1) * block <= live)
+    def _():
+        absorb(scored(keys[...]))
+
+    @pl.when((step * block < live) & (live < (step + 1) * block))
+    def _():
+        positions = step * block + lax.broadcasted_iota(jnp.int32, (rows.shape[0], block), 1)
+        absorb(jnp.where(positions < live, scored(keys[...]), MASKED))
 
     @pl.when(step == pl.num_programs(0) - 1)
     def _():
@@ -188,27 +197,30 @@
         top1, total1 = own[numbers, :1], own[numbers, head - 1 :]
         top2, total2 = came[numbers, :1], came[numbers, head - 1 :]
         highest = jnp.maximum(top1, top2)
-        factor1, factor2 = jnp.exp(top1 - highest), jnp.exp(top2 - highest)
+        factor1, factor2 = jnp.exp2(top1 - highest), jnp.exp2(top2 - highest)
         total = total1 * factor1 + total2 * factor2
         value = (own[here, :] * factor1 + came[here, :] * factor2) / total
         out[:, j * head : (j + 1) * head] = value.astype(out.dtype)
 
 
-def attended_parts(queries, tree_keys, tree_values, keys, values, length, parent_row, core):
+def attended_parts(queries, tree_keys, tree_values, keys, values, lengths, parent_row):
     nodes, width = queries.shape
     half_len, head = keys.shape
     rows = width // head * nodes
     block = min(KB, half_len)
-    live = jnp.clip(length - core * half_len, 0, half_len)
-    info = jnp.stack([live, core]).astype(jnp.int32)
-    whole = lambda shape: pl.BlockSpec(shape, lambda i, info: (0, 0))
-    last = lambda i, info: (jnp.minimum(i, jnp.maximum(info[0] - 1, 0) // block), 0)
+    place = jnp.stack([lax.axis_index(REQ), lax.axis_index("core")]).astype(jnp.int32)
+    whole = lambda shape: pl.BlockSpec(shape, lambda i, place, lengths: (0, 0))
+
+    def last(i, place, lengths):
+        live = live_positions(place, lengths, half_len)
+        return jnp.minimum(i, jnp.maximum(live - 1, 0) // block), 0
+
     side = jax.ShapeDtypeStruct((rows, head), jnp.float32)
     return pl.pallas_call(
         attend_kernel,
         out_shape=(side, side),
         grid_spec=pltpu.PrefetchScalarGridSpec(
-            num_scalar_prefetch=1,
+            num_scalar_prefetch=2,
             grid=(half_len // block,),
             in_specs=[
                 whole((nodes, width)),
@@ -233,16 +245,17 @@
             transcendentals=rows * half_len,
         ),
         name="attend",
-    )(info, queries, tree_keys, tree_values, parent_row[:, None], keys, values)
-
-
-def attended(own, other, half):
+    )(place, lengths, queries, tree_keys, tree_values, parent_row[:, None], keys, values)
+
+
+def attended(own, came, half):
     rows, head = own.shape
     return pl.pallas_call(
         combine_kernel,
         out_shape=jax.ShapeDtypeStruct((half, rows // 2 // half * head), jnp.bfloat16),
+        compiler_params=pltpu.CompilerParams(vmem_limit_bytes=8 << 20),
         name="combine",
-    )(own, over_core(other))
+    )(own, came)
 
 
 def local(
@@ -262,7 +275,7 @@
 ):
     core = lax.axis_index("core")
     features = norm_gain.shape[0] * 8
-    out_weight = columns_over_y(out_weight)
+    columns = [over_y(out_weight, mask) for mask in (1, 3, 2)]
     other_gate = over_core(gate_weight)
     other_up = over_core(up_weight)
     length = lax.dynamic_index_in_dim(lengths, lax.axis_index(REQ), keepdims=False)
@@ -272,20 +285,27 @@
         tree_token_values[0],
         cache_keys[0, 0],
         cached_value_rows[0, 0],
-        length,
+        lengths,
         parents[0],
-        core,
-    )
-    parts, out_weight, other_gate, other_up = lax.optimization_barrier(
-        (parts, out_weight, other_gate, other_up)
-    )
-    attention = attended(*parts, queries.shape[1] // 2)
-    other_out = over_core(out_weight)
+    )
+    own, came, near1, near3, other0 = lax.optimization_barrier(
+        (parts[0], over_core(parts[1]), *columns[:2], over_core(out_weight))
+    )
+    attention = attended(own, came, queries.shape[1] // 2)
+    attention, other1, other3 = lax.optimization_barrier(
+        (attention, over_core(near1), over_core(near3))
+    )
     tokens = attention.shape[0]
 
-    rows = jnp.concatenate([sent(attention, near_target(place)) for place in range(4)])
-    rows, out_weight, other_out = lax.optimization_barrier((rows, out_weight, other_out))
-    y, zh, x = [lax.axis_index(name) for name in ("y", "zh", "x")]
+    rows = [sent(attention, near_target(place)) for place in range(4)]
+    *rows, farthest = lax.optimization_barrier((*rows, columns[2]))
+    out_weight = jnp.concatenate([out_weight, farthest, near1, near3], axis=1)
+    other_out = jnp.concatenate([other0, over_core(farthest), other1, other3], axis=1)
+    rows, *weights = lax.optimization_barrier(
+        (jnp.concatenate(rows), gate_weight, up_weight, down_weight)
+    )
+    other_gate, other_up, other_down = [over_core(weight) for weight in weights]
+    core, y, zh, x = [lax.axis_index(name) for name in ("core", "y", "zh", "x")]
     odd = ((y & 1) ^ (x >> 1)) == 1
 
     def classes(products):
@@ -304,6 +324,9 @@
     theirs_came = over_x(theirs_away, 3)
     mine = mine[:half] + mine_came
     theirs = theirs_stay + theirs_came
+    mine, theirs, other_gate, other_up, other_down = lax.optimization_barrier(
+        (mine, theirs, other_gate, other_up, other_down)
+    )
     width = mine.shape[1] // 2
     swap = (zh ^ (y >> 1)) == 1
 
@@ -334,8 +357,6 @@
     normed = (state * lax.rsqrt(squares / features + EPSILON)[:, None] * norm_gain).astype(
         jnp.bfloat16
     )
-
-    other_down = over_core(down_weight)
 
     first, second = summed_over_x(
         gathered(normed), [gate_weight, up_weight], [other_gate, other_up], jnp.bfloat16

time: 252 us -> 241 us (0.956)
  waiting for transfers between devices: 121 us -> 115 us
  Pallas kernels: 10 us -> 6.61 us
    ppermute x3, waiting for transfers between devices: 11 us -> 6.12 us  [over_y(): return lax.ppermute(array, 'y', [(i, i ^ mask) for i in range(4)])]
    ppermute x2, waiting for transfers between devices: 27.4 us -> 32.2 us  [over_zh(): return lax.ppermute(array, 'zh', [(0, 1), (1, 0)])]
    ppermute x2, starting transfers between devices: 4.04 us -> 0.19 us  [over_zh(): return lax.ppermute(array, 'zh', [(0, 1), (1, 0)])]
    ppermute x24, starting transfers between devices: 52.4 us -> 55.7 us  [sent(): return lax.ppermute(array, GRID, pairs)]
    ppermute x24, waiting for transfers between devices: 32 us -> 28.9 us  [sent(): return lax.ppermute(array, GRID, pairs)]
  transfers between devices with their start and end apart: 46 -> 49, of which waited for: 27 -> 28; matrix products, arithmetic and copies ran while one was open for 6% -> 6% of each run, Pallas kernels for 4% -> 3%
where the time goes in v2:
time: 241 us; the launch traced here: 238 us
  waiting for transfers between devices  115 us (48%)
  starting transfers between devices  73.2 us (30%)
  blocking collectives  17.6 us (7%)
  matrix products  17.4 us (7%)
  Pallas kernels  6.61 us (3%)
  local copies, waits for them, and re-layouts  3.57 us (1%)
  other arithmetic  3.49 us (1%)
    ppermute x24, starting transfers between devices, sent(): return lax.ppermute(array, GRID, pairs)  55.7 us
    ppermute x12, waiting for transfers between devices, over_x(): return lax.ppermute(array, 'x', [(i, i ^ mask) for i in range(4)])  45.9 us
    ppermute x2, waiting for transfers between devices, over_zh(): return lax.ppermute(array, 'zh', [(0, 1), (1, 0)])  32.2 us
    ppermute x24, waiting for transfers between devices, sent(): return lax.ppermute(array, GRID, pairs)  28.9 us
    all_to_all x1, blocking collectives, local(): squares = lax.all_to_all(squares, KVH, 0, 0, tiled=True).sum(axis=(0, 1))  17.6 us
    dot_general x18, matrix products, dot(): return jnp.dot(a, b, preferred_element_type=jnp.float32)  17.4 us
    ppermute x12, starting transfers between devices, over_x(): return lax.ppermute(array, 'x', [(i, i ^ mask) for i in range(4)])  13.2 us
    pallas_call x1, Pallas kernels, attended_parts(): pl.pallas_call(attend_kernel, out_shape=(side, side), grid_spec=pltpu.Pre...  6.16 us
  transfers between devices with their start and end apart: 49, of which 28 were waited for; matrix products, arithmetic and copies ran while one was open for 6% of the time, Pallas kernels for 3%

profile of v2, /device:TPU:24, one launch (start us, length us, event | category | flops | bytes accessed | tf_op | source)
XLA Modules:
  0.0 237.9 jit_solution(12007644492489381574)
XLA Ops:
  4.0 6.2 %attend.1 = (f32[512,128]{1,0:T(8,128)}, f32[512,128]{1,0:T(8,128)}) custom-call(s32[2]{0:T(128)} %pad_add_fusion.place, s32[16]{0:T(128)} %lengths.1, bf16[64,1024]{1,0:T(8,128)(2,1)} %bitcast.41, bf16[64,128]{1,0:T(8,128)(2,1)} %bitcast.42, bf16[64,128]{1,0:T(8,128)(2,1)} %bitcast.43, s32[64,1]{1,0:T(8,128)} %copy.16.parents, bf16[4096,128]{1,0:T(8,128)(2,1)} %bitcast.39, ...), custom_call_target="tpu_custom_call" | custom-call | flops 1610612736 | bytes 2097152 | tf_op jit(solution)/shard_map/attend/pallas_call | solution.py:219
  10.1 1.7 collective-permute-done.came
  11.9 2.0 collective-permute-done.1
  13.9 1.7 collective-permute-done.2
  19.0 2.0 collective-permute-start.7
  21.0 6.8 %collective-permute-start.8 = (bf16[32,1024]{1,0:T(8,128)(2,1)S(1)}, bf16[32,1024]{1,0:T(8,128)(2,1)S(1)}, u32[]{:S(2)}, u32[]{:S(2)}) collective-permute-start(bf16[32,1024]{1,0:T(8,128)(2,1)S(1)} %combine.1), channel_id=1, source_target_pairs={{0,32},{2,2},{4,4},{6,38},{8,40},{10,10},{12,12},{14,46},{16,48},{... | collective-permute-start | bytes 196616 | tf_op jit(solution)/shard_map/ppermute | solution.py:27
  29.2 2.5 %collective-permute-done.10 = bf16[1024,256]{1,0:T(8,128)(2,1)} collective-permute-done((bf16[1024,256]{1,0:T(8,128)(2,1)S(1)}, bf16[1024,256]{1,0:T(8,128)(2,1)}, u32[]{:S(2)}, u32[]{:S(2)}) %collective-permute-start.10) | collective-permute-done | bytes 524320 | tf_op jit(solution)/shard_map/ppermute | solution.py:71
  31.7 2.3 collective-permute-done.9
  35.1 1.7 fusion
  38.8 2.2 collective-permute-start.12
  41.1 5.6 %collective-permute-done.14 = f32[64,1024]{1,0:T(8,128)S(1)} collective-permute-done((f32[64,1024]{1,0:T(8,128)S(1)}, f32[64,1024]{1,0:T(8,128)S(1)}, u32[]{:S(2)}, u32[]{:S(2)}) %collective-permute-start.14) | collective-permute-done | bytes 262176 | tf_op jit(solution)/shard_map/ppermute | solution.py:31
  46.8 2.8 %collective-permute-start.15 = (f32[64,512]{1,0:T(8,128)S(1)}, f32[64,512]{1,0:T(8,128)S(1)}, u32[]{:S(2)}, u32[]{:S(2)}) collective-permute-start(f32[64,512]{1,0:T(8,128)S(1)} %slice_select_fusion.1), channel_id=1, source_target_pairs={{0,6},{2,4},{4,2},{6,0},{1,7},{3,5},{5,3},{7,1},{8,14},{10,12},{12... | collective-permute-start | bytes 393224 | tf_op jit(solution)/shard_map/ppermute | solution.py:31
  49.8 3.2 %collective-permute-done.15 = f32[64,512]{1,0:T(8,128)S(1)} collective-permute-done((f32[64,512]{1,0:T(8,128)S(1)}, f32[64,512]{1,0:T(8,128)S(1)}, u32[]{:S(2)}, u32[]{:S(2)}) %collective-permute-start.15) | collective-permute-done | bytes 131104 | tf_op jit(solution)/shard_map/ppermute | solution.py:31
  53.1 1.7 collective-permute-done.13
  55.6 5.5 %collective-permute-start.20 = (f32[32,512]{1,0:T(8,128)S(1)}, f32[32,512]{1,0:T(8,128)S(1)}, u32[]{:S(2)}, u32[]{:S(2)}) collective-permute-start(f32[32,512]{1,0:T(8,128)S(1)} %get-tuple-element.81), channel_id=1, source_target_pairs={{0,8},{2,40},{4,44},{6,12},{8,0},{10,32},{12,36},{14,4},{16,24},{1... | collective-permute-start | bytes 196616 | tf_op jit(solution)/shard_map/ppermute | solution.py:27
  62.2 1.6 collective-permute-done.20
  63.9 1.6 collective-permute-done.21
  65.4 3.8 %collective-permute-done.22 = f32[32,512]{1,0:T(8,128)S(1)} collective-permute-done((f32[32,512]{1,0:T(8,128)S(1)}, f32[32,512]{1,0:T(8,128)S(1)}, u32[]{:S(2)}, u32[]{:S(2)}) %collective-permute-start.22) | collective-permute-done | bytes 65568 | tf_op jit(solution)/shard_map/ppermute | solution.py:27
  69.4 17.6 %all_to_all.5 = f32[8,1,32]{2,1,0:T(1,128)S(1)} all-to-all(f32[8,1,32]{2,1,0:T(1,128)S(1)} %broadcast_in_dim.2), channel_id=1, replica_groups=mesh['y'=4,'zl'=4,'zh'=2,'x'=4,'core'=2] {'zh','x'}, dimensions={0} | all-to-all | bytes 2048 | tf_op jit(solution)/shard_map/all_to_all | solution.py:356
  88.5 4.1 %collective-permute-start.25 = (bf16[32,1024]{1,0:T(8,128)(2,1)S(1)}, bf16[32,1024]{1,0:T(8,128)(2,1)S(1)}, u32[]{:S(2)}, u32[]{:S(2)}) collective-permute-start(bf16[32,1024]{1,0:T(8,128)(2,1)S(1)} %multiply_convert_fusion), channel_id=1, source_target_pairs={{0,32},{2,34},{4,36},{6,38},{8,8},{10,10},{12,12},{14,14},{16,48},... | collective-permute-start | bytes 196616 | tf_op jit(solution)/shard_map/ppermute | solution.py:27
  92.6 1.7 collective-permute-start.26
  95.6 3.2 %collective-permute-done.26 = bf16[32,1024]{1,0:T(8,128)(2,1)S(1)} collective-permute-done((bf16[32,1024]{1,0:T(8,128)(2,1)S(1)}, bf16[32,1024]{1,0:T(8,128)(2,1)S(1)}, u32[]{:S(2)}, u32[]{:S(2)}) %collective-permute-start.26) | collective-permute-done | bytes 65568 | tf_op jit(solution)/shard_map/ppermute | solution.py:27
  99.5 3.1 %collective-permute-start.29 = (bf16[128,1024]{1,0:T(8,128)(2,1)S(1)}, bf16[128,1024]{1,0:T(8,128)(2,1)S(1)}, u32[]{:S(2)}, u32[]{:S(2)}) collective-permute-start(bf16[128,1024]{1,0:T(8,128)(2,1)S(1)} %constant_dynamic-update-slice_fusion), channel_id=1, source_target_pairs={{0,64},{2,2},{4,196},{6,134},{8,72},{10,10},{12,204},{14,142},{16,... | collective-permute-start | bytes 786440 | tf_op jit(solution)/shard_map/ppermute | solution.py:27
  102.6 3.8 %collective-permute-start.28 = (bf16[128,1024]{1,0:T(8,128)(2,1)S(1)}, bf16[128,1024]{1,0:T(8,128)(2,1)S(1)}, u32[]{:S(2)}, u32[]{:S(2)}) collective-permute-start(bf16[128,1024]{1,0:T(8,128)(2,1)S(1)} %constant_dynamic-update-slice_fusion), channel_id=1, source_target_pairs={{0,192},{2,130},{4,68},{6,6},{8,200},{10,138},{12,76},{14,14},{16,... | collective-permute-start | bytes 786440 | tf_op jit(solution)/shard_map/ppermute | solution.py:27
  106.4 3.0 %collective-permute-start.30 = (bf16[128,1024]{1,0:T(8,128)(2,1)S(1)}, bf16[128,1024]{1,0:T(8,128)(2,1)S(1)}, u32[]{:S(2)}, u32[]{:S(2)}) collective-permute-start(bf16[128,1024]{1,0:T(8,128)(2,1)S(1)} %constant_dynamic-update-slice_fusion), channel_id=1, source_target_pairs={{0,128},{2,194},{4,4},{6,70},{8,136},{10,202},{12,12},{14,78},{16,... | collective-permute-start | bytes 786440 | tf_op jit(solution)/shard_map/ppermute | solution.py:27
  110.2 4.1 %collective-permute-done.28 = bf16[128,1024]{1,0:T(8,128)(2,1)S(1)} collective-permute-done((bf16[128,1024]{1,0:T(8,128)(2,1)S(1)}, bf16[128,1024]{1,0:T(8,128)(2,1)S(1)}, u32[]{:S(2)}, u32[]{:S(2)}) %collective-permute-start.28) | collective-permute-done | bytes 262176 | tf_op jit(solution)/shard_map/ppermute | solution.py:27
  114.4 1.8 collective-permute-done.30
  118.4 2.2 convolution_convert_fusion.1
  120.6 2.2 convolution_convert_fusion
  123.1 1.7 collective-permute-start.31
  124.8 16.3 %collective-permute-done.33 = bf16[256,1792]{1,0:T(8,128)(2,1)S(1)} collective-permute-done((bf16[256,1792]{1,0:T(8,128)(2,1)S(1)}, bf16[256,1792]{1,0:T(8,128)(2,1)S(1)}, u32[]{:S(2)}, u32[]{:S(2)}) %collective-permute-start.33) | collective-permute-done | bytes 917536 | tf_op jit(solution)/shard_map/ppermute | solution.py:31
  141.0 2.2 convolution_add_fusion
  143.3 2.2 convolution_add_fusion.1
  149.4 4.8 %collective-permute-done.34 = bf16[128,1792]{1,0:T(8,128)(2,1)S(1)} collective-permute-done((bf16[128,1792]{1,0:T(8,128)(2,1)S(1)}, bf16[128,1792]{1,0:T(8,128)(2,1)S(1)}, u32[]{:S(2)}, u32[]{:S(2)}) %collective-permute-start.34) | collective-permute-done | bytes 458784 | tf_op jit(solution)/shard_map/ppermute | solution.py:31
  154.3 3.9 %collective-permute-done.32 = bf16[128,1792]{1,0:T(8,128)(2,1)S(1)} collective-permute-done((bf16[128,1792]{1,0:T(8,128)(2,1)S(1)}, bf16[128,1792]{1,0:T(8,128)(2,1)S(1)}, u32[]{:S(2)}, u32[]{:S(2)}) %collective-permute-start.32) | collective-permute-done | bytes 458784 | tf_op jit(solution)/shard_map/ppermute | solution.py:31
  158.5 19.9 %collective-permute-done.35 = bf16[64,3584]{1,0:T(8,128)(2,1)S(1)} collective-permute-done((bf16[64,3584]{1,0:T(8,128)(2,1)S(1)}, bf16[64,3584]{1,0:T(8,128)(2,1)S(1)}, u32[]{:S(2)}, u32[]{:S(2)}) %collective-permute-start.35) | collective-permute-done | bytes 458784 | tf_op jit(solution)/shard_map/ppermute | solution.py:35
  178.7 12.2 %collective-permute-done.36 = bf16[64,1792]{1,0:T(8,128)(2,1)S(1)} collective-permute-done((bf16[64,1792]{1,0:T(8,128)(2,1)S(1)}, bf16[64,1792]{1,0:T(8,128)(2,1)S(1)}, u32[]{:S(2)}, u32[]{:S(2)}) %collective-permute-start.36) | collective-permute-done | bytes 229408 | tf_op jit(solution)/shard_map/ppermute | solution.py:35
  191.7 5.4 %collective-permute-done.39 = bf16[128,896]{1,0:T(8,128)(2,1)S(1)} collective-permute-done((bf16[128,896]{1,0:T(8,128)(2,1)S(1)}, bf16[128,896]{1,0:T(8,128)(2,1)S(1)}, u32[]{:S(2)}, u32[]{:S(2)}) %collective-permute-start.39) | collective-permute-done | bytes 229408 | tf_op jit(solution)/shard_map/ppermute | solution.py:31
  197.2 2.5 %collective-permute-start.40 = (bf16[256,896]{1,0:T(8,128)(2,1)S(1)}, bf16[256,896]{1,0:T(8,128)(2,1)S(1)}, u32[]{:S(2)}, u32[]{:S(2)}) collective-permute-start(bf16[256,896]{1,0:T(8,128)(2,1)S(1)} %pad_maximum_fusion.5), channel_id=1, source_target_pairs={{0,6},{2,4},{4,2},{6,0},{1,7},{3,5},{5,3},{7,1},{8,14},{10,12},{12... | collective-permute-start | bytes 1376264 | tf_op jit(solution)/shard_map/ppermute | solution.py:31
  201.9 5.1 %collective-permute-done.40 = bf16[256,896]{1,0:T(8,128)(2,1)S(1)} collective-permute-done((bf16[256,896]{1,0:T(8,128)(2,1)S(1)}, bf16[256,896]{1,0:T(8,128)(2,1)S(1)}, u32[]{:S(2)}, u32[]{:S(2)}) %collective-permute-start.40) | collective-permute-done | bytes 458784 | tf_op jit(solution)/shard_map/ppermute | solution.py:31
  207.9 3.3 %collective-permute-start.41 = (bf16[128,1024]{1,0:T(8,128)(2,1)S(1)}, bf16[128,1024]{1,0:T(8,128)(2,1)S(1)}, u32[]{:S(2)}, u32[]{:S(2)}) collective-permute-start(bf16[128,1024]{1,0:T(8,128)(2,1)S(1)} %fusion.17), channel_id=1, source_target_pairs={{0,192},{2,130},{4,68},{6,6},{8,200},{10,138},{12,76},{14,14},{16,... | collective-permute-start | bytes 786440 | tf_op jit(solution)/shard_map/ppermute | solution.py:27
  211.6 1.9 collective-permute-start.43
  214.4 5.2 %collective-permute-start.44 = (bf16[128,1024]{1,0:T(8,128)(2,1)S(1)}, bf16[128,1024]{1,0:T(8,128)(2,1)S(1)}, u32[]{:S(2)}, u32[]{:S(2)}) collective-permute-start(bf16[128,1024]{1,0:T(8,128)(2,1)S(1)} %fusion.19), channel_id=1, source_target_pairs={{0,128},{2,194},{4,4},{6,70},{8,136},{10,202},{12,12},{14,78},{16,... | collective-permute-start | bytes 786440 | tf_op jit(solution)/shard_map/ppermute | solution.py:27
  219.9 4.3 %collective-permute-done.44 = bf16[128,1024]{1,0:T(8,128)(2,1)S(1)} collective-permute-done((bf16[128,1024]{1,0:T(8,128)(2,1)S(1)}, bf16[128,1024]{1,0:T(8,128)(2,1)S(1)}, u32[]{:S(2)}, u32[]{:S(2)}) %collective-permute-start.44) | collective-permute-done | bytes 262176 | tf_op jit(solution)/shard_map/ppermute | solution.py:27
  225.1 3.6 %collective-permute-start.46 = (bf16[32,1024]{1,0:T(8,128)(2,1)S(1)}, bf16[32,1024]{1,0:T(8,128)(2,1)S(1)}, u32[]{:S(2)}, u32[]{:S(2)}) collective-permute-start(bf16[32,1024]{1,0:T(8,128)(2,1)S(1)} %get-tuple-element.70), channel_id=1, source_target_pairs={{0,16},{2,18},{4,20},{6,22},{8,56},{10,58},{12,60},{14,62},{16,0},... | collective-permute-start | bytes 196616 | tf_op jit(solution)/shard_map/ppermute | solution.py:27
  228.7 2.3 collective-permute-start.47
  231.0 2.1 collective-permute-start.48
  233.1 2.8 %collective-permute-done.47 = bf16[32,1024]{1,0:T(8,128)(2,1)S(1)} collective-permute-done((bf16[32,1024]{1,0:T(8,128)(2,1)S(1)}, bf16[32,1024]{1,0:T(8,128)(2,1)S(1)}, u32[]{:S(2)}, u32[]{:S(2)}) %collective-permute-start.47) | collective-permute-done | bytes 65568 | tf_op jit(solution)/shard_map/ppermute | solution.py:27
  (157 shorter events, 33.6 us)
Async XLA Ops:
  0.0 13.9 %collective-permute-start.1 = (bf16[1024,256]{1,0:T(8,128)(2,1)}, bf16[1024,256]{1,0:T(8,128)(2,1)S(1)}, u32[]{:S(2)}, u32[]{:S(2)}) collective-permute-start(bf16[1024,256]{1,0:T(8,128)(2,1)} %param.21), channel_id=1, source_target_pairs={{0,64},{64,0},{128,192},{192,128},{1,65},{65,1},{129,193},{193,129... | collective-permute-start | bytes 1572872 | tf_op jit(solution)/shard_map/ppermute | solution.py:71
  0.7 14.8 %collective-permute-start.2 = (bf16[1024,256]{1,0:T(8,128)(2,1)}, bf16[1024,256]{1,0:T(8,128)(2,1)S(1)}, u32[]{:S(2)}, u32[]{:S(2)}) collective-permute-start(bf16[1024,256]{1,0:T(8,128)(2,1)} %param.21), channel_id=1, source_target_pairs={{0,192},{64,128},{128,64},{192,0},{1,193},{65,129},{129,65},{193,1... | collective-permute-start | bytes 1572872 | tf_op jit(solution)/shard_map/ppermute | solution.py:71
  2.0 13.6 %collective-permute-start.3 = (bf16[1024,256]{1,0:T(8,128)(2,1)}, bf16[1024,256]{1,0:T(8,128)(2,1)S(1)}, u32[]{:S(2)}, u32[]{:S(2)}) collective-permute-start(bf16[1024,256]{1,0:T(8,128)(2,1)} %param.21), channel_id=1, source_target_pairs={{0,1},{1,0},{2,3},{3,2},{4,5},{5,4},{6,7},{7,6},{8,9},{9,8},{10,11... | collective-permute-start | bytes 1572872 | tf_op jit(solution)/shard_map/ppermute | solution.py:39
  15.6 2.4 %collective-permute-start.4 = (bf16[1024,256]{1,0:T(8,128)(2,1)S(1)}, bf16[1024,256]{1,0:T(8,128)(2,1)S(1)}, u32[]{:S(2)}, u32[]{:S(2)}) collective-permute-start(bf16[1024,256]{1,0:T(8,128)(2,1)S(1)} %collective-permute-done.1), channel_id=1, source_target_pairs={{0,1},{1,0},{2,3},{3,2},{4,5},{5,4},{6,7},{7,6},{8,9},{9,8},{10,11... | collective-permute-start | bytes 1572872 | tf_op jit(solution)/shard_map/ppermute | solution.py:39
  15.7 2.6 %collective-permute-start.5 = (bf16[1024,256]{1,0:T(8,128)(2,1)S(1)}, bf16[1024,256]{1,0:T(8,128)(2,1)S(1)}, u32[]{:S(2)}, u32[]{:S(2)}) collective-permute-start(bf16[1024,256]{1,0:T(8,128)(2,1)S(1)} %collective-permute-done.2), channel_id=1, source_target_pairs={{0,1},{1,0},{2,3},{3,2},{4,5},{5,4},{6,7},{7,6},{8,9},{9,8},{10,11... | collective-permute-start | bytes 1572872 | tf_op jit(solution)/shard_map/ppermute | solution.py:39
  16.2 15.5 %collective-permute-start.10 = (bf16[1024,256]{1,0:T(8,128)(2,1)S(1)}, bf16[1024,256]{1,0:T(8,128)(2,1)}, u32[]{:S(2)}, u32[]{:S(2)}) collective-permute-start(bf16[1024,256]{1,0:T(8,128)(2,1)S(1)} %copy-done.6), channel_id=1, source_target_pairs={{0,128},{64,192},{128,0},{192,64},{1,129},{65,193},{129,1},{193,65... | collective-permute-start | bytes 1572872 | tf_op jit(solution)/shard_map/ppermute | solution.py:71
  18.3 13.4 %collective-permute-start.6 = (bf16[32,1024]{1,0:T(8,128)(2,1)S(1)}, bf16[32,1024]{1,0:T(8,128)(2,1)S(1)}, u32[]{:S(2)}, u32[]{:S(2)}) collective-permute-start(bf16[32,1024]{1,0:T(8,128)(2,1)S(1)} %combine.1), channel_id=1, source_target_pairs={{0,0},{2,34},{4,36},{6,6},{8,8},{10,42},{12,44},{14,14},{16,16},{1... | collective-permute-start | bytes 196616 | tf_op jit(solution)/shard_map/ppermute | solution.py:27
  19.0 12.7 %collective-permute-start.7 = (bf16[32,1024]{1,0:T(8,128)(2,1)S(1)}, bf16[32,1024]{1,0:T(8,128)(2,1)S(1)}, u32[]{:S(2)}, u32[]{:S(2)}) collective-permute-start(bf16[32,1024]{1,0:T(8,128)(2,1)S(1)} %combine.1), channel_id=1, source_target_pairs={{0,16},{2,50},{4,52},{6,22},{8,24},{10,58},{12,60},{14,30},{16,0},... | collective-permute-start | bytes 196616 | tf_op jit(solution)/shard_map/ppermute | solution.py:27
  21.0 10.7 %collective-permute-start.8 = (bf16[32,1024]{1,0:T(8,128)(2,1)S(1)}, bf16[32,1024]{1,0:T(8,128)(2,1)S(1)}, u32[]{:S(2)}, u32[]{:S(2)}) collective-permute-start(bf16[32,1024]{1,0:T(8,128)(2,1)S(1)} %combine.1), channel_id=1, source_target_pairs={{0,32},{2,2},{4,4},{6,38},{8,40},{10,10},{12,12},{14,46},{16,48},{... | collective-permute-start | bytes 196616 | tf_op jit(solution)/shard_map/ppermute | solution.py:27
  27.7 6.3 %collective-permute-start.9 = (bf16[32,1024]{1,0:T(8,128)(2,1)S(1)}, bf16[32,1024]{1,0:T(8,128)(2,1)S(1)}, u32[]{:S(2)}, u32[]{:S(2)}) collective-permute-start(bf16[32,1024]{1,0:T(8,128)(2,1)S(1)} %combine.1), channel_id=1, source_target_pairs={{0,48},{2,18},{4,20},{6,54},{8,56},{10,26},{12,28},{14,62},{16,32}... | collective-permute-start | bytes 196616 | tf_op jit(solution)/shard_map/ppermute | solution.py:27
  34.0 3.6 %collective-permute-start.11 = (bf16[1024,256]{1,0:T(8,128)(2,1)}, bf16[1024,256]{1,0:T(8,128)(2,1)S(1)}, u32[]{:S(2)}, u32[]{:S(2)}) collective-permute-start(bf16[1024,256]{1,0:T(8,128)(2,1)} %collective-permute-done.10), channel_id=1, source_target_pairs={{0,1},{1,0},{2,3},{3,2},{4,5},{5,4},{6,7},{7,6},{8,9},{9,8},{10,11... | collective-permute-start | bytes 1572872 | tf_op jit(solution)/shard_map/ppermute | solution.py:39
  34.0 20.8 %collective-permute-start.16 = (bf16[1024,896]{1,0:T(8,128)(2,1)}, bf16[1024,896]{1,0:T(8,128)(2,1)}, u32[]{:S(2)}, u32[]{:S(2)}) collective-permute-start(bf16[1024,896]{1,0:T(8,128)(2,1)} %param.23), channel_id=1, source_target_pairs={{0,1},{1,0},{2,3},{3,2},{4,5},{5,4},{6,7},{7,6},{8,9},{9,8},{10,11... | collective-permute-start | bytes 5505032 | tf_op jit(solution)/shard_map/ppermute | solution.py:39
  34.6 20.2 %collective-permute-start.17 = (bf16[1024,896]{1,0:T(8,128)(2,1)}, bf16[1024,896]{1,0:T(8,128)(2,1)}, u32[]{:S(2)}, u32[]{:S(2)}) collective-permute-start(bf16[1024,896]{1,0:T(8,128)(2,1)} %param.24), channel_id=1, source_target_pairs={{0,1},{1,0},{2,3},{3,2},{4,5},{5,4},{6,7},{7,6},{8,9},{9,8},{10,11... | collective-permute-start | bytes 5505032 | tf_op jit(solution)/shard_map/ppermute | solution.py:39
  34.7 20.1 %collective-permute-start.18 = (bf16[896,1024]{1,0:T(8,128)(2,1)}, bf16[896,1024]{1,0:T(8,128)(2,1)S(1)}, u32[]{:S(2)}, u32[]{:S(2)}) collective-permute-start(bf16[896,1024]{1,0:T(8,128)(2,1)} %param.25), channel_id=1, source_target_pairs={{0,1},{1,0},{2,3},{3,2},{4,5},{5,4},{6,7},{7,6},{8,9},{9,8},{10,11... | collective-permute-start | bytes 5505032 | tf_op jit(solution)/shard_map/ppermute | solution.py:39
  38.1 8.6 %collective-permute-start.14 = (f32[64,1024]{1,0:T(8,128)S(1)}, f32[64,1024]{1,0:T(8,128)S(1)}, u32[]{:S(2)}, u32[]{:S(2)}) collective-permute-start(f32[64,1024]{1,0:T(8,128)S(1)} %slice.194), channel_id=1, source_target_pairs={{0,2},{2,0},{4,6},{6,4},{1,3},{3,1},{5,7},{7,5},{8,10},{10,8},{12,... | collective-permute-start | bytes 786440 | tf_op jit(solution)/shard_map/ppermute | solution.py:31
  38.8 10.8 %collective-permute-start.12 = (f32[128,512]{1,0:T(8,128)}, f32[128,512]{1,0:T(8,128)S(1)}, u32[]{:S(2)}, u32[]{:S(2)}) collective-permute-start(f32[128,512]{1,0:T(8,128)} %slice_select_fusion), channel_id=1, source_target_pairs={{0,6},{2,4},{4,2},{6,0},{1,7},{3,5},{5,3},{7,1},{8,14},{10,12},{12... | collective-permute-start | bytes 786440 | tf_op jit(solution)/shard_map/ppermute | solution.py:31
  46.8 6.3 %collective-permute-start.15 = (f32[64,512]{1,0:T(8,128)S(1)}, f32[64,512]{1,0:T(8,128)S(1)}, u32[]{:S(2)}, u32[]{:S(2)}) collective-permute-start(f32[64,512]{1,0:T(8,128)S(1)} %slice_select_fusion.1), channel_id=1, source_target_pairs={{0,6},{2,4},{4,2},{6,0},{1,7},{3,5},{5,3},{7,1},{8,14},{10,12},{12... | collective-permute-start | bytes 393224 | tf_op jit(solution)/shard_map/ppermute | solution.py:31
  49.7 5.1 %collective-permute-start.13 = (f32[64,512]{1,0:T(8,128)S(1)}, f32[64,512]{1,0:T(8,128)S(1)}, u32[]{:S(2)}, u32[]{:S(2)}) collective-permute-start(f32[64,512]{1,0:T(8,128)S(1)} %slice.196), channel_id=1, source_target_pairs={{0,2},{2,0},{4,6},{6,4},{1,3},{3,1},{5,7},{7,5},{8,10},{10,8},{12,... | collective-permute-start | bytes 393224 | tf_op jit(solution)/shard_map/ppermute | solution.py:31
  54.9 7.3 %collective-permute-start.19 = (f32[32,512]{1,0:T(8,128)S(1)}, f32[32,512]{1,0:T(8,128)S(1)}, u32[]{:S(2)}, u32[]{:S(2)}) collective-permute-start(f32[32,512]{1,0:T(8,128)S(1)} %get-tuple-element.82), channel_id=1, source_target_pairs={{0,0},{2,32},{4,36},{6,4},{8,8},{10,40},{12,44},{14,12},{16,16},{1... | collective-permute-start | bytes 196616 | tf_op jit(solution)/shard_map/ppermute | solution.py:27
  55.6 8.3 %collective-permute-start.20 = (f32[32,512]{1,0:T(8,128)S(1)}, f32[32,512]{1,0:T(8,128)S(1)}, u32[]{:S(2)}, u32[]{:S(2)}) collective-permute-start(f32[32,512]{1,0:T(8,128)S(1)} %get-tuple-element.81), channel_id=1, source_target_pairs={{0,8},{2,40},{4,44},{6,12},{8,0},{10,32},{12,36},{14,4},{16,24},{1... | collective-permute-start | bytes 196616 | tf_op jit(solution)/shard_map/ppermute | solution.py:27
  61.0 4.4 %collective-permute-start.21 = (f32[32,512]{1,0:T(8,128)S(1)}, f32[32,512]{1,0:T(8,128)S(1)}, u32[]{:S(2)}, u32[]{:S(2)}) collective-permute-start(f32[32,512]{1,0:T(8,128)S(1)} %get-tuple-element.92), channel_id=1, source_target_pairs={{0,16},{2,48},{4,52},{6,20},{8,24},{10,56},{12,60},{14,28},{16,0},... | collective-permute-start | bytes 196616 | tf_op jit(solution)/shard_map/ppermute | solution.py:27
  61.9 7.4 %collective-permute-start.22 = (f32[32,512]{1,0:T(8,128)S(1)}, f32[32,512]{1,0:T(8,128)S(1)}, u32[]{:S(2)}, u32[]{:S(2)}) collective-permute-start(f32[32,512]{1,0:T(8,128)S(1)} %get-tuple-element.91), channel_id=1, source_target_pairs={{0,24},{2,56},{4,60},{6,28},{8,16},{10,48},{12,52},{14,20},{16,8},... | collective-permute-start | bytes 196616 | tf_op jit(solution)/shard_map/ppermute | solution.py:27
  87.2 7.1 %collective-permute-start.23 = (bf16[32,1024]{1,0:T(8,128)(2,1)S(1)}, bf16[32,1024]{1,0:T(8,128)(2,1)S(1)}, u32[]{:S(2)}, u32[]{:S(2)}) collective-permute-start(bf16[32,1024]{1,0:T(8,128)(2,1)S(1)} %multiply_convert_fusion), channel_id=1, source_target_pairs={{0,0},{2,2},{4,4},{6,6},{8,40},{10,42},{12,44},{14,46},{16,16},{18... | collective-permute-start | bytes 196616 | tf_op jit(solution)/shard_map/ppermute | solution.py:27
  87.8 6.5 %collective-permute-start.24 = (bf16[32,1024]{1,0:T(8,128)(2,1)S(1)}, bf16[32,1024]{1,0:T(8,128)(2,1)S(1)}, u32[]{:S(2)}, u32[]{:S(2)}) collective-permute-start(bf16[32,1024]{1,0:T(8,128)(2,1)S(1)} %multiply_convert_fusion), channel_id=1, source_target_pairs={{0,16},{2,18},{4,20},{6,22},{8,56},{10,58},{12,60},{14,62},{16,0},... | collective-permute-start | bytes 196616 | tf_op jit(solution)/shard_map/ppermute | solution.py:27
  88.5 7.0 %collective-permute-start.25 = (bf16[32,1024]{1,0:T(8,128)(2,1)S(1)}, bf16[32,1024]{1,0:T(8,128)(2,1)S(1)}, u32[]{:S(2)}, u32[]{:S(2)}) collective-permute-start(bf16[32,1024]{1,0:T(8,128)(2,1)S(1)} %multiply_convert_fusion), channel_id=1, source_target_pairs={{0,32},{2,34},{4,36},{6,38},{8,8},{10,10},{12,12},{14,14},{16,48},... | collective-permute-start | bytes 196616 | tf_op jit(solution)/shard_map/ppermute | solution.py:27
  92.6 6.2 %collective-permute-start.26 = (bf16[32,1024]{1,0:T(8,128)(2,1)S(1)}, bf16[32,1024]{1,0:T(8,128)(2,1)S(1)}, u32[]{:S(2)}, u32[]{:S(2)}) collective-permute-start(bf16[32,1024]{1,0:T(8,128)(2,1)S(1)} %multiply_convert_fusion), channel_id=1, source_target_pairs={{0,48},{2,50},{4,52},{6,54},{8,24},{10,26},{12,28},{14,30},{16,32}... | collective-permute-start | bytes 196616 | tf_op jit(solution)/shard_map/ppermute | solution.py:27
  98.8 10.7 %collective-permute-start.27 = (bf16[128,1024]{1,0:T(8,128)(2,1)S(1)}, bf16[128,1024]{1,0:T(8,128)(2,1)S(1)}, u32[]{:S(2)}, u32[]{:S(2)}) collective-permute-start(bf16[128,1024]{1,0:T(8,128)(2,1)S(1)} %constant_dynamic-update-slice_fusion), channel_id=1, source_target_pairs={{0,0},{2,66},{4,132},{6,198},{8,8},{10,74},{12,140},{14,206},{16,1... | collective-permute-start | bytes 786440 | tf_op jit(solution)/shard_map/ppermute | solution.py:27
  99.5 10.7 %collective-permute-start.29 = (bf16[128,1024]{1,0:T(8,128)(2,1)S(1)}, bf16[128,1024]{1,0:T(8,128)(2,1)S(1)}, u32[]{:S(2)}, u32[]{:S(2)}) collective-permute-start(bf16[128,1024]{1,0:T(8,128)(2,1)S(1)} %constant_dynamic-update-slice_fusion), channel_id=1, source_target_pairs={{0,64},{2,2},{4,196},{6,134},{8,72},{10,10},{12,204},{14,142},{16,... | collective-permute-start | bytes 786440 | tf_op jit(solution)/shard_map/ppermute | solution.py:27
  102.6 11.7 %collective-permute-start.28 = (bf16[128,1024]{1,0:T(8,128)(2,1)S(1)}, bf16[128,1024]{1,0:T(8,128)(2,1)S(1)}, u32[]{:S(2)}, u32[]{:S(2)}) collective-permute-start(bf16[128,1024]{1,0:T(8,128)(2,1)S(1)} %constant_dynamic-update-slice_fusion), channel_id=1, source_target_pairs={{0,192},{2,130},{4,68},{6,6},{8,200},{10,138},{12,76},{14,14},{16,... | collective-permute-start | bytes 786440 | tf_op jit(solution)/shard_map/ppermute | solution.py:27
  106.4 9.8 %collective-permute-start.30 = (bf16[128,1024]{1,0:T(8,128)(2,1)S(1)}, bf16[128,1024]{1,0:T(8,128)(2,1)S(1)}, u32[]{:S(2)}, u32[]{:S(2)}) collective-permute-start(bf16[128,1024]{1,0:T(8,128)(2,1)S(1)} %constant_dynamic-update-slice_fusion), channel_id=1, source_target_pairs={{0,128},{2,194},{4,4},{6,70},{8,136},{10,202},{12,12},{14,78},{16,... | collective-permute-start | bytes 786440 | tf_op jit(solution)/shard_map/ppermute | solution.py:27
  123.0 18.1 %collective-permute-start.33 = (bf16[256,1792]{1,0:T(8,128)(2,1)S(1)}, bf16[256,1792]{1,0:T(8,128)(2,1)S(1)}, u32[]{:S(2)}, u32[]{:S(2)}) collective-permute-start(bf16[256,1792]{1,0:T(8,128)(2,1)S(1)} %pad_maximum_fusion.1), channel_id=1, source_target_pairs={{0,6},{2,4},{4,2},{6,0},{1,7},{3,5},{5,3},{7,1},{8,14},{10,12},{12... | collective-permute-start | bytes 2752520 | tf_op jit(solution)/shard_map/ppermute | solution.py:31
  123.1 23.8 %collective-permute-start.31 = (bf16[256,1792]{1,0:T(8,128)(2,1)S(1)}, bf16[256,1792]{1,0:T(8,128)(2,1)S(1)}, u32[]{:S(2)}, u32[]{:S(2)}) collective-permute-start(bf16[256,1792]{1,0:T(8,128)(2,1)S(1)} %pad_maximum_fusion), channel_id=1, source_target_pairs={{0,2},{2,0},{4,6},{6,4},{1,3},{3,1},{5,7},{7,5},{8,10},{10,8},{12,... | collective-permute-start | bytes 2752520 | tf_op jit(solution)/shard_map/ppermute | solution.py:31
  145.6 8.6 %collective-permute-start.34 = (bf16[128,1792]{1,0:T(8,128)(2,1)S(1)}, bf16[128,1792]{1,0:T(8,128)(2,1)S(1)}, u32[]{:S(2)}, u32[]{:S(2)}) collective-permute-start(bf16[128,1792]{1,0:T(8,128)(2,1)S(1)} %pad_maximum_fusion.3), channel_id=1, source_target_pairs={{0,2},{2,0},{4,6},{6,4},{1,3},{3,1},{5,7},{7,5},{8,10},{10,8},{12,... | collective-permute-start | bytes 1376264 | tf_op jit(solution)/shard_map/ppermute | solution.py:31
  148.5 9.8 %collective-permute-start.32 = (bf16[128,1792]{1,0:T(8,128)(2,1)S(1)}, bf16[128,1792]{1,0:T(8,128)(2,1)S(1)}, u32[]{:S(2)}, u32[]{:S(2)}) collective-permute-start(bf16[128,1792]{1,0:T(8,128)(2,1)S(1)} %pad_maximum_fusion.2), channel_id=1, source_target_pairs={{0,6},{2,4},{4,2},{6,0},{1,7},{3,5},{5,3},{7,1},{8,14},{10,12},{12... | collective-permute-start | bytes 1376264 | tf_op jit(solution)/shard_map/ppermute | solution.py:31
  158.4 20.0 %collective-permute-start.35 = (bf16[64,3584]{1,0:T(8,128)(2,1)S(1)}, bf16[64,3584]{1,0:T(8,128)(2,1)S(1)}, u32[]{:S(2)}, u32[]{:S(2)}) collective-permute-start(bf16[64,3584]{1,0:T(8,128)(2,1)S(1)} %pad_maximum_fusion.4), channel_id=1, source_target_pairs={{0,8},{8,0},{1,9},{9,1},{2,10},{10,2},{3,11},{11,3},{4,12},{12,4},... | collective-permute-start | bytes 1376264 | tf_op jit(solution)/shard_map/ppermute | solution.py:35
  178.6 12.3 %collective-permute-start.36 = (bf16[64,1792]{1,0:T(8,128)(2,1)S(1)}, bf16[64,1792]{1,0:T(8,128)(2,1)S(1)}, u32[]{:S(2)}, u32[]{:S(2)}) collective-permute-start(bf16[64,1792]{1,0:T(8,128)(2,1)S(1)} %pad_maximum_fusion.8), channel_id=1, source_target_pairs={{0,8},{8,0},{1,9},{9,1},{2,10},{10,2},{3,11},{11,3},{4,12},{12,4},... | collective-permute-start | bytes 688136 | tf_op jit(solution)/shard_map/ppermute | solution.py:35
  191.0 6.1 %collective-permute-start.39 = (bf16[128,896]{1,0:T(8,128)(2,1)S(1)}, bf16[128,896]{1,0:T(8,128)(2,1)S(1)}, u32[]{:S(2)}, u32[]{:S(2)}) collective-permute-start(bf16[128,896]{1,0:T(8,128)(2,1)S(1)} %pad_maximum_fusion.10), channel_id=1, source_target_pairs={{0,2},{2,0},{4,6},{6,4},{1,3},{3,1},{5,7},{7,5},{8,10},{10,8},{12,... | collective-permute-start | bytes 688136 | tf_op jit(solution)/shard_map/ppermute | solution.py:31
  191.2 9.6 %collective-permute-start.38 = (bf16[128,896]{1,0:T(8,128)(2,1)S(1)}, bf16[128,896]{1,0:T(8,128)(2,1)S(1)}, u32[]{:S(2)}, u32[]{:S(2)}) collective-permute-start(bf16[128,896]{1,0:T(8,128)(2,1)S(1)} %pad_maximum_fusion.9), channel_id=1, source_target_pairs={{0,6},{2,4},{4,2},{6,0},{1,7},{3,5},{5,3},{7,1},{8,14},{10,12},{12... | collective-permute-start | bytes 688136 | tf_op jit(solution)/shard_map/ppermute | solution.py:31
  197.2 9.8 %collective-permute-start.40 = (bf16[256,896]{1,0:T(8,128)(2,1)S(1)}, bf16[256,896]{1,0:T(8,128)(2,1)S(1)}, u32[]{:S(2)}, u32[]{:S(2)}) collective-permute-start(bf16[256,896]{1,0:T(8,128)(2,1)S(1)} %pad_maximum_fusion.5), channel_id=1, source_target_pairs={{0,6},{2,4},{4,2},{6,0},{1,7},{3,5},{5,3},{7,1},{8,14},{10,12},{12... | collective-permute-start | bytes 1376264 | tf_op jit(solution)/shard_map/ppermute | solution.py:31
  200.1 19.6 %collective-permute-start.37 = (bf16[128,1024]{1,0:T(8,128)(2,1)S(1)}, bf16[128,1024]{1,0:T(8,128)(2,1)S(1)}, u32[]{:S(2)}, u32[]{:S(2)}) collective-permute-start(bf16[128,1024]{1,0:T(8,128)(2,1)S(1)} %fusion.16), channel_id=1, source_target_pairs={{0,0},{2,66},{4,132},{6,198},{8,8},{10,74},{12,140},{14,206},{16,1... | collective-permute-start | bytes 786440 | tf_op jit(solution)/shard_map/ppermute | solution.py:27
  200.8 10.3 %collective-permute-start.42 = (bf16[256,896]{1,0:T(8,128)(2,1)S(1)}, bf16[256,896]{1,0:T(8,128)(2,1)S(1)}, u32[]{:S(2)}, u32[]{:S(2)}) collective-permute-start(bf16[256,896]{1,0:T(8,128)(2,1)S(1)} %pad_maximum_fusion.6), channel_id=1, source_target_pairs={{0,2},{2,0},{4,6},{6,4},{1,3},{3,1},{5,7},{7,5},{8,10},{10,8},{12,... | collective-permute-start | bytes 1376264 | tf_op jit(solution)/shard_map/ppermute | solution.py:31
  207.9 11.8 %collective-permute-start.41 = (bf16[128,1024]{1,0:T(8,128)(2,1)S(1)}, bf16[128,1024]{1,0:T(8,128)(2,1)S(1)}, u32[]{:S(2)}, u32[]{:S(2)}) collective-permute-start(bf16[128,1024]{1,0:T(8,128)(2,1)S(1)} %fusion.17), channel_id=1, source_target_pairs={{0,192},{2,130},{4,68},{6,6},{8,200},{10,138},{12,76},{14,14},{16,... | collective-permute-start | bytes 786440 | tf_op jit(solution)/shard_map/ppermute | solution.py:27
  211.6 8.3 %collective-permute-start.43 = (bf16[128,1024]{1,0:T(8,128)(2,1)S(1)}, bf16[128,1024]{1,0:T(8,128)(2,1)S(1)}, u32[]{:S(2)}, u32[]{:S(2)}) collective-permute-start(bf16[128,1024]{1,0:T(8,128)(2,1)S(1)} %fusion.18), channel_id=1, source_target_pairs={{0,64},{2,2},{4,196},{6,134},{8,72},{10,10},{12,204},{14,142},{16,... | collective-permute-start | bytes 786440 | tf_op jit(solution)/shard_map/ppermute | solution.py:27
  214.4 9.8 %collective-permute-start.44 = (bf16[128,1024]{1,0:T(8,128)(2,1)S(1)}, bf16[128,1024]{1,0:T(8,128)(2,1)S(1)}, u32[]{:S(2)}, u32[]{:S(2)}) collective-permute-start(bf16[128,1024]{1,0:T(8,128)(2,1)S(1)} %fusion.19), channel_id=1, source_target_pairs={{0,128},{2,194},{4,4},{6,70},{8,136},{10,202},{12,12},{14,78},{16,... | collective-permute-start | bytes 786440 | tf_op jit(solution)/shard_map/ppermute | solution.py:27
  224.4 8.7 %collective-permute-start.45 = (bf16[32,1024]{1,0:T(8,128)(2,1)S(1)}, bf16[32,1024]{1,0:T(8,128)(2,1)S(1)}, u32[]{:S(2)}, u32[]{:S(2)}) collective-permute-start(bf16[32,1024]{1,0:T(8,128)(2,1)S(1)} %get-tuple-element.67), channel_id=1, source_target_pairs={{0,0},{2,2},{4,4},{6,6},{8,40},{10,42},{12,44},{14,46},{16,16},{18... | collective-permute-start | bytes 196616 | tf_op jit(solution)/shard_map/ppermute | solution.py:27
  225.1 8.0 %collective-permute-start.46 = (bf16[32,1024]{1,0:T(8,128)(2,1)S(1)}, bf16[32,1024]{1,0:T(8,128)(2,1)S(1)}, u32[]{:S(2)}, u32[]{:S(2)}) collective-permute-start(bf16[32,1024]{1,0:T(8,128)(2,1)S(1)} %get-tuple-element.70), channel_id=1, source_target_pairs={{0,16},{2,18},{4,20},{6,22},{8,56},{10,58},{12,60},{14,62},{16,0},... | collective-permute-start | bytes 196616 | tf_op jit(solution)/shard_map/ppermute | solution.py:27
  228.7 7.2 %collective-permute-start.47 = (bf16[32,1024]{1,0:T(8,128)(2,1)S(1)}, bf16[32,1024]{1,0:T(8,128)(2,1)S(1)}, u32[]{:S(2)}, u32[]{:S(2)}) collective-permute-start(bf16[32,1024]{1,0:T(8,128)(2,1)S(1)} %get-tuple-element.69), channel_id=1, source_target_pairs={{0,32},{2,34},{4,36},{6,38},{8,8},{10,10},{12,12},{14,14},{16,48},... | collective-permute-start | bytes 196616 | tf_op jit(solution)/shard_map/ppermute | solution.py:27
  231.0 6.3 %collective-permute-start.48 = (bf16[32,1024]{1,0:T(8,128)(2,1)S(1)}, bf16[32,1024]{1,0:T(8,128)(2,1)S(1)}, u32[]{:S(2)}, u32[]{:S(2)}) collective-permute-start(bf16[32,1024]{1,0:T(8,128)(2,1)S(1)} %get-tuple-element.68), channel_id=1, source_target_pairs={{0,48},{2,50},{4,52},{6,54},{8,24},{10,26},{12,28},{14,30},{16,32}... | collective-permute-start | bytes 196616 | tf_op jit(solution)/shard_map/ppermute | solution.py:27
  (15 other events, 155.1 us)

commit v3 on v2

--- a/solution.py
+++ b/solution.py
@@ -15,7 +15,6 @@
 SIZES = (4, 4, 2, 4)
 MASKED = -1e30
 EPSILON = 1e-05
-MASKS = (0, 3, 1, 2)
 
 
 def sent(array, target):
@@ -39,20 +38,6 @@
     return lax.ppermute(array, "core", [(0, 1), (1, 0)])
 
 
-def line_target(place):
-    part, step = divmod(place, 2)
-    return lambda y, zl, zh, x: (y, zl ^ (2 * (part ^ zh) + step), zh, x)
-
-
-def ring_target(mask):
-    return lambda y, zl, zh, x: (y ^ x ^ mask, zl, zh, x)
-
-
-def near_target(place):
-    part, step = divmod(place, 2)
-    return lambda y, zl, zh, x: (y, zl ^ (2 * (part ^ turn(x)) + step), zh, x)
-
-
 def turn(x):
     return (x >> 1) ^ (x & 1)
 
@@ -71,9 +56,24 @@
     return lax.ppermute(array, "y", [(i, i ^ mask) for i in range(4)])
 
 
-def gathered(rows):
-    line = jnp.concatenate([sent(rows, line_target(place)) for place in range(4)])
-    return {mask: sent(line, ring_target(mask)) for mask in MASKS}
+def over_zl(array, mask):
+    return lax.ppermute(array, "zl", [(i, i ^ mask) for i in range(4)])
+
+
+def halves_in_order(array, turned):
+    half = array.shape[0] // 2
+    return jnp.where(turned, jnp.concatenate([array[half:], array[:half]]), array)
+
+
+def from_all_zl(rows, turned):
+    return halves_in_order(
+        jnp.concatenate([rows] + [over_zl(rows, mask) for mask in (1, 2, 3)]), turned
+    )
+
+
+def from_all_y(line, places):
+    blocks = jnp.stack([line] + [over_y(line, mask) for mask in (1, 2, 3)])
+    return [lax.dynamic_index_in_dim(blocks, place, keepdims=False) for place in places]
 
 
 def together(move, arrays, *how):
@@ -275,6 +275,16 @@
 ):
     core = lax.axis_index("core")
     features = norm_gain.shape[0] * 8
+    core, y, zl, zh, x = [lax.axis_index(name) for name in ("core", "y", "zl", "zh", "x")]
+    odd = ((y & 1) ^ (x >> 1)) == 1
+    swap = (zh ^ (y >> 1)) == 1
+    own_first = core == 0
+    even = (zl & 1) == 0
+    turned_x, turned_zh = turn(x) == 1, zh == 1
+    places = [x ^ mask for mask in range(4)]
+    odd, swap, own_first, even, turned_x, turned_zh, *places, queries = lax.optimization_barrier(
+        (odd, swap, own_first, even, turned_x, turned_zh, *places, queries)
+    )
     columns = [over_y(out_weight, mask) for mask in (1, 3, 2)]
     other_gate = over_core(gate_weight)
     other_up = over_core(up_weight)
@@ -297,16 +307,14 @@
     )
     tokens = attention.shape[0]
 
-    rows = [sent(attention, near_target(place)) for place in range(4)]
-    *rows, farthest = lax.optimization_barrier((*rows, columns[2]))
+    rows = from_all_zl(attention, turned_x)
+    rows, farthest = lax.optimization_barrier((rows, columns[2]))
     out_weight = jnp.concatenate([out_weight, farthest, near1, near3], axis=1)
     other_out = jnp.concatenate([other0, over_core(farthest), other1, other3], axis=1)
     rows, *weights = lax.optimization_barrier(
-        (jnp.concatenate(rows), gate_weight, up_weight, down_weight)
+        (rows, gate_weight, up_weight, down_weight)
     )
     other_gate, other_up, other_down = [over_core(weight) for weight in weights]
-    core, y, zh, x = [lax.axis_index(name) for name in ("core", "y", "zh", "x")]
-    odd = ((y & 1) ^ (x >> 1)) == 1
 
     def classes(products):
         half = products.shape[1] // 2
@@ -328,7 +336,6 @@
         (mine, theirs, other_gate, other_up, other_down)
     )
     width = mine.shape[1] // 2
-    swap = (zh ^ (y >> 1)) == 1
 
     def item(part, step):
         near, far = [
@@ -338,7 +345,6 @@
         return jnp.where(swap, far, near)
 
     came = [sent(item(*divmod(place, 2)), home_target(place)) for place in range(4)]
-    own_first = core == 0
     sides = []
     for step in range(2):
         total = came[step] + came[2 + step]
@@ -346,20 +352,20 @@
         sides.append(
             jnp.concatenate([jnp.where(own_first, a, b), jnp.where(own_first, b, a)], axis=1)
         )
-    even = lax.axis_index("zl") % 2 == 0
     projected = jnp.concatenate(
         [jnp.where(even, sides[0], sides[1]), jnp.where(even, sides[1], sides[0])], axis=1
     )
     state = residual + projected
 
     squares = jnp.broadcast_to(jnp.sum(state * state, axis=1), (8, 1, tokens))
-    squares = lax.all_to_all(squares, KVH, 0, 0, tiled=True).sum(axis=(0, 1))
+    squares = lax.all_to_all(squares, KVH, 0, 0, tiled=True)
+    squares = sum([squares[k, 0] for k in range(1, 8)], squares[0, 0])
     normed = (state * lax.rsqrt(squares / features + EPSILON)[:, None] * norm_gain).astype(
         jnp.bfloat16
     )
 
     first, second = summed_over_x(
-        gathered(normed), [gate_weight, up_weight], [other_gate, other_up], jnp.bfloat16
+        from_all_y(from_all_zl(normed, turned_zh), places), [gate_weight, up_weight], [other_gate, other_up], jnp.bfloat16
     )
     half = 2 * tokens
 
@@ -383,16 +389,21 @@
         1: (one12[:block], two1),
         2: (one12[block:], two32[block:]),
     }
-    line = 0.0
-    for mask in MASKS:
-        a, b = parts[mask]
-        down = (dot(a, down_weight) + dot(b, other_down)).astype(jnp.bfloat16)
-        line = line + sent(down, ring_target(mask)).astype(jnp.float32)
-    line = line.astype(jnp.bfloat16)
-    result = state
-    for place in range(4):
-        piece = line[place * tokens : (place + 1) * tokens]
-        result = result + sent(piece, line_target(place)).astype(jnp.float32)
+    down = jnp.stack(
+        [
+            (dot(a, down_weight) + dot(b, other_down)).astype(jnp.bfloat16)
+            for a, b in (parts[mask] for mask in range(4))
+        ]
+    )
+    block = [lax.dynamic_index_in_dim(down, place, keepdims=False) for place in places]
+    line = block[0].astype(jnp.float32)
+    for mask in (2, 1, 3):
+        line = line + over_y(block[mask], mask).astype(jnp.float32)
+    line = halves_in_order(line, turned_zh)
+    result = state + line[:tokens]
+    for mask in (2, 3, 1):
+        piece = line[mask * tokens : (mask + 1) * tokens].astype(jnp.bfloat16)
+        result = result + over_zl(piece, mask).astype(jnp.float32)
     return result
 
 

time: 241 us -> 235 us (0.975)
  starting transfers between devices: 73.2 us -> 69.2 us
  waiting for transfers between devices: 115 us -> 112 us
    ppermute x24 -> x4, starting transfers between devices: 55.7 us -> 9.02 us  [sent(): return lax.ppermute(array, GRID, pairs)]
    ppermute x24 -> x4, waiting for transfers between devices: 28.9 us -> 7.29 us  [sent(): return lax.ppermute(array, GRID, pairs)]
    ppermute x0 -> x9, starting transfers between devices: none -> 18.7 us  [over_zl(): return lax.ppermute(array, 'zl', [(i, i ^ mask) for i in range(4)])]
    ppermute x12, starting transfers between devices: 13.2 us -> 27.1 us  [over_x(): return lax.ppermute(array, 'x', [(i, i ^ mask) for i in range(4)])]
    ppermute x0 -> x9, waiting for transfers between devices: none -> 13.6 us  [over_zl(): return lax.ppermute(array, 'zl', [(i, i ^ mask) for i in range(4)])]
    ppermute x3 -> x9, waiting for transfers between devices: 6.12 us -> 18.4 us  [over_y(): return lax.ppermute(array, 'y', [(i, i ^ mask) for i in range(4)])]
    ppermute x3 -> x9, starting transfers between devices: 2.39 us -> 11.5 us  [over_y(): return lax.ppermute(array, 'y', [(i, i ^ mask) for i in range(4)])]
    ppermute x2, waiting for transfers between devices: 32.2 us -> 24 us  [over_zh(): return lax.ppermute(array, 'zh', [(0, 1), (1, 0)])]
  transfers between devices with their start and end apart: 49 -> 44, of which waited for: 28 -> 32; matrix products, arithmetic and copies ran while one was open for 6% -> 5% of each run, Pallas kernels for 3% -> 4%
where the time goes in v3:
time: 235 us; the launch traced here: 231 us
  waiting for transfers between devices  112 us (48%)
  starting transfers between devices  69.2 us (29%)
  blocking collectives  17.6 us (7%)
  matrix products  16.3 us (7%)
  Pallas kernels  8.49 us (4%)
  local copies, waits for them, and re-layouts  3.58 us (2%)
  other arithmetic  3.16 us (1%)
    ppermute x12, waiting for transfers between devices, over_x(): return lax.ppermute(array, 'x', [(i, i ^ mask) for i in range(4)])  45.6 us
    ppermute x12, starting transfers between devices, over_x(): return lax.ppermute(array, 'x', [(i, i ^ mask) for i in range(4)])  27.1 us
    ppermute x2, waiting for transfers between devices, over_zh(): return lax.ppermute(array, 'zh', [(0, 1), (1, 0)])  24 us
    ppermute x9, starting transfers between devices, over_zl(): return lax.ppermute(array, 'zl', [(i, i ^ mask) for i in range(4)])  18.7 us
    ppermute x9, waiting for transfers between devices, over_y(): return lax.ppermute(array, 'y', [(i, i ^ mask) for i in range(4)])  18.4 us
    all_to_all x1, blocking collectives, local(): squares = lax.all_to_all(squares, KVH, 0, 0, tiled=True)  17.6 us
    dot_general x18, matrix products, dot(): return jnp.dot(a, b, preferred_element_type=jnp.float32)  16.3 us
    ppermute x9, waiting for transfers between devices, over_zl(): return lax.ppermute(array, 'zl', [(i, i ^ mask) for i in range(4)])  13.6 us
  transfers between devices with their start and end apart: 44, of which 32 were waited for; matrix products, arithmetic and copies ran while one was open for 5% of the time, Pallas kernels for 4%

profile of v3, /device:TPU:24, one launch (start us, length us, event | category | flops | bytes accessed | tf_op | source)
XLA Modules:
  0.0 231.1 jit_solution(10242564431142641780)
XLA Ops:
  2.0 1.4 copy.14.parents
  3.9 8.0 %attend.1 = (f32[512,128]{1,0:T(8,128)}, f32[512,128]{1,0:T(8,128)}) custom-call(s32[2]{0:T(128)} %pad_add_fusion.place, s32[16]{0:T(128)} %lengths.1, bf16[64,1024]{1,0:T(8,128)(2,1)} %bitcast.76, bf16[64,128]{1,0:T(8,128)(2,1)} %bitcast.77, bf16[64,128]{1,0:T(8,128)(2,1)} %bitcast.78, s32[64,1]{1,0:T(8,128)} %copy.14.parents, bf16[4096,128]{1,0:T(8,128)(2,1)} %bitcast.74, ...), custom_call_target="tpu_custom_call" | custom-call | flops 1610612736 | bytes 2097152 | tf_op jit(solution)/shard_map/attend/pallas_call | solution.py:219
  11.9 1.7 collective-permute-done.came
  13.9 1.7 collective-permute-done.2
  18.2 3.3 %collective-permute-start.6 = (bf16[32,1024]{1,0:T(8,128)(2,1)S(1)}, bf16[32,1024]{1,0:T(8,128)(2,1)S(1)}, u32[]{:S(2)}, u32[]{:S(2)}) collective-permute-start(bf16[32,1024]{1,0:T(8,128)(2,1)S(1)} %combine.1), channel_id=1, source_target_pairs={{0,32},{16,48},{32,0},{48,16},{1,33},{17,49},{33,1},{49,17},{2,34}... | collective-permute-start | bytes 196616 | tf_op jit(solution)/shard_map/ppermute | solution.py:60
  21.5 3.2 %collective-permute-start.7 = (bf16[32,1024]{1,0:T(8,128)(2,1)S(1)}, bf16[32,1024]{1,0:T(8,128)(2,1)S(1)}, u32[]{:S(2)}, u32[]{:S(2)}) collective-permute-start(bf16[32,1024]{1,0:T(8,128)(2,1)S(1)} %combine.1), channel_id=1, source_target_pairs={{0,48},{16,32},{32,16},{48,0},{1,49},{17,33},{33,17},{49,1},{2,50}... | collective-permute-start | bytes 196616 | tf_op jit(solution)/shard_map/ppermute | solution.py:60
  25.2 3.4 %collective-permute-done.7 = bf16[32,1024]{1,0:T(8,128)(2,1)S(1)} collective-permute-done((bf16[32,1024]{1,0:T(8,128)(2,1)S(1)}, bf16[32,1024]{1,0:T(8,128)(2,1)S(1)}, u32[]{:S(2)}, u32[]{:S(2)}) %collective-permute-start.7) | collective-permute-done | bytes 65568 | tf_op jit(solution)/shard_map/ppermute | solution.py:60
  29.7 1.7 collective-permute-done.9
  34.5 1.6 collective-permute-start.13
  36.1 2.1 collective-permute-start.11
  38.2 4.8 %collective-permute-done.13 = f32[64,1024]{1,0:T(8,128)S(1)} collective-permute-done((f32[64,1024]{1,0:T(8,128)S(1)}, f32[64,1024]{1,0:T(8,128)S(1)}, u32[]{:S(2)}, u32[]{:S(2)}) %collective-permute-start.13) | collective-permute-done | bytes 262176 | tf_op jit(solution)/shard_map/ppermute | solution.py:30
  43.0 2.8 %collective-permute-start.14 = (f32[64,512]{1,0:T(8,128)S(1)}, f32[64,512]{1,0:T(8,128)S(1)}, u32[]{:S(2)}, u32[]{:S(2)}) collective-permute-start(f32[64,512]{1,0:T(8,128)S(1)} %slice_select_fusion.1), channel_id=1, source_target_pairs={{0,6},{2,4},{4,2},{6,0},{1,7},{3,5},{5,3},{7,1},{8,14},{10,12},{12... | collective-permute-start | bytes 393224 | tf_op jit(solution)/shard_map/ppermute | solution.py:30
  46.3 3.0 %collective-permute-done.14 = f32[64,512]{1,0:T(8,128)S(1)} collective-permute-done((f32[64,512]{1,0:T(8,128)S(1)}, f32[64,512]{1,0:T(8,128)S(1)}, u32[]{:S(2)}, u32[]{:S(2)}) %collective-permute-start.14) | collective-permute-done | bytes 131104 | tf_op jit(solution)/shard_map/ppermute | solution.py:30
  49.3 1.7 collective-permute-done.12
  51.8 7.3 %collective-permute-start.19 = (f32[32,512]{1,0:T(8,128)S(1)}, f32[32,512]{1,0:T(8,128)S(1)}, u32[]{:S(2)}, u32[]{:S(2)}) collective-permute-start(f32[32,512]{1,0:T(8,128)S(1)} %get-tuple-element.101), channel_id=1, source_target_pairs={{0,8},{2,40},{4,44},{6,12},{8,0},{10,32},{12,36},{14,4},{16,24},{1... | collective-permute-start | bytes 196616 | tf_op jit(solution)/shard_map/ppermute | solution.py:26
  60.2 1.4 collective-permute-done.19
  61.6 2.4 %collective-permute-done.20 = f32[32,512]{1,0:T(8,128)S(1)} collective-permute-done((f32[32,512]{1,0:T(8,128)S(1)}, f32[32,512]{1,0:T(8,128)S(1)}, u32[]{:S(2)}, u32[]{:S(2)}) %collective-permute-start.20) | collective-permute-done | bytes 65568 | tf_op jit(solution)/shard_map/ppermute | solution.py:26
  64.1 3.4 %collective-permute-done.21 = f32[32,512]{1,0:T(8,128)S(1)} collective-permute-done((f32[32,512]{1,0:T(8,128)S(1)}, f32[32,512]{1,0:T(8,128)S(1)}, u32[]{:S(2)}, u32[]{:S(2)}) %collective-permute-start.21) | collective-permute-done | bytes 65568 | tf_op jit(solution)/shard_map/ppermute | solution.py:26
  67.7 17.6 %all_to_all.5 = f32[8,1,32]{2,1,0:T(1,128)S(1)} all-to-all(f32[8,1,32]{2,1,0:T(1,128)S(1)} %broadcast_in_dim.2), channel_id=1, replica_groups=mesh['y'=4,'zl'=4,'zh'=2,'x'=4,'core'=2] {'zh','x'}, dimensions={0} | all-to-all | bytes 2048 | tf_op jit(solution)/shard_map/all_to_all | solution.py:361
  85.4 2.6 %collective-permute-start.22 = (bf16[32,1024]{1,0:T(8,128)(2,1)S(1)}, bf16[32,1024]{1,0:T(8,128)(2,1)S(1)}, u32[]{:S(2)}, u32[]{:S(2)}) collective-permute-start(bf16[32,1024]{1,0:T(8,128)(2,1)S(1)} %multiply_convert_fusion), channel_id=1, source_target_pairs={{0,32},{16,48},{32,0},{48,16},{1,33},{17,49},{33,1},{49,17},{2,34}... | collective-permute-start | bytes 196616 | tf_op jit(solution)/shard_map/ppermute | solution.py:60
  89.1 1.6 collective-permute-done.22
  90.6 3.4 %collective-permute-done.23 = bf16[32,1024]{1,0:T(8,128)(2,1)S(1)} collective-permute-done((bf16[32,1024]{1,0:T(8,128)(2,1)S(1)}, bf16[32,1024]{1,0:T(8,128)(2,1)S(1)}, u32[]{:S(2)}, u32[]{:S(2)}) %collective-permute-start.23) | collective-permute-done | bytes 65568 | tf_op jit(solution)/shard_map/ppermute | solution.py:60
  94.6 2.4 %collective-permute-start.26 = (bf16[128,1024]{1,0:T(8,128)(2,1)S(1)}, bf16[128,1024]{1,0:T(8,128)(2,1)S(1)}, u32[]{:S(2)}, u32[]{:S(2)}) collective-permute-start(bf16[128,1024]{1,0:T(8,128)(2,1)S(1)} %maximum_select_fusion.3), channel_id=1, source_target_pairs={{0,128},{64,192},{128,0},{192,64},{1,129},{65,193},{129,1},{193,65... | collective-permute-start | bytes 786440 | tf_op jit(solution)/shard_map/ppermute | solution.py:56
  97.0 1.9 collective-permute-start.27
  99.0 1.6 collective-permute-done.25
  100.6 3.7 %collective-permute-done.26 = bf16[128,1024]{1,0:T(8,128)(2,1)S(1)} collective-permute-done((bf16[128,1024]{1,0:T(8,128)(2,1)S(1)}, bf16[128,1024]{1,0:T(8,128)(2,1)S(1)}, u32[]{:S(2)}, u32[]{:S(2)}) %collective-permute-start.26) | collective-permute-done | bytes 262176 | tf_op jit(solution)/shard_map/ppermute | solution.py:56
  104.3 2.7 %collective-permute-done.27 = bf16[128,1024]{1,0:T(8,128)(2,1)S(1)} collective-permute-done((bf16[128,1024]{1,0:T(8,128)(2,1)S(1)}, bf16[128,1024]{1,0:T(8,128)(2,1)S(1)}, u32[]{:S(2)}, u32[]{:S(2)}) %collective-permute-start.27) | collective-permute-done | bytes 262176 | tf_op jit(solution)/shard_map/ppermute | solution.py:56
  107.2 2.2 convolution_convert_fusion.3
  109.5 2.4 %convolution_convert_fusion.2 = bf16[256,896]{1,0:T(8,128)(2,1)S(1)} fusion(bf16[1024,896]{1,0:T(8,128)(2,1)} %param.24, bf16[128,1024]{1,0:T(8,128)(2,1)S(1)} %get-tuple-element.83, bf16[128,1024]{1,0:T(8,128)(2,1)S(1)} %get-tuple-element.84), kind=kOutput, calls=%fused_computation.20 | convolution fusion | flops 471040000 | bytes 2818048 | tf_op jit(solution)/shard_map/dot_general | solution.py:86
  114.2 10.2 %collective-permute-start.30 = (bf16[256,1792]{1,0:T(8,128)(2,1)S(1)}, bf16[256,1792]{1,0:T(8,128)(2,1)S(1)}, u32[]{:S(2)}, u32[]{:S(2)}) collective-permute-start(bf16[256,1792]{1,0:T(8,128)(2,1)S(1)} %pad_maximum_fusion.3), channel_id=1, source_target_pairs={{0,6},{2,4},{4,2},{6,0},{1,7},{3,5},{5,3},{7,1},{8,14},{10,12},{12... | collective-permute-start | bytes 2752520 | tf_op jit(solution)/shard_map/ppermute | solution.py:30
  124.4 15.7 %collective-permute-done.30 = bf16[256,1792]{1,0:T(8,128)(2,1)S(1)} collective-permute-done((bf16[256,1792]{1,0:T(8,128)(2,1)S(1)}, bf16[256,1792]{1,0:T(8,128)(2,1)S(1)}, u32[]{:S(2)}, u32[]{:S(2)}) %collective-permute-start.30) | collective-permute-done | bytes 917536 | tf_op jit(solution)/shard_map/ppermute | solution.py:30
  142.6 2.2 convert_add_fusion
  144.8 2.2 convert_add_fusion.1
  147.2 3.1 %collective-permute-start.29 = (bf16[128,1792]{1,0:T(8,128)(2,1)S(1)}, bf16[128,1792]{1,0:T(8,128)(2,1)S(1)}, u32[]{:S(2)}, u32[]{:S(2)}) collective-permute-start(bf16[128,1792]{1,0:T(8,128)(2,1)S(1)} %pad_maximum_fusion.8), channel_id=1, source_target_pairs={{0,6},{2,4},{4,2},{6,0},{1,7},{3,5},{5,3},{7,1},{8,14},{10,12},{12... | collective-permute-start | bytes 1376264 | tf_op jit(solution)/shard_map/ppermute | solution.py:30
  150.4 6.5 %collective-permute-done.29 = bf16[128,1792]{1,0:T(8,128)(2,1)S(1)} collective-permute-done((bf16[128,1792]{1,0:T(8,128)(2,1)S(1)}, bf16[128,1792]{1,0:T(8,128)(2,1)S(1)}, u32[]{:S(2)}, u32[]{:S(2)}) %collective-permute-start.29) | collective-permute-done | bytes 458784 | tf_op jit(solution)/shard_map/ppermute | solution.py:30
  157.8 14.4 %collective-permute-done.32 = bf16[64,3584]{1,0:T(8,128)(2,1)S(1)} collective-permute-done((bf16[64,3584]{1,0:T(8,128)(2,1)S(1)}, bf16[64,3584]{1,0:T(8,128)(2,1)S(1)}, u32[]{:S(2)}, u32[]{:S(2)}) %collective-permute-start.32) | collective-permute-done | bytes 458784 | tf_op jit(solution)/shard_map/ppermute | solution.py:34
  172.9 9.6 %collective-permute-done.33 = bf16[64,1792]{1,0:T(8,128)(2,1)S(1)} collective-permute-done((bf16[64,1792]{1,0:T(8,128)(2,1)S(1)}, bf16[64,1792]{1,0:T(8,128)(2,1)S(1)}, u32[]{:S(2)}, u32[]{:S(2)}) %collective-permute-start.33) | collective-permute-done | bytes 229408 | tf_op jit(solution)/shard_map/ppermute | solution.py:34
  182.5 4.8 %collective-permute-start.36 = (bf16[128,896]{1,0:T(8,128)(2,1)S(1)}, bf16[128,896]{1,0:T(8,128)(2,1)S(1)}, u32[]{:S(2)}, u32[]{:S(2)}) collective-permute-start(bf16[128,896]{1,0:T(8,128)(2,1)S(1)} %pad_maximum_fusion.27), channel_id=1, source_target_pairs={{0,2},{2,0},{4,6},{6,4},{1,3},{3,1},{5,7},{7,5},{8,10},{10,8},{12,... | collective-permute-start | bytes 688136 | tf_op jit(solution)/shard_map/ppermute | solution.py:30
  187.9 5.9 %collective-permute-done.36 = bf16[128,896]{1,0:T(8,128)(2,1)S(1)} collective-permute-done((bf16[128,896]{1,0:T(8,128)(2,1)S(1)}, bf16[128,896]{1,0:T(8,128)(2,1)S(1)}, u32[]{:S(2)}, u32[]{:S(2)}) %collective-permute-start.36) | collective-permute-done | bytes 229408 | tf_op jit(solution)/shard_map/ppermute | solution.py:30
  193.9 1.9 collective-permute-start.37
  196.8 6.9 %collective-permute-done.37 = bf16[256,896]{1,0:T(8,128)(2,1)S(1)} collective-permute-done((bf16[256,896]{1,0:T(8,128)(2,1)S(1)}, bf16[256,896]{1,0:T(8,128)(2,1)S(1)}, u32[]{:S(2)}, u32[]{:S(2)}) %collective-permute-start.37) | collective-permute-done | bytes 458784 | tf_op jit(solution)/shard_map/ppermute | solution.py:30
  206.4 2.4 %collective-permute-start.38 = (bf16[128,1024]{1,0:T(8,128)(2,1)S(1)}, bf16[128,1024]{1,0:T(8,128)(2,1)S(1)}, u32[]{:S(2)}, u32[]{:S(2)}) collective-permute-start(bf16[128,1024]{1,0:T(8,128)(2,1)S(1)} %get-tuple-element.79), channel_id=1, source_target_pairs={{0,128},{64,192},{128,0},{192,64},{1,129},{65,193},{129,1},{193,65... | collective-permute-start | bytes 786440 | tf_op jit(solution)/shard_map/ppermute | solution.py:56
  210.8 3.6 %collective-permute-done.38 = bf16[128,1024]{1,0:T(8,128)(2,1)S(1)} collective-permute-done((bf16[128,1024]{1,0:T(8,128)(2,1)S(1)}, bf16[128,1024]{1,0:T(8,128)(2,1)S(1)}, u32[]{:S(2)}, u32[]{:S(2)}) %collective-permute-start.38) | collective-permute-done | bytes 262176 | tf_op jit(solution)/shard_map/ppermute | solution.py:56
  214.4 2.6 %collective-permute-done.39 = bf16[128,1024]{1,0:T(8,128)(2,1)S(1)} collective-permute-done((bf16[128,1024]{1,0:T(8,128)(2,1)S(1)}, bf16[128,1024]{1,0:T(8,128)(2,1)S(1)}, u32[]{:S(2)}, u32[]{:S(2)}) %collective-permute-start.39) | collective-permute-done | bytes 262176 | tf_op jit(solution)/shard_map/ppermute | solution.py:56
  218.0 4.2 %collective-permute-start.41 = (bf16[32,1024]{1,0:T(8,128)(2,1)S(1)}, bf16[32,1024]{1,0:T(8,128)(2,1)S(1)}, u32[]{:S(2)}, u32[]{:S(2)}) collective-permute-start(bf16[32,1024]{1,0:T(8,128)(2,1)S(1)} %get-tuple-element.94), channel_id=1, source_target_pairs={{0,32},{16,48},{32,0},{48,16},{1,33},{17,49},{33,1},{49,17},{2,34}... | collective-permute-start | bytes 196616 | tf_op jit(solution)/shard_map/ppermute | solution.py:60
  222.1 3.8 %collective-permute-start.42 = (bf16[32,1024]{1,0:T(8,128)(2,1)S(1)}, bf16[32,1024]{1,0:T(8,128)(2,1)S(1)}, u32[]{:S(2)}, u32[]{:S(2)}) collective-permute-start(bf16[32,1024]{1,0:T(8,128)(2,1)S(1)} %get-tuple-element.96), channel_id=1, source_target_pairs={{0,48},{16,32},{32,16},{48,0},{1,49},{17,33},{33,17},{49,1},{2,50}... | collective-permute-start | bytes 196616 | tf_op jit(solution)/shard_map/ppermute | solution.py:60
  225.9 2.9 %collective-permute-done.42 = bf16[32,1024]{1,0:T(8,128)(2,1)S(1)} collective-permute-done((bf16[32,1024]{1,0:T(8,128)(2,1)S(1)}, bf16[32,1024]{1,0:T(8,128)(2,1)S(1)}, u32[]{:S(2)}, u32[]{:S(2)}) %collective-permute-start.42) | collective-permute-done | bytes 65568 | tf_op jit(solution)/shard_map/ppermute | solution.py:60
  228.9 1.3 collective-permute-done.43
  (139 shorter events, 29.2 us)
Async XLA Ops:
  0.0 13.9 %collective-permute-start.1 = (bf16[1024,256]{1,0:T(8,128)(2,1)}, bf16[1024,256]{1,0:T(8,128)(2,1)S(1)}, u32[]{:S(2)}, u32[]{:S(2)}) collective-permute-start(bf16[1024,256]{1,0:T(8,128)(2,1)} %param.21), channel_id=1, source_target_pairs={{0,64},{64,0},{128,192},{192,128},{1,65},{65,1},{129,193},{193,129... | collective-permute-start | bytes 1572872 | tf_op jit(solution)/shard_map/ppermute | solution.py:56
  0.7 14.8 %collective-permute-start.2 = (bf16[1024,256]{1,0:T(8,128)(2,1)}, bf16[1024,256]{1,0:T(8,128)(2,1)S(1)}, u32[]{:S(2)}, u32[]{:S(2)}) collective-permute-start(bf16[1024,256]{1,0:T(8,128)(2,1)} %param.21), channel_id=1, source_target_pairs={{0,192},{64,128},{128,64},{192,0},{1,193},{65,129},{129,65},{193,1... | collective-permute-start | bytes 1572872 | tf_op jit(solution)/shard_map/ppermute | solution.py:56
  2.0 13.6 %collective-permute-start.3 = (bf16[1024,256]{1,0:T(8,128)(2,1)}, bf16[1024,256]{1,0:T(8,128)(2,1)S(1)}, u32[]{:S(2)}, u32[]{:S(2)}) collective-permute-start(bf16[1024,256]{1,0:T(8,128)(2,1)} %param.21), channel_id=1, source_target_pairs={{0,1},{1,0},{2,3},{3,2},{4,5},{5,4},{6,7},{7,6},{8,9},{9,8},{10,11... | collective-permute-start | bytes 1572872 | tf_op jit(solution)/shard_map/ppermute | solution.py:38
  3.9 28.0 %copy-start.1 = (bf16[896,1024]{1,0:T(8,128)(2,1)S(1)}, bf16[896,1024]{1,0:T(8,128)(2,1)}, u32[]{:S(2)}) copy-start(bf16[896,1024]{1,0:T(8,128)(2,1)} %param.25) | copy-start | bytes 5505028
  11.9 1.7 collective-permute-start
  15.6 2.4 %collective-permute-start.4 = (bf16[1024,256]{1,0:T(8,128)(2,1)S(1)}, bf16[1024,256]{1,0:T(8,128)(2,1)S(1)}, u32[]{:S(2)}, u32[]{:S(2)}) collective-permute-start(bf16[1024,256]{1,0:T(8,128)(2,1)S(1)} %collective-permute-done.1), channel_id=1, source_target_pairs={{0,1},{1,0},{2,3},{3,2},{4,5},{5,4},{6,7},{7,6},{8,9},{9,8},{10,11... | collective-permute-start | bytes 1572872 | tf_op jit(solution)/shard_map/ppermute | solution.py:38
  15.6 2.7 %collective-permute-start.5 = (bf16[1024,256]{1,0:T(8,128)(2,1)S(1)}, bf16[1024,256]{1,0:T(8,128)(2,1)S(1)}, u32[]{:S(2)}, u32[]{:S(2)}) collective-permute-start(bf16[1024,256]{1,0:T(8,128)(2,1)S(1)} %collective-permute-done.2), channel_id=1, source_target_pairs={{0,1},{1,0},{2,3},{3,2},{4,5},{5,4},{6,7},{7,6},{8,9},{9,8},{10,11... | collective-permute-start | bytes 1572872 | tf_op jit(solution)/shard_map/ppermute | solution.py:38
  16.1 15.3 %collective-permute-start.9 = (bf16[1024,256]{1,0:T(8,128)(2,1)S(1)}, bf16[1024,256]{1,0:T(8,128)(2,1)S(1)}, u32[]{:S(2)}, u32[]{:S(2)}) collective-permute-start(bf16[1024,256]{1,0:T(8,128)(2,1)S(1)} %copy-done.9), channel_id=1, source_target_pairs={{0,128},{64,192},{128,0},{192,64},{1,129},{65,193},{129,1},{193,65... | collective-permute-start | bytes 1572872 | tf_op jit(solution)/shard_map/ppermute | solution.py:56
  18.2 7.0 %collective-permute-start.6 = (bf16[32,1024]{1,0:T(8,128)(2,1)S(1)}, bf16[32,1024]{1,0:T(8,128)(2,1)S(1)}, u32[]{:S(2)}, u32[]{:S(2)}) collective-permute-start(bf16[32,1024]{1,0:T(8,128)(2,1)S(1)} %combine.1), channel_id=1, source_target_pairs={{0,32},{16,48},{32,0},{48,16},{1,33},{17,49},{33,1},{49,17},{2,34}... | collective-permute-start | bytes 196616 | tf_op jit(solution)/shard_map/ppermute | solution.py:60
  21.5 7.1 %collective-permute-start.7 = (bf16[32,1024]{1,0:T(8,128)(2,1)S(1)}, bf16[32,1024]{1,0:T(8,128)(2,1)S(1)}, u32[]{:S(2)}, u32[]{:S(2)}) collective-permute-start(bf16[32,1024]{1,0:T(8,128)(2,1)S(1)} %combine.1), channel_id=1, source_target_pairs={{0,48},{16,32},{32,16},{48,0},{1,49},{17,33},{33,17},{49,1},{2,50}... | collective-permute-start | bytes 196616 | tf_op jit(solution)/shard_map/ppermute | solution.py:60
  24.7 5.0 %collective-permute-start.8 = (bf16[32,1024]{1,0:T(8,128)(2,1)S(1)}, bf16[32,1024]{1,0:T(8,128)(2,1)S(1)}, u32[]{:S(2)}, u32[]{:S(2)}) collective-permute-start(bf16[32,1024]{1,0:T(8,128)(2,1)S(1)} %combine.1), channel_id=1, source_target_pairs={{0,16},{16,0},{32,48},{48,32},{1,17},{17,1},{33,49},{49,33},{2,18}... | collective-permute-start | bytes 196616 | tf_op jit(solution)/shard_map/ppermute | solution.py:60
  31.4 2.6 %collective-permute-start.10 = (bf16[1024,256]{1,0:T(8,128)(2,1)S(1)}, bf16[1024,256]{1,0:T(8,128)(2,1)S(1)}, u32[]{:S(2)}, u32[]{:S(2)}) collective-permute-start(bf16[1024,256]{1,0:T(8,128)(2,1)S(1)} %collective-permute-done.9), channel_id=1, source_target_pairs={{0,1},{1,0},{2,3},{3,2},{4,5},{5,4},{6,7},{7,6},{8,9},{9,8},{10,11... | collective-permute-start | bytes 1572872 | tf_op jit(solution)/shard_map/ppermute | solution.py:38
  31.4 19.6 %collective-permute-start.15 = (bf16[1024,896]{1,0:T(8,128)(2,1)}, bf16[1024,896]{1,0:T(8,128)(2,1)S(1)}, u32[]{:S(2)}, u32[]{:S(2)}) collective-permute-start(bf16[1024,896]{1,0:T(8,128)(2,1)} %param.23), channel_id=1, source_target_pairs={{0,1},{1,0},{2,3},{3,2},{4,5},{5,4},{6,7},{7,6},{8,9},{9,8},{10,11... | collective-permute-start | bytes 5505032 | tf_op jit(solution)/shard_map/ppermute | solution.py:38
  31.9 19.1 %collective-permute-start.16 = (bf16[1024,896]{1,0:T(8,128)(2,1)}, bf16[1024,896]{1,0:T(8,128)(2,1)S(1)}, u32[]{:S(2)}, u32[]{:S(2)}) collective-permute-start(bf16[1024,896]{1,0:T(8,128)(2,1)} %param.24), channel_id=1, source_target_pairs={{0,1},{1,0},{2,3},{3,2},{4,5},{5,4},{6,7},{7,6},{8,9},{9,8},{10,11... | collective-permute-start | bytes 5505032 | tf_op jit(solution)/shard_map/ppermute | solution.py:38
  31.9 19.1 %collective-permute-start.17 = (bf16[896,1024]{1,0:T(8,128)(2,1)S(1)}, bf16[896,1024]{1,0:T(8,128)(2,1)S(1)}, u32[]{:S(2)}, u32[]{:S(2)}) collective-permute-start(bf16[896,1024]{1,0:T(8,128)(2,1)S(1)} %copy-done.1), channel_id=1, source_target_pairs={{0,1},{1,0},{2,3},{3,2},{4,5},{5,4},{6,7},{7,6},{8,9},{9,8},{10,11... | collective-permute-start | bytes 5505032 | tf_op jit(solution)/shard_map/ppermute | solution.py:38
  34.5 8.4 %collective-permute-start.13 = (f32[64,1024]{1,0:T(8,128)S(1)}, f32[64,1024]{1,0:T(8,128)S(1)}, u32[]{:S(2)}, u32[]{:S(2)}) collective-permute-start(f32[64,1024]{1,0:T(8,128)S(1)} %slice.245), channel_id=1, source_target_pairs={{0,2},{2,0},{4,6},{6,4},{1,3},{3,1},{5,7},{7,5},{8,10},{10,8},{12,... | collective-permute-start | bytes 786440 | tf_op jit(solution)/shard_map/ppermute | solution.py:30
  36.1 9.8 %collective-permute-start.11 = (f32[128,512]{1,0:T(8,128)S(1)}, f32[128,512]{1,0:T(8,128)S(1)}, u32[]{:S(2)}, u32[]{:S(2)}) collective-permute-start(f32[128,512]{1,0:T(8,128)S(1)} %slice_select_fusion), channel_id=1, source_target_pairs={{0,6},{2,4},{4,2},{6,0},{1,7},{3,5},{5,3},{7,1},{8,14},{10,12},{12... | collective-permute-start | bytes 786440 | tf_op jit(solution)/shard_map/ppermute | solution.py:30
  43.0 6.3 %collective-permute-start.14 = (f32[64,512]{1,0:T(8,128)S(1)}, f32[64,512]{1,0:T(8,128)S(1)}, u32[]{:S(2)}, u32[]{:S(2)}) collective-permute-start(f32[64,512]{1,0:T(8,128)S(1)} %slice_select_fusion.1), channel_id=1, source_target_pairs={{0,6},{2,4},{4,2},{6,0},{1,7},{3,5},{5,3},{7,1},{8,14},{10,12},{12... | collective-permute-start | bytes 393224 | tf_op jit(solution)/shard_map/ppermute | solution.py:30
  45.9 39.4 %copy-start.4 = (f32[1024]{0:T(1024)S(1)}, f32[1024]{0:T(1024)}, u32[]{:S(2)}) copy-start(f32[1024]{0:T(1024)} %param.22) | copy-start | bytes 12292
  45.9 5.1 %collective-permute-start.12 = (f32[64,512]{1,0:T(8,128)S(1)}, f32[64,512]{1,0:T(8,128)S(1)}, u32[]{:S(2)}, u32[]{:S(2)}) collective-permute-start(f32[64,512]{1,0:T(8,128)S(1)} %slice.247), channel_id=1, source_target_pairs={{0,2},{2,0},{4,6},{6,4},{1,3},{3,1},{5,7},{7,5},{8,10},{10,8},{12,... | collective-permute-start | bytes 393224 | tf_op jit(solution)/shard_map/ppermute | solution.py:30
  51.0 36.9 %copy-start.5 = (bf16[1024,896]{1,0:T(8,128)(2,1)}, bf16[1024,896]{1,0:T(8,128)(2,1)S(1)}, u32[]{:S(2)}) copy-start(bf16[1024,896]{1,0:T(8,128)(2,1)S(1)} %collective-permute-done.15) | copy-start | bytes 5505028
  51.1 38.0 %copy-start.7 = (bf16[1024,896]{1,0:T(8,128)(2,1)}, bf16[1024,896]{1,0:T(8,128)(2,1)S(1)}, u32[]{:S(2)}) copy-start(bf16[1024,896]{1,0:T(8,128)(2,1)S(1)} %collective-permute-done.16) | copy-start | bytes 5505028
  51.1 9.1 %collective-permute-start.18 = (f32[32,512]{1,0:T(8,128)S(1)}, f32[32,512]{1,0:T(8,128)S(1)}, u32[]{:S(2)}, u32[]{:S(2)}) collective-permute-start(f32[32,512]{1,0:T(8,128)S(1)} %get-tuple-element.102), channel_id=1, source_target_pairs={{0,0},{2,32},{4,36},{6,4},{8,8},{10,40},{12,44},{14,12},{16,16},{1... | collective-permute-start | bytes 196616 | tf_op jit(solution)/shard_map/ppermute | solution.py:26
  51.8 9.8 %collective-permute-start.19 = (f32[32,512]{1,0:T(8,128)S(1)}, f32[32,512]{1,0:T(8,128)S(1)}, u32[]{:S(2)}, u32[]{:S(2)}) collective-permute-start(f32[32,512]{1,0:T(8,128)S(1)} %get-tuple-element.101), channel_id=1, source_target_pairs={{0,8},{2,40},{4,44},{6,12},{8,0},{10,32},{12,36},{14,4},{16,24},{1... | collective-permute-start | bytes 196616 | tf_op jit(solution)/shard_map/ppermute | solution.py:26
  59.1 5.0 %collective-permute-start.20 = (f32[32,512]{1,0:T(8,128)S(1)}, f32[32,512]{1,0:T(8,128)S(1)}, u32[]{:S(2)}, u32[]{:S(2)}) collective-permute-start(f32[32,512]{1,0:T(8,128)S(1)} %get-tuple-element.112), channel_id=1, source_target_pairs={{0,16},{2,48},{4,52},{6,20},{8,24},{10,56},{12,60},{14,28},{16,0},... | collective-permute-start | bytes 196616 | tf_op jit(solution)/shard_map/ppermute | solution.py:26
  60.2 7.3 %collective-permute-start.21 = (f32[32,512]{1,0:T(8,128)S(1)}, f32[32,512]{1,0:T(8,128)S(1)}, u32[]{:S(2)}, u32[]{:S(2)}) collective-permute-start(f32[32,512]{1,0:T(8,128)S(1)} %get-tuple-element.111), channel_id=1, source_target_pairs={{0,24},{2,56},{4,60},{6,28},{8,16},{10,48},{12,52},{14,20},{16,8},... | collective-permute-start | bytes 196616 | tf_op jit(solution)/shard_map/ppermute | solution.py:26
  85.4 5.3 %collective-permute-start.22 = (bf16[32,1024]{1,0:T(8,128)(2,1)S(1)}, bf16[32,1024]{1,0:T(8,128)(2,1)S(1)}, u32[]{:S(2)}, u32[]{:S(2)}) collective-permute-start(bf16[32,1024]{1,0:T(8,128)(2,1)S(1)} %multiply_convert_fusion), channel_id=1, source_target_pairs={{0,32},{16,48},{32,0},{48,16},{1,33},{17,49},{33,1},{49,17},{2,34}... | collective-permute-start | bytes 196616 | tf_op jit(solution)/shard_map/ppermute | solution.py:60
  87.9 6.1 %collective-permute-start.23 = (bf16[32,1024]{1,0:T(8,128)(2,1)S(1)}, bf16[32,1024]{1,0:T(8,128)(2,1)S(1)}, u32[]{:S(2)}, u32[]{:S(2)}) collective-permute-start(bf16[32,1024]{1,0:T(8,128)(2,1)S(1)} %multiply_convert_fusion), channel_id=1, source_target_pairs={{0,48},{16,32},{32,16},{48,0},{1,49},{17,33},{33,17},{49,1},{2,50}... | collective-permute-start | bytes 196616 | tf_op jit(solution)/shard_map/ppermute | solution.py:60
  89.1 5.0 %collective-permute-start.24 = (bf16[32,1024]{1,0:T(8,128)(2,1)S(1)}, bf16[32,1024]{1,0:T(8,128)(2,1)S(1)}, u32[]{:S(2)}, u32[]{:S(2)}) collective-permute-start(bf16[32,1024]{1,0:T(8,128)(2,1)S(1)} %multiply_convert_fusion), channel_id=1, source_target_pairs={{0,16},{16,0},{32,48},{48,32},{1,17},{17,1},{33,49},{49,33},{2,18}... | collective-permute-start | bytes 196616 | tf_op jit(solution)/shard_map/ppermute | solution.py:60
  94.1 6.5 %collective-permute-start.25 = (bf16[128,1024]{1,0:T(8,128)(2,1)S(1)}, bf16[128,1024]{1,0:T(8,128)(2,1)S(1)}, u32[]{:S(2)}, u32[]{:S(2)}) collective-permute-start(bf16[128,1024]{1,0:T(8,128)(2,1)S(1)} %maximum_select_fusion.3), channel_id=1, source_target_pairs={{0,64},{64,0},{128,192},{192,128},{1,65},{65,1},{129,193},{193,129... | collective-permute-start | bytes 786440 | tf_op jit(solution)/shard_map/ppermute | solution.py:56
  94.6 9.7 %collective-permute-start.26 = (bf16[128,1024]{1,0:T(8,128)(2,1)S(1)}, bf16[128,1024]{1,0:T(8,128)(2,1)S(1)}, u32[]{:S(2)}, u32[]{:S(2)}) collective-permute-start(bf16[128,1024]{1,0:T(8,128)(2,1)S(1)} %maximum_select_fusion.3), channel_id=1, source_target_pairs={{0,128},{64,192},{128,0},{192,64},{1,129},{65,193},{129,1},{193,65... | collective-permute-start | bytes 786440 | tf_op jit(solution)/shard_map/ppermute | solution.py:56
  97.0 10.0 %collective-permute-start.27 = (bf16[128,1024]{1,0:T(8,128)(2,1)S(1)}, bf16[128,1024]{1,0:T(8,128)(2,1)S(1)}, u32[]{:S(2)}, u32[]{:S(2)}) collective-permute-start(bf16[128,1024]{1,0:T(8,128)(2,1)S(1)} %maximum_select_fusion.3), channel_id=1, source_target_pairs={{0,192},{64,128},{128,64},{192,0},{1,193},{65,129},{129,65},{193,1... | collective-permute-start | bytes 786440 | tf_op jit(solution)/shard_map/ppermute | solution.py:56
  114.2 25.9 %collective-permute-start.30 = (bf16[256,1792]{1,0:T(8,128)(2,1)S(1)}, bf16[256,1792]{1,0:T(8,128)(2,1)S(1)}, u32[]{:S(2)}, u32[]{:S(2)}) collective-permute-start(bf16[256,1792]{1,0:T(8,128)(2,1)S(1)} %pad_maximum_fusion.3), channel_id=1, source_target_pairs={{0,6},{2,4},{4,2},{6,0},{1,7},{3,5},{5,3},{7,1},{8,14},{10,12},{12... | collective-permute-start | bytes 2752520 | tf_op jit(solution)/shard_map/ppermute | solution.py:30
  124.4 18.2 %collective-permute-start.28 = (bf16[256,1792]{1,0:T(8,128)(2,1)S(1)}, bf16[256,1792]{1,0:T(8,128)(2,1)S(1)}, u32[]{:S(2)}, u32[]{:S(2)}) collective-permute-start(bf16[256,1792]{1,0:T(8,128)(2,1)S(1)} %pad_maximum_fusion.2), channel_id=1, source_target_pairs={{0,2},{2,0},{4,6},{6,4},{1,3},{3,1},{5,7},{7,5},{8,10},{10,8},{12,... | collective-permute-start | bytes 2752520 | tf_op jit(solution)/shard_map/ppermute | solution.py:30
  141.6 8.7 %collective-permute-start.31 = (bf16[128,1792]{1,0:T(8,128)(2,1)S(1)}, bf16[128,1792]{1,0:T(8,128)(2,1)S(1)}, u32[]{:S(2)}, u32[]{:S(2)}) collective-permute-start(bf16[128,1792]{1,0:T(8,128)(2,1)S(1)} %pad_maximum_fusion.9), channel_id=1, source_target_pairs={{0,2},{2,0},{4,6},{6,4},{1,3},{3,1},{5,7},{7,5},{8,10},{10,8},{12,... | collective-permute-start | bytes 1376264 | tf_op jit(solution)/shard_map/ppermute | solution.py:30
  147.2 9.8 %collective-permute-start.29 = (bf16[128,1792]{1,0:T(8,128)(2,1)S(1)}, bf16[128,1792]{1,0:T(8,128)(2,1)S(1)}, u32[]{:S(2)}, u32[]{:S(2)}) collective-permute-start(bf16[128,1792]{1,0:T(8,128)(2,1)S(1)} %pad_maximum_fusion.8), channel_id=1, source_target_pairs={{0,6},{2,4},{4,2},{6,0},{1,7},{3,5},{5,3},{7,1},{8,14},{10,12},{12... | collective-permute-start | bytes 1376264 | tf_op jit(solution)/shard_map/ppermute | solution.py:30
  157.2 15.1 %collective-permute-start.32 = (bf16[64,3584]{1,0:T(8,128)(2,1)S(1)}, bf16[64,3584]{1,0:T(8,128)(2,1)S(1)}, u32[]{:S(2)}, u32[]{:S(2)}) collective-permute-start(bf16[64,3584]{1,0:T(8,128)(2,1)S(1)} %pad_maximum_fusion.10), channel_id=1, source_target_pairs={{0,8},{8,0},{1,9},{9,1},{2,10},{10,2},{3,11},{11,3},{4,12},{12,4},... | collective-permute-start | bytes 1376264 | tf_op jit(solution)/shard_map/ppermute | solution.py:34
  172.5 10.0 %collective-permute-start.33 = (bf16[64,1792]{1,0:T(8,128)(2,1)S(1)}, bf16[64,1792]{1,0:T(8,128)(2,1)S(1)}, u32[]{:S(2)}, u32[]{:S(2)}) collective-permute-start(bf16[64,1792]{1,0:T(8,128)(2,1)S(1)} %pad_maximum_fusion.25), channel_id=1, source_target_pairs={{0,8},{8,0},{1,9},{9,1},{2,10},{10,2},{3,11},{11,3},{4,12},{12,4},... | collective-permute-start | bytes 688136 | tf_op jit(solution)/shard_map/ppermute | solution.py:34
  182.5 11.3 %collective-permute-start.36 = (bf16[128,896]{1,0:T(8,128)(2,1)S(1)}, bf16[128,896]{1,0:T(8,128)(2,1)S(1)}, u32[]{:S(2)}, u32[]{:S(2)}) collective-permute-start(bf16[128,896]{1,0:T(8,128)(2,1)S(1)} %pad_maximum_fusion.27), channel_id=1, source_target_pairs={{0,2},{2,0},{4,6},{6,4},{1,3},{3,1},{5,7},{7,5},{8,10},{10,8},{12,... | collective-permute-start | bytes 688136 | tf_op jit(solution)/shard_map/ppermute | solution.py:30
  187.4 8.8 %collective-permute-start.34 = (bf16[128,896]{1,0:T(8,128)(2,1)S(1)}, bf16[128,896]{1,0:T(8,128)(2,1)S(1)}, u32[]{:S(2)}, u32[]{:S(2)}) collective-permute-start(bf16[128,896]{1,0:T(8,128)(2,1)S(1)} %pad_maximum_fusion.26), channel_id=1, source_target_pairs={{0,6},{2,4},{4,2},{6,0},{1,7},{3,5},{5,3},{7,1},{8,14},{10,12},{12... | collective-permute-start | bytes 688136 | tf_op jit(solution)/shard_map/ppermute | solution.py:30
  193.9 9.8 %collective-permute-start.37 = (bf16[256,896]{1,0:T(8,128)(2,1)S(1)}, bf16[256,896]{1,0:T(8,128)(2,1)S(1)}, u32[]{:S(2)}, u32[]{:S(2)}) collective-permute-start(bf16[256,896]{1,0:T(8,128)(2,1)S(1)} %pad_maximum_fusion.12), channel_id=1, source_target_pairs={{0,6},{2,4},{4,2},{6,0},{1,7},{3,5},{5,3},{7,1},{8,14},{10,12},{12... | collective-permute-start | bytes 1376264 | tf_op jit(solution)/shard_map/ppermute | solution.py:30
  196.3 8.6 %collective-permute-start.35 = (bf16[256,896]{1,0:T(8,128)(2,1)S(1)}, bf16[256,896]{1,0:T(8,128)(2,1)S(1)}, u32[]{:S(2)}, u32[]{:S(2)}) collective-permute-start(bf16[256,896]{1,0:T(8,128)(2,1)S(1)} %pad_maximum_fusion.11), channel_id=1, source_target_pairs={{0,2},{2,0},{4,6},{6,4},{1,3},{3,1},{5,7},{7,5},{8,10},{10,8},{12,... | collective-permute-start | bytes 1376264 | tf_op jit(solution)/shard_map/ppermute | solution.py:30
  206.4 8.0 %collective-permute-start.38 = (bf16[128,1024]{1,0:T(8,128)(2,1)S(1)}, bf16[128,1024]{1,0:T(8,128)(2,1)S(1)}, u32[]{:S(2)}, u32[]{:S(2)}) collective-permute-start(bf16[128,1024]{1,0:T(8,128)(2,1)S(1)} %get-tuple-element.79), channel_id=1, source_target_pairs={{0,128},{64,192},{128,0},{192,64},{1,129},{65,193},{129,1},{193,65... | collective-permute-start | bytes 786440 | tf_op jit(solution)/shard_map/ppermute | solution.py:56
  208.8 8.2 %collective-permute-start.39 = (bf16[128,1024]{1,0:T(8,128)(2,1)S(1)}, bf16[128,1024]{1,0:T(8,128)(2,1)S(1)}, u32[]{:S(2)}, u32[]{:S(2)}) collective-permute-start(bf16[128,1024]{1,0:T(8,128)(2,1)S(1)} %get-tuple-element.81), channel_id=1, source_target_pairs={{0,64},{64,0},{128,192},{192,128},{1,65},{65,1},{129,193},{193,129... | collective-permute-start | bytes 786440 | tf_op jit(solution)/shard_map/ppermute | solution.py:56
  210.1 7.6 %collective-permute-start.40 = (bf16[128,1024]{1,0:T(8,128)(2,1)S(1)}, bf16[128,1024]{1,0:T(8,128)(2,1)S(1)}, u32[]{:S(2)}, u32[]{:S(2)}) collective-permute-start(bf16[128,1024]{1,0:T(8,128)(2,1)S(1)} %get-tuple-element.80), channel_id=1, source_target_pairs={{0,192},{64,128},{128,64},{192,0},{1,193},{65,129},{129,65},{193,1... | collective-permute-start | bytes 786440 | tf_op jit(solution)/shard_map/ppermute | solution.py:56
  218.0 8.0 %collective-permute-start.41 = (bf16[32,1024]{1,0:T(8,128)(2,1)S(1)}, bf16[32,1024]{1,0:T(8,128)(2,1)S(1)}, u32[]{:S(2)}, u32[]{:S(2)}) collective-permute-start(bf16[32,1024]{1,0:T(8,128)(2,1)S(1)} %get-tuple-element.94), channel_id=1, source_target_pairs={{0,32},{16,48},{32,0},{48,16},{1,33},{17,49},{33,1},{49,17},{2,34}... | collective-permute-start | bytes 196616 | tf_op jit(solution)/shard_map/ppermute | solution.py:60
  222.1 6.7 %collective-permute-start.42 = (bf16[32,1024]{1,0:T(8,128)(2,1)S(1)}, bf16[32,1024]{1,0:T(8,128)(2,1)S(1)}, u32[]{:S(2)}, u32[]{:S(2)}) collective-permute-start(bf16[32,1024]{1,0:T(8,128)(2,1)S(1)} %get-tuple-element.96), channel_id=1, source_target_pairs={{0,48},{16,32},{32,16},{48,0},{1,49},{17,33},{33,17},{49,1},{2,50}... | collective-permute-start | bytes 196616 | tf_op jit(solution)/shard_map/ppermute | solution.py:60
  225.9 4.3 %collective-permute-start.43 = (bf16[32,1024]{1,0:T(8,128)(2,1)S(1)}, bf16[32,1024]{1,0:T(8,128)(2,1)S(1)}, u32[]{:S(2)}, u32[]{:S(2)}) collective-permute-start(bf16[32,1024]{1,0:T(8,128)(2,1)S(1)} %get-tuple-element.95), channel_id=1, source_target_pairs={{0,16},{16,0},{32,48},{48,32},{1,17},{17,1},{33,49},{49,33},{2,18}... | collective-permute-start | bytes 196616 | tf_op jit(solution)/shard_map/ppermute | solution.py:60
  (6 other events, 47.1 us)
